TPU v7x, 32 devices: a whole 2x2x4 slice. The times are simulated.
32 devices in a mesh: seq: 8 (over z, y), head: 4 (over x, core).
Axes of the slice: x: 2, y: 2, z: 4, core: 2. Of those that a mesh axis runs over, the one named last changes fastest.
Arguments:
- tokens: bfloat16 [2048, 4096], P('seq', 'head'), may hold values from -6 to 6
- light_input: bfloat16 [3, 4096, 1024], P(None, None, 'head'), may hold values from -14 to 14
- light_output: bfloat16 [1024, 4096], P('head'), may hold values from -0.75 to 0.75
- heavy_input: bfloat16 [3, 4096, 4096], P(None, 'seq', 'head'), may hold values from -14 to 14
- heavy_output: bfloat16 [4096, 4096], P('head', 'seq'), may hold values from -0.75 to 0.75
- query_tokens: int32 [8, 32], replicated, may hold values from -1 to 255, as said below
- context_tokens: int32 [8, 32], replicated, may hold values from -1 to 255, as said below
- query_gate: float32 [8, 32], P('seq'), may hold values from 0.25 to 2
Outputs:
- mixed: bfloat16 [2048, 4096], P('seq', 'head')
Inputs may be any that keep to these rules, and one draw needn't show every extreme that they name: `query_tokens`: row s lists, in its first entries, distinct positions within sequence shard s of routed query tokens, and -1 after them; 64 positions are listed over all rows, at most 32 in a row, and exactly 32 in some row. `context_tokens`: row s lists, in its first entries, distinct positions within sequence shard s of routed key-value tokens, and -1 after them; 64 positions are listed over all rows, at most 32 in a row, and exactly 32 in some row.
All inputs are finite; a program needn't handle non-finite values.
Results may differ from a plain program's by a relative error of at most 0.012.
Values may be sent and summed in bfloat16 or wider, within the bound.
No kernel may reach another device: no remote copies, remote signals or barrier semaphores. Data moves between devices by JAX's collectives and lax.ppermute only.
A program may use at most 64 MiB of HBM per device.

v0:
```python
import math

import jax
import jax.numpy as jnp
from jax import lax
from jax.sharding import PartitionSpec as P

HD = 128
LB = 128
ROUTE = 32


def attend(queries, key_rows, value_rows):
    scores = jnp.einsum(
        "bqhe,bkhe->bhqk", queries, key_rows, preferred_element_type=jnp.float32
    ) / math.sqrt(queries.shape[-1])
    highest = jnp.max(scores, axis=-1, keepdims=True)
    expanded = jnp.exp(scores - highest)
    totals = jnp.sum(expanded, axis=-1)
    weighted = jnp.einsum(
        "bhqk,bkhe->bqhe",
        expanded.astype(jnp.bfloat16),
        value_rows,
        preferred_element_type=jnp.float32,
    )
    return (weighted / jnp.transpose(totals, (0, 2, 1))[..., None]).astype(jnp.bfloat16)


def routed_map(table, routed):
    counts = jnp.sum((table >= 0).astype(jnp.int32), axis=1)
    upper_end = jnp.cumsum(counts)
    lower_end = upper_end - counts
    compact_rows = jnp.arange(routed, dtype=jnp.int32)
    source_shard = jnp.sum((upper_end[None, :] <= compact_rows[:, None]).astype(jnp.int32), axis=1)
    onehot_shard = (
        source_shard[:, None] == jnp.arange(table.shape[0], dtype=jnp.int32)[None, :]
    ).astype(jnp.int32)
    within = compact_rows - jnp.sum(onehot_shard * lower_end[None, :], axis=1)
    return (source_shard * table.shape[1] + within, lower_end)


def project(query_part, source_part, weights):
    stacked = jnp.stack((query_part, source_part, source_part))
    return jnp.einsum("cmd,cdw->mcw", stacked, weights, preferred_element_type=jnp.float32)


def pick_rows(gathered, own_list):
    chosen = jnp.take(gathered, jnp.maximum(own_list, 0), axis=0)
    return jnp.where((own_list >= 0)[:, None], chosen, jnp.zeros_like(chosen))


def per_device(
    tokens,
    light_input,
    light_output,
    heavy_input,
    heavy_output,
    query_tokens,
    context_tokens,
    query_gate,
):
    gathered = lax.all_gather(tokens, "head", axis=1, tiled=True)
    tok_rows = gathered.shape[0]
    light_mapped = jnp.einsum(
        "td,cdw->ctw", gathered, light_input, preferred_element_type=jnp.float32
    ).astype(jnp.bfloat16)
    light_blocks = light_mapped.reshape(3, tok_rows // LB, LB, -1, HD)
    light_heads = attend(light_blocks[0], light_blocks[1], light_blocks[2]).reshape(tok_rows, -1)
    light_part = jnp.dot(light_heads, light_output, preferred_element_type=jnp.float32)
    seq_count = lax.axis_size("seq")
    routed = seq_count * tok_rows // ROUTE
    slot_count = query_tokens.shape[1]
    seq_index = lax.axis_index("seq")
    own_queries = lax.dynamic_index_in_dim(query_tokens, seq_index, 0, keepdims=False)
    own_sources = lax.dynamic_index_in_dim(context_tokens, seq_index, 0, keepdims=False)
    query_cols, source_cols = (
        lax.all_to_all(
            pick_rows(gathered, own_queries), "seq", split_axis=1, concat_axis=0, tiled=True
        ),
        lax.all_to_all(
            pick_rows(gathered, own_sources), "seq", split_axis=1, concat_axis=0, tiled=True
        ),
    )
    query_index, query_lower = routed_map(query_tokens, routed)
    source_index = routed_map(context_tokens, routed)[0]
    query_rows = jnp.take(query_cols, query_index, axis=0)
    source_rows = jnp.take(source_cols, source_index, axis=0)
    summed = lax.psum(project(query_rows, source_rows, heavy_input), "seq").astype(jnp.bfloat16)
    heavy_heads = attend(
        summed[:, 0].reshape(1, routed, -1, HD),
        summed[:, 1].reshape(1, routed, -1, HD),
        summed[:, 2].reshape(1, routed, -1, HD),
    ).reshape(routed, -1)
    heavy_part = jnp.dot(heavy_heads, heavy_output, preferred_element_type=jnp.float32)
    slot_live = query_tokens >= 0
    compact = query_lower[:, None] + jnp.arange(slot_count, dtype=jnp.int32)[None, :]
    outgoing = jnp.take(heavy_part, jnp.where(slot_live, compact, 0).reshape(-1), axis=0)
    outgoing = jnp.where(slot_live.reshape(-1)[:, None], outgoing, jnp.zeros_like(outgoing))
    returned = lax.all_to_all(
        outgoing.astype(jnp.bfloat16), "seq", split_axis=0, concat_axis=1, tiled=True
    ).astype(outgoing.dtype)
    scaled = returned * query_gate[0][:, None]
    targets = jnp.where(own_queries >= 0, own_queries, tok_rows)
    combined = light_part.at[targets].add(scaled, mode="drop")
    return lax.psum_scatter(combined.astype(jnp.bfloat16), "head", scatter_dimension=1, tiled=True)


def solution(mesh):
    placed = (
        P("seq", "head"),
        P(None, None, "head"),
        P("head", None),
        P(None, "seq", "head"),
        P("head", "seq"),
        P(),
        P(),
        P("seq", None),
    )
    return jax.shard_map(
        per_device, mesh=mesh, in_specs=placed, out_specs=P("seq", "head"), check_vma=False
    )
```

profile of v0, /device:TPU:0, one launch (start us, length us, event | category | flops | bytes accessed | tf_op | source)
XLA Modules:
  0.0 186.6 jit_solution(15479127844773450853)
XLA Ops:
  6.5 0.7 all-gather.2.cloned.1.call-update
  7.3 1.0 convert_reduce_fusion.1
  8.5 0.8 convert_reduce_fusion.3
  9.3 0.2 reduce-window.14
  9.6 1.2 fusion.40
  10.8 0.7 compare_bitcast_fusion
  11.5 0.7 compare_and_fusion.2
  12.4 0.5 compare_and_fusion.3
  13.2 0.6 compare_and_fusion.1
  13.8 0.6 pad_clamp_fusion.1
  14.4 0.7 compare_and_fusion
  15.0 19.2 %all-gather.2.cloned.1.call-done = bf16[256,4096]{1,0:T(8,128)(2,1)} async-done(((bf16[256,1024]{1,0:T(8,128)(2,1)}), bf16[256,4096]{1,0:T(8,128)(2,1)}) %all-gather.2.cloned.1.call-update) | async-done | bytes 2097168 | tf_op jit(solution)/shard_map/all_gather | solution.py:62
  34.2 2.8 %gather_fusion.1 = bf16[32,4096]{1,0:T(8,128)(2,1)S(1)} fusion(bf16[256,4096]{1,0:T(8,128)(2,1)} %all-gather.2.cloned.1.call-done, s32[1024]{0:T(1024)S(1)} %pad_clamp_fusion.4), kind=kCustom, calls=%fused_computation.clone | custom fusion | bytes 524416 | tf_op jit(solution)/shard_map/jit(_take)/gather | solution.py:48
  37.2 0.7 copy.109
  37.9 5.5 %all-to-all-start = ((bf16[32,8,512]{2,0,1:T(8,128)(2,1)}), bf16[32,8,512]{2,0,1:T(8,128)(2,1)S(1)}, u32[]{:S(2)}, u32[]{:S(2)}) async-start(bf16[32,8,512]{2,0,1:T(8,128)(2,1)} %bitcast.115), calls=%async_computation | async-start | bytes 524288 | tf_op jit(solution)/shard_map/all_to_all | solution.py:77
  43.4 3.5 %gather_fusion.3 = bf16[32,4096]{1,0:T(8,128)(2,1)} fusion(bf16[256,4096]{1,0:T(8,128)(2,1)} %all-gather.2.cloned.1.call-done, s32[1024]{0:T(1024)S(1)} %pad_clamp_fusion.2), kind=kCustom, calls=%fused_computation.2.clone | custom fusion | bytes 524416 | tf_op jit(solution)/shard_map/jit(_take)/gather | solution.py:48
  46.9 1.1 select_select_fusion
  48.0 5.2 %fusion.5 = bf16[3,256,256]{1,2,0:T(8,128)(2,1)S(1)} fusion(bf16[3,4096,256]{2,1,0:T(8,128)(2,1)} %param.13, bf16[256,4096]{1,0:T(8,128)(2,1)} %all-gather.2.cloned.1.call-done), kind=kOutput, calls=%fused_computation.10 | convolution fusion | flops 1610809344 | bytes 8781824 | tf_op jit(solution)/shard_map/td,cdw->ctw/dot_general | solution.py:64
  53.3 0.7 copy.108
  54.0 0.7 fusion.42
  54.7 1.6 squeeze.16
  56.3 1.6 squeeze.15
  57.9 6.0 %all-to-all-start.1 = ((bf16[32,8,512]{2,0,1:T(8,128)(2,1)}), bf16[32,8,512]{2,0,1:T(8,128)(2,1)}, u32[]{:S(2)}, u32[]{:S(2)}) async-start(bf16[32,8,512]{2,0,1:T(8,128)(2,1)} %bitcast.114), calls=%async_computation.1 | async-start | bytes 524288 | tf_op jit(solution)/shard_map/all_to_all | solution.py:80
  63.9 1.9 %fusion.43 = (f32[2,2,128]{2,1,0:T(2,128)S(1)}, f32[2,2,128,128]{2,3,1,0:T(8,128)}) fusion(bf16[2,128,2,128]{1,0,3,2:T(2,128)(2,1)} %squeeze.16, bf16[2,128,2,128]{1,0,3,2:T(2,128)(2,1)} %squeeze.15), kind=kOutput, calls=%fused_computation.97 | convolution fusion | flops 16907776 | bytes 526336 | tf_op jit(solution)/shard_map/bqhe,bkhe->bhqk/dot_general | solution.py:14
  65.8 0.7 squeeze.14
  66.5 1.6 fusion.15
  68.1 0.7 gather_fusion.2
  68.8 0.7 select_bitcast_fusion.1
  69.4 3.3 %all-to-all-done.1 = bf16[32,8,512]{2,0,1:T(8,128)(2,1)} async-done(((bf16[32,8,512]{2,0,1:T(8,128)(2,1)}), bf16[32,8,512]{2,0,1:T(8,128)(2,1)}, u32[]{:S(2)}, u32[]{:S(2)}) %all-to-all-start.1) | async-done | bytes 262176 | tf_op jit(solution)/shard_map/all_to_all | solution.py:80
  72.7 1.8 gather_fusion.4
  74.6 0.8 select_bitcast_fusion
  75.3 1.5 convolution_bitcast_fusion
  76.9 45.5 %all-reduce.1 = bf16[64,3,1024]{2,0,1:T(8,128)(2,1)S(1)} all-reduce(f32[64,3,1024]{2,0,1:T(8,128)} %convolution_bitcast_fusion), channel_id=1, replica_groups=mesh['seq'=8,'head'=4] {'seq'}, use_global_device_ids=true, to_apply=%region_10.13 | all-reduce | flops 196608 | bytes 1179648 | tf_op jit(solution)/shard_map/psum | solution.py:88
  122.5 0.2 fusion.44
  122.8 0.2 fusion.11
  123.2 0.4 copy-done.1
  123.6 0.3 fusion.26
  123.9 1.2 gather_fusion
  125.1 0.8 select_convert_fusion
  125.9 4.0 %all-to-all-start.2 = ((bf16[8,32,512]{2,1,0:T(8,128)(2,1)}), bf16[8,32,512]{2,1,0:T(8,128)(2,1)S(1)}, u32[]{:S(2)}, u32[]{:S(2)}) async-start(bf16[8,32,512]{2,1,0:T(8,128)(2,1)} %select_convert_fusion), calls=%async_computation.2 | async-start | bytes 524288 | tf_op jit(solution)/shard_map/all_to_all | solution.py:99
  129.9 1.8 fusion.9
  131.8 1.0 copy.58
  132.8 4.2 %fusion.29 = f32[256,4096]{1,0:T(8,128)} fusion(bf16[256,4096]{1,0:T(8,128)(2,1)} %param.14, bf16[32,8,2,128]{3,2,1,0:T(2,128)(2,1)S(1)} %bitcast.119), kind=kOutput, calls=%fused_computation.42 | convolution fusion | flops 536870912 | bytes 6422528 | tf_op jit(solution)/shard_map/dot_general | solution.py:69
  137.1 1.0 all-to-all-done.2
  138.2 0.8 copy.72
  139.0 5.9 %scatter_custom_fusion = f32[256,4096]{1,0:T(8,128)} fusion(f32[256,4096]{1,0:T(8,128)} %fusion.29, s32[32]{0:T(128)} %fusion.40, f32[32,4096]{1,0:T(8,128)} %bitcast.112, f32[32]{0:T(128)S(1)} %bitcast.126), kind=kCustom, calls=%fused_computation.20 | custom fusion | flops 262144 | bytes 4718720 | tf_op jit(solution)/shard_map/scatter-add | solution.py:104
  144.9 3.8 %convert_element_type.67 = bf16[256,4096]{1,0:T(8,128)(2,1)} convert(f32[256,4096]{1,0:T(8,128)} %scatter_custom_fusion) | non-fusion elementwise | flops 1048576 | bytes 6291456 | tf_op jit(solution)/shard_map/convert_element_type | solution.py:105
  148.7 31.0 %reduce-scatter.2.cloned.1.call-done = bf16[256,1024]{1,0:T(8,128)(2,1)} async-done(((bf16[256,4096]{1,0:T(8,128)(2,1)}), bf16[256,1024]{1,0:T(8,128)(2,1)}) %reduce-scatter.2.cloned.1.call-update) | async-done | bytes 524304 | tf_op jit(solution)/shard_map/reduce_scatter | solution.py:105
  (35 shorter events, 1.2 us)
Async XLA Ops:
  6.5 68.8 %copy-start = (bf16[3,512,1024]{2,1,0:T(8,128)(2,1)S(1)}, bf16[3,512,1024]{2,1,0:T(8,128)(2,1)}, u32[]{:S(2)}) copy-start(bf16[3,512,1024]{2,1,0:T(8,128)(2,1)} %param.15) | copy-start | bytes 9437188
  6.5 27.7 %all-gather.2.cloned.1.call-start = ((), (), s32[]{:S(2)}) async-start(), calls=%async_computation.4 | async-start | bytes 2621440 | tf_op jit(solution)/shard_map/all_gather | solution.py:62
  37.9 20.0 %all-to-all-start = ((bf16[32,8,512]{2,0,1:T(8,128)(2,1)}), bf16[32,8,512]{2,0,1:T(8,128)(2,1)S(1)}, u32[]{:S(2)}, u32[]{:S(2)}) async-start(bf16[32,8,512]{2,0,1:T(8,128)(2,1)} %bitcast.115), calls=%async_computation | async-start | bytes 524288 | tf_op jit(solution)/shard_map/all_to_all | solution.py:77
  57.9 14.9 %all-to-all-start.1 = ((bf16[32,8,512]{2,0,1:T(8,128)(2,1)}), bf16[32,8,512]{2,0,1:T(8,128)(2,1)}, u32[]{:S(2)}, u32[]{:S(2)}) async-start(bf16[32,8,512]{2,0,1:T(8,128)(2,1)} %bitcast.114), calls=%async_computation.1 | async-start | bytes 524288 | tf_op jit(solution)/shard_map/all_to_all | solution.py:80
  122.4 1.2 copy-start.1
  122.5 2.6 %copy-start.2 = (pred[8,32]{1,0:T(8,128)(4,1)S(1)}, pred[8,32]{1,0:T(8,128)(4,1)}, u32[]{:S(2)}) copy-start(pred[8,32]{1,0:T(8,128)(4,1)} %compare_and_fusion) | copy-start | bytes 772
  122.7 7.2 %copy-start.3 = (f32[2,2,128]{2,1,0:T(2,128)S(1)}, f32[2,2,128]{2,1,0:T(2,128)}, u32[]{:S(2)}) copy-start(f32[2,2,128]{2,1,0:T(2,128)} %fusion.15) | copy-start | bytes 6148
  125.9 12.2 %all-to-all-start.2 = ((bf16[8,32,512]{2,1,0:T(8,128)(2,1)}), bf16[8,32,512]{2,1,0:T(8,128)(2,1)S(1)}, u32[]{:S(2)}, u32[]{:S(2)}) async-start(bf16[8,32,512]{2,1,0:T(8,128)(2,1)} %select_convert_fusion), calls=%async_computation.2 | async-start | bytes 524288 | tf_op jit(solution)/shard_map/all_to_all | solution.py:99
  129.9 49.9 %reduce-scatter.2.cloned.1.call-start = ((), (), s32[]{:S(2)}) async-start(), calls=%async_computation.5 | async-start | bytes 2621440 | tf_op jit(solution)/shard_map/reduce_scatter | solution.py:105
  132.8 6.2 %copy-start.4 = (f32[1,32]{1,0:T(1,128)S(1)}, f32[1,32]{1,0:T(1,128)}, u32[]{:S(2)}) copy-start(f32[1,32]{1,0:T(1,128)} %param.19) | copy-start | bytes 388
Sparse Core Ops, SparseCore 0:
  8.9 25.2 all-gather.1
  148.9 30.8 reduce-scatter.1
where the time goes:
time: 188 us; the launch traced here: 187 us
  waiting for transfers between devices  55.3 us (29%)
  blocking collectives  45.5 us (24%)
  other arithmetic  22.5 us (12%)
  local copies, waits for them, and re-layouts  18.6 us (10%)
  starting transfers between devices  15.5 us (8%)
  matrix products  15.5 us (8%)
  between operations  13.6 us (7%)
    psum x1, blocking collectives, per_device(): lax.psum(project(query_rows, source_rows, heavy_input), 'seq')  45.5 us
    reduce_scatter x1, waiting for transfers between devices, per_device(): lax.psum_scatter(combined.astype(jnp.bfloat16), 'head', scatter_dimension...  31 us
    all_gather x1, waiting for transfers between devices, per_device(): gathered = lax.all_gather(tokens, 'head', axis=1, tiled=True)  19.2 us
    gather x2, local copies, waits for them, and re-layouts, pick_rows(): chosen = jnp.take(gathered, jnp.maximum(own_list, 0), axis=0)  6.33 us
    all_to_all x1, starting transfers between devices, per_device(): lax.all_to_all(pick_rows(gathered, own_sources), 'seq', split_axis=1, con...  6 us
    scatter-add x1, other arithmetic, per_device(): combined = light_part.at[targets].add(scaled, mode='drop')  5.91 us
    all_to_all x1, starting transfers between devices, per_device(): lax.all_to_all(pick_rows(gathered, own_queries), 'seq', split_axis=1, con...  5.52 us
    dot_general x1, matrix products, per_device(): jnp.einsum('td,cdw->ctw', gathered, light_input, preferred_element_type=j...  5.25 us
  transfers between devices with their start and end apart: 5, of which 4 were waited for; matrix products, arithmetic and copies ran while one was open for 19% of the time, Pallas kernels for 0%

commit v1 on v0

--- a/solution.py
+++ b/solution.py
@@ -28,7 +28,8 @@
 
 def routed_map(table, routed):
     counts = jnp.sum((table >= 0).astype(jnp.int32), axis=1)
-    upper_end = jnp.cumsum(counts)
+    shard = jnp.arange(table.shape[0], dtype=jnp.int32)
+    upper_end = jnp.sum(jnp.where(shard[None, :] <= shard[:, None], counts[None, :], 0), axis=1)
     lower_end = upper_end - counts
     compact_rows = jnp.arange(routed, dtype=jnp.int32)
     source_shard = jnp.sum((upper_end[None, :] <= compact_rows[:, None]).astype(jnp.int32), axis=1)

time: 188 us -> 188 us (level)
  no operation moved by 1% of the time
where the time goes in v1:
time: 188 us; the launch traced here: 187 us
  waiting for transfers between devices  55.4 us (29%)
  blocking collectives  45.5 us (24%)
  other arithmetic  22.4 us (12%)
  local copies, waits for them, and re-layouts  18.6 us (10%)
  starting transfers between devices  15.5 us (8%)
  matrix products  15.5 us (8%)
  between operations  13.6 us (7%)
    psum x1, blocking collectives, per_device(): lax.psum(project(query_rows, source_rows, heavy_input), 'seq')  45.5 us
    reduce_scatter x1, waiting for transfers between devices, per_device(): lax.psum_scatter(combined.astype(jnp.bfloat16), 'head', scatter_dimension...  31 us
    all_gather x1, waiting for transfers between devices, per_device(): gathered = lax.all_gather(tokens, 'head', axis=1, tiled=True)  19.3 us
    gather x2, local copies, waits for them, and re-layouts, pick_rows(): chosen = jnp.take(gathered, jnp.maximum(own_list, 0), axis=0)  6.33 us
    all_to_all x1, starting transfers between devices, per_device(): lax.all_to_all(pick_rows(gathered, own_sources), 'seq', split_axis=1, con...  6 us
    scatter-add x1, other arithmetic, per_device(): combined = light_part.at[targets].add(scaled, mode='drop')  5.91 us
    all_to_all x1, starting transfers between devices, per_device(): lax.all_to_all(pick_rows(gathered, own_queries), 'seq', split_axis=1, con...  5.52 us
    dot_general x1, matrix products, per_device(): jnp.einsum('td,cdw->ctw', gathered, light_input, preferred_element_type=j...  5.25 us
  transfers between devices with their start and end apart: 5, of which 4 were waited for; matrix products, arithmetic and copies ran while one was open for 19% of the time, Pallas kernels for 0%

profile of v1, /device:TPU:0, one launch (start us, length us, event | category | flops | bytes accessed | tf_op | source)
XLA Modules:
  0.0 186.6 jit_solution(7812252662612536759)
XLA Ops:
  6.5 0.7 all-gather.2.cloned.1.call-update
  7.3 1.0 convert_reduce_fusion.1
  8.4 0.8 convert_reduce_fusion.3
  9.2 0.1 select_reduce_fusion.3
  9.5 1.2 fusion.40
  10.7 0.7 compare_bitcast_fusion
  11.4 0.7 compare_and_fusion.2
  12.3 0.5 compare_and_fusion.3
  13.0 0.6 compare_and_fusion.1
  13.6 0.6 pad_clamp_fusion.1
  14.2 0.7 compare_and_fusion
  14.9 19.3 %all-gather.2.cloned.1.call-done = bf16[256,4096]{1,0:T(8,128)(2,1)} async-done(((bf16[256,1024]{1,0:T(8,128)(2,1)}), bf16[256,4096]{1,0:T(8,128)(2,1)}) %all-gather.2.cloned.1.call-update) | async-done | bytes 2097168 | tf_op jit(solution)/shard_map/all_gather | solution.py:63
  34.2 2.8 %gather_fusion.1 = bf16[32,4096]{1,0:T(8,128)(2,1)S(1)} fusion(bf16[256,4096]{1,0:T(8,128)(2,1)} %all-gather.2.cloned.1.call-done, s32[1024]{0:T(1024)S(1)} %pad_clamp_fusion.4), kind=kCustom, calls=%fused_computation.clone | custom fusion | bytes 524416 | tf_op jit(solution)/shard_map/jit(_take)/gather | solution.py:49
  37.2 0.7 copy.109
  37.9 5.5 %all-to-all-start = ((bf16[32,8,512]{2,0,1:T(8,128)(2,1)}), bf16[32,8,512]{2,0,1:T(8,128)(2,1)S(1)}, u32[]{:S(2)}, u32[]{:S(2)}) async-start(bf16[32,8,512]{2,0,1:T(8,128)(2,1)} %bitcast.109), calls=%async_computation | async-start | bytes 524288 | tf_op jit(solution)/shard_map/all_to_all | solution.py:78
  43.4 3.5 %gather_fusion.3 = bf16[32,4096]{1,0:T(8,128)(2,1)} fusion(bf16[256,4096]{1,0:T(8,128)(2,1)} %all-gather.2.cloned.1.call-done, s32[1024]{0:T(1024)S(1)} %pad_clamp_fusion.2), kind=kCustom, calls=%fused_computation.2.clone | custom fusion | bytes 524416 | tf_op jit(solution)/shard_map/jit(_take)/gather | solution.py:49
  46.9 1.1 select_select_fusion
  48.0 5.2 %fusion.5 = bf16[3,256,256]{1,2,0:T(8,128)(2,1)S(1)} fusion(bf16[3,4096,256]{2,1,0:T(8,128)(2,1)} %param.13, bf16[256,4096]{1,0:T(8,128)(2,1)} %all-gather.2.cloned.1.call-done), kind=kOutput, calls=%fused_computation.10 | convolution fusion | flops 1610809344 | bytes 8781824 | tf_op jit(solution)/shard_map/td,cdw->ctw/dot_general | solution.py:65
  53.3 0.7 copy.108
  54.0 0.7 fusion.42
  54.7 1.6 squeeze.16
  56.3 1.6 squeeze.15
  57.9 6.0 %all-to-all-start.1 = ((bf16[32,8,512]{2,0,1:T(8,128)(2,1)}), bf16[32,8,512]{2,0,1:T(8,128)(2,1)}, u32[]{:S(2)}, u32[]{:S(2)}) async-start(bf16[32,8,512]{2,0,1:T(8,128)(2,1)} %bitcast.108), calls=%async_computation.1 | async-start | bytes 524288 | tf_op jit(solution)/shard_map/all_to_all | solution.py:81
  63.9 1.9 %fusion.43 = (f32[2,2,128]{2,1,0:T(2,128)S(1)}, f32[2,2,128,128]{2,3,1,0:T(8,128)}) fusion(bf16[2,128,2,128]{1,0,3,2:T(2,128)(2,1)} %squeeze.16, bf16[2,128,2,128]{1,0,3,2:T(2,128)(2,1)} %squeeze.15), kind=kOutput, calls=%fused_computation.98 | convolution fusion | flops 16907776 | bytes 526336 | tf_op jit(solution)/shard_map/bqhe,bkhe->bhqk/dot_general | solution.py:14
  65.8 0.7 squeeze.14
  66.5 1.6 fusion.15
  68.1 0.7 gather_fusion.2
  68.8 0.7 select_bitcast_fusion.1
  69.4 3.3 %all-to-all-done.1 = bf16[32,8,512]{2,0,1:T(8,128)(2,1)} async-done(((bf16[32,8,512]{2,0,1:T(8,128)(2,1)}), bf16[32,8,512]{2,0,1:T(8,128)(2,1)}, u32[]{:S(2)}, u32[]{:S(2)}) %all-to-all-start.1) | async-done | bytes 262176 | tf_op jit(solution)/shard_map/all_to_all | solution.py:81
  72.7 1.8 gather_fusion.4
  74.6 0.8 select_bitcast_fusion
  75.3 1.5 convolution_bitcast_fusion
  76.9 45.5 %all-reduce.1 = bf16[64,3,1024]{2,0,1:T(8,128)(2,1)S(1)} all-reduce(f32[64,3,1024]{2,0,1:T(8,128)} %convolution_bitcast_fusion), channel_id=1, replica_groups=mesh['seq'=8,'head'=4] {'seq'}, use_global_device_ids=true, to_apply=%region_10.13 | all-reduce | flops 196608 | bytes 1179648 | tf_op jit(solution)/shard_map/psum | solution.py:89
  122.5 0.2 fusion.44
  122.8 0.2 fusion.11
  123.2 0.4 copy-done.1
  123.6 0.3 fusion.26
  123.9 1.2 gather_fusion
  125.1 0.8 select_convert_fusion
  125.9 4.0 %all-to-all-start.2 = ((bf16[8,32,512]{2,1,0:T(8,128)(2,1)}), bf16[8,32,512]{2,1,0:T(8,128)(2,1)S(1)}, u32[]{:S(2)}, u32[]{:S(2)}) async-start(bf16[8,32,512]{2,1,0:T(8,128)(2,1)} %select_convert_fusion), calls=%async_computation.2 | async-start | bytes 524288 | tf_op jit(solution)/shard_map/all_to_all | solution.py:100
  129.9 1.8 fusion.9
  131.8 1.0 copy.58
  132.8 4.2 %fusion.29 = f32[256,4096]{1,0:T(8,128)} fusion(bf16[256,4096]{1,0:T(8,128)(2,1)} %param.14, bf16[32,8,2,128]{3,2,1,0:T(2,128)(2,1)S(1)} %bitcast.113), kind=kOutput, calls=%fused_computation.42 | convolution fusion | flops 536870912 | bytes 6422528 | tf_op jit(solution)/shard_map/dot_general | solution.py:70
  137.1 1.0 all-to-all-done.2
  138.2 0.8 copy.72
  139.0 5.9 %scatter_custom_fusion = f32[256,4096]{1,0:T(8,128)} fusion(f32[256,4096]{1,0:T(8,128)} %fusion.29, s32[32]{0:T(128)} %fusion.40, f32[32,4096]{1,0:T(8,128)} %bitcast.106, f32[32]{0:T(128)S(1)} %bitcast.120), kind=kCustom, calls=%fused_computation.20 | custom fusion | flops 262144 | bytes 4718720 | tf_op jit(solution)/shard_map/scatter-add | solution.py:105
  144.9 3.8 %convert_element_type.67 = bf16[256,4096]{1,0:T(8,128)(2,1)} convert(f32[256,4096]{1,0:T(8,128)} %scatter_custom_fusion) | non-fusion elementwise | flops 1048576 | bytes 6291456 | tf_op jit(solution)/shard_map/convert_element_type | solution.py:106
  148.7 31.0 %reduce-scatter.2.cloned.1.call-done = bf16[256,1024]{1,0:T(8,128)(2,1)} async-done(((bf16[256,4096]{1,0:T(8,128)(2,1)}), bf16[256,1024]{1,0:T(8,128)(2,1)}) %reduce-scatter.2.cloned.1.call-update) | async-done | bytes 524304 | tf_op jit(solution)/shard_map/reduce_scatter | solution.py:106
  (35 shorter events, 1.1 us)
Async XLA Ops:
  6.5 68.8 %copy-start = (bf16[3,512,1024]{2,1,0:T(8,128)(2,1)S(1)}, bf16[3,512,1024]{2,1,0:T(8,128)(2,1)}, u32[]{:S(2)}) copy-start(bf16[3,512,1024]{2,1,0:T(8,128)(2,1)} %param.15) | copy-start | bytes 9437188
  6.5 27.7 %all-gather.2.cloned.1.call-start = ((), (), s32[]{:S(2)}) async-start(), calls=%async_computation.4 | async-start | bytes 2621440 | tf_op jit(solution)/shard_map/all_gather | solution.py:63
  37.9 20.0 %all-to-all-start = ((bf16[32,8,512]{2,0,1:T(8,128)(2,1)}), bf16[32,8,512]{2,0,1:T(8,128)(2,1)S(1)}, u32[]{:S(2)}, u32[]{:S(2)}) async-start(bf16[32,8,512]{2,0,1:T(8,128)(2,1)} %bitcast.109), calls=%async_computation | async-start | bytes 524288 | tf_op jit(solution)/shard_map/all_to_all | solution.py:78
  57.9 14.9 %all-to-all-start.1 = ((bf16[32,8,512]{2,0,1:T(8,128)(2,1)}), bf16[32,8,512]{2,0,1:T(8,128)(2,1)}, u32[]{:S(2)}, u32[]{:S(2)}) async-start(bf16[32,8,512]{2,0,1:T(8,128)(2,1)} %bitcast.108), calls=%async_computation.1 | async-start | bytes 524288 | tf_op jit(solution)/shard_map/all_to_all | solution.py:81
  122.4 1.2 copy-start.1
  122.5 2.6 %copy-start.2 = (pred[8,32]{1,0:T(8,128)(4,1)S(1)}, pred[8,32]{1,0:T(8,128)(4,1)}, u32[]{:S(2)}) copy-start(pred[8,32]{1,0:T(8,128)(4,1)} %compare_and_fusion) | copy-start | bytes 772
  122.7 7.2 %copy-start.3 = (f32[2,2,128]{2,1,0:T(2,128)S(1)}, f32[2,2,128]{2,1,0:T(2,128)}, u32[]{:S(2)}) copy-start(f32[2,2,128]{2,1,0:T(2,128)} %fusion.15) | copy-start | bytes 6148
  125.9 12.2 %all-to-all-start.2 = ((bf16[8,32,512]{2,1,0:T(8,128)(2,1)}), bf16[8,32,512]{2,1,0:T(8,128)(2,1)S(1)}, u32[]{:S(2)}, u32[]{:S(2)}) async-start(bf16[8,32,512]{2,1,0:T(8,128)(2,1)} %select_convert_fusion), calls=%async_computation.2 | async-start | bytes 524288 | tf_op jit(solution)/shard_map/all_to_all | solution.py:100
  129.9 49.9 %reduce-scatter.2.cloned.1.call-start = ((), (), s32[]{:S(2)}) async-start(), calls=%async_computation.5 | async-start | bytes 2621440 | tf_op jit(solution)/shard_map/reduce_scatter | solution.py:106
  132.8 6.2 %copy-start.4 = (f32[1,32]{1,0:T(1,128)S(1)}, f32[1,32]{1,0:T(1,128)}, u32[]{:S(2)}) copy-start(f32[1,32]{1,0:T(1,128)} %param.19) | copy-start | bytes 388
Sparse Core Ops, SparseCore 0:
  8.9 25.2 all-gather.1
  148.9 30.8 reduce-scatter.1

commit v2 on v1

--- a/solution.py
+++ b/solution.py
@@ -1,13 +1,21 @@
+import functools
 import math
 
 import jax
 import jax.numpy as jnp
 from jax import lax
+from jax.experimental import pallas as pl
+from jax.experimental.pallas import tpu as pltpu
 from jax.sharding import PartitionSpec as P
 
 HD = 128
 LB = 128
 ROUTE = 32
+BF = jnp.bfloat16
+F32 = jnp.float32
+VMEM = pl.BlockSpec(memory_space=pltpu.VMEM)
+FIRST = (((0,), (0,)), ((), ()))
+LAST = (((1,), (1,)), ((), ()))
 
 
 def attend(queries, key_rows, value_rows):
@@ -50,7 +58,7 @@
     return jnp.where((own_list >= 0)[:, None], chosen, jnp.zeros_like(chosen))
 
 
-def per_device(
+def general(
     tokens,
     light_input,
     light_output,
@@ -106,6 +114,304 @@
     return lax.psum_scatter(combined.astype(jnp.bfloat16), "head", scatter_dimension=1, tiled=True)
 
 
+def own_row(table, index):
+    rows = lax.broadcasted_iota(jnp.int32, table.shape, 0)
+    return jnp.sum(jnp.where(rows == index, table, 0), axis=0, keepdims=True)
+
+
+def compact_onehot(flat, routed):
+    slots = flat.shape[1]
+    live = flat >= 0
+    before = lax.broadcasted_iota(jnp.int32, (slots, slots), 0) < lax.broadcasted_iota(
+        jnp.int32, (slots, slots), 1
+    )
+    place = jnp.dot(
+        live.astype(F32).astype(BF), before.astype(F32).astype(BF), preferred_element_type=F32
+    ).astype(jnp.int32)
+    row = lax.broadcasted_iota(jnp.int32, (routed, slots), 0)
+    return ((row == place) & live).astype(F32).astype(BF)
+
+
+def pick_kernel(where_ref, tok_ref, query_ref, source_ref, keep_ref, send_ref):
+    seq_index, odd = where_ref[0], where_ref[1] % 2
+    own_q = own_row(query_ref[...], seq_index)
+    own_s = own_row(source_ref[...], seq_index)
+    tok_rows = tok_ref.shape[0]
+    spot = lax.broadcasted_iota(jnp.int32, (tok_rows, own_q.shape[1]), 0)
+    for ref, wanted in ((keep_ref, 0), (send_ref, 1)):
+        listed = jnp.where(odd == wanted, own_q, own_s)
+        chosen = (spot == listed).astype(F32).astype(BF)
+        ref[...] = lax.dot_general(
+            chosen, tok_ref[...], FIRST, preferred_element_type=F32
+        ).astype(BF)
+
+
+def spread_kernel(where_ref, keep_ref, got_ref, out_ref):
+    odd = where_ref[1] % 2
+    keep, got = keep_ref[...], got_ref[...]
+    width = out_ref.shape[2]
+    per = keep.shape[1] // width
+    for part, block in enumerate((jnp.where(odd == 0, keep, got), jnp.where(odd == 0, got, keep))):
+        for j in range(per):
+            for at in range(part * per + j, out_ref.shape[0], 2 * per):
+                out_ref[at] = block[:, j * width : (j + 1) * width]
+
+
+def compact_kernel(where_ref, slots_ref, query_ref, source_ref, out_ref):
+    odd = where_ref[1] % 2
+    flat = jnp.where(odd == 0, query_ref[...], source_ref[...])
+    chosen = compact_onehot(flat, out_ref.shape[0])
+    rows = slots_ref[...].reshape(-1, slots_ref.shape[2])
+    out_ref[...] = jnp.dot(chosen, rows, preferred_element_type=F32).astype(BF)
+
+
+def project_kernel(where_ref, mine_ref, other_ref, weight_ref, out_ref):
+    odd = where_ref[1] % 2
+    mine, other = mine_ref[...], other_ref[...]
+    query = jnp.where(odd == 0, mine, other)
+    source = jnp.where(odd == 0, other, mine)
+    for c, rows in enumerate((query, source, source)):
+        part = jnp.dot(rows, weight_ref[c], preferred_element_type=F32).astype(BF)
+        for g in range(out_ref.shape[0]):
+            out_ref[g, c] = part[:, g * HD : (g + 1) * HD]
+
+
+def one_head(query, key, value):
+    scores = lax.dot_general(query, key, LAST, preferred_element_type=F32) / math.sqrt(HD)
+    expanded = jnp.exp(scores - jnp.max(scores, axis=-1, keepdims=True))
+    totals = jnp.sum(expanded, axis=-1, keepdims=True)
+    weighted = jnp.dot(expanded.astype(BF), value, preferred_element_type=F32)
+    return (weighted / totals).astype(BF)
+
+
+def heavy_attend_kernel(parts_ref, out_ref):
+    total = parts_ref[0].astype(F32)
+    for s in range(1, parts_ref.shape[0]):
+        total = total + parts_ref[s].astype(F32)
+    total = total.astype(BF)
+    result = one_head(total[0], total[1], total[2])
+    for s in range(out_ref.shape[0]):
+        out_ref[s] = result
+
+
+def heavy_output_kernel(heads_ref, weight_ref, query_ref, out_ref):
+    routed = heads_ref.shape[1]
+    part = jnp.zeros((routed, weight_ref.shape[1]), F32)
+    rows = jnp.concatenate([heads_ref[g] for g in range(heads_ref.shape[0])], axis=1)
+    part = jnp.dot(rows, weight_ref[...], preferred_element_type=F32).astype(BF)
+    chosen = compact_onehot(query_ref[...], routed)
+    spread = lax.dot_general(chosen, part, FIRST, preferred_element_type=F32).astype(BF)
+    out_ref[...] = spread.reshape(out_ref.shape)
+
+
+def finish_kernel(where_ref, light_ref, mine_ref, got_ref, last_ref, query_ref, gate_ref, out_ref):
+    seq_index, head = where_ref[0], where_ref[1]
+    per = last_ref.shape[0]
+    own_q = own_row(query_ref[...], seq_index)
+    slots = own_q.shape[1]
+    at = pl.multiple_of(head * per, per)
+    outer = pl.multiple_of((head // 2) * per, per)
+    heavy = (
+        mine_ref[pl.ds(at, per)].astype(F32)
+        + got_ref[pl.ds(outer, per)].astype(F32)
+        + last_ref[...].astype(F32)
+    )
+    diagonal = lax.broadcasted_iota(jnp.int32, (slots, slots), 0) == lax.broadcasted_iota(
+        jnp.int32, (slots, slots), 1
+    )
+    gate = jnp.sum(jnp.where(diagonal, gate_ref[...], 0.0), axis=1, keepdims=True)
+    tok_rows = light_ref.shape[0]
+    spot = lax.broadcasted_iota(jnp.int32, (tok_rows, slots), 0)
+    chosen = (spot == own_q).astype(F32).astype(BF)
+    width = heavy.shape[2]
+    for j in range(per):
+        scaled = heavy[j] * gate
+        coarse = scaled.astype(BF)
+        fine = (scaled - coarse.astype(F32)).astype(BF)
+        added = jnp.dot(chosen, coarse, preferred_element_type=F32) + jnp.dot(
+            chosen, fine, preferred_element_type=F32
+        )
+        cols = slice(j * width, (j + 1) * width)
+        out_ref[:, cols] = (light_ref[:, cols].astype(F32) + added).astype(BF)
+
+
+def light_kernel(tok_ref, weight_ref, out_ref, acc_ref):
+    step = pl.program_id(0)
+
+    @pl.when(step == 0)
+    def _():
+        acc_ref[...] = jnp.zeros_like(acc_ref)
+
+    for c in range(3):
+        acc_ref[c] += jnp.dot(tok_ref[...], weight_ref[c], preferred_element_type=F32)
+
+    @pl.when(step == pl.num_programs(0) - 1)
+    def _():
+        for b in range(out_ref.shape[0] // LB):
+            for g in range(out_ref.shape[1] // HD):
+                at = (slice(b * LB, (b + 1) * LB), slice(g * HD, (g + 1) * HD))
+                out_ref[at] = one_head(*(acc_ref[(c, *at)].astype(BF) for c in range(3)))
+
+
+def light_output_kernel(heads_ref, weight_ref, out_ref):
+    out_ref[...] = jnp.dot(heads_ref[...], weight_ref[...], preferred_element_type=F32).astype(BF)
+
+
+def cost(flops, moved):
+    return pl.CostEstimate(flops=int(flops), bytes_accessed=int(moved), transcendentals=0)
+
+
+SMEM = pl.BlockSpec(memory_space=pltpu.SMEM)
+
+
+def one_head_a_device(
+    tokens,
+    light_input,
+    light_output,
+    heavy_input,
+    heavy_output,
+    query_tokens,
+    context_tokens,
+    query_gate,
+):
+    seq_count, head_count = lax.axis_size("seq"), lax.axis_size("head")
+    seq_index, head_index = lax.axis_index("seq"), lax.axis_index("head")
+    where = jnp.stack([seq_index, head_index]).astype(jnp.int32)
+    tok_rows, own_width = tokens.shape
+    slots = query_tokens.shape[1]
+    routed = seq_count * tok_rows // ROUTE
+    part_width = heavy_input.shape[1]
+    head_cols = heavy_input.shape[2]
+    out_cols = heavy_output.shape[1]
+    flat_q = query_tokens.reshape(1, -1)
+    flat_s = context_tokens.reshape(1, -1)
+    pair = [(i, i ^ 1) for i in range(head_count)]
+    across = [(i, i ^ 2) for i in range(head_count)]
+    half = seq_count // (head_count // 2)
+
+    gathered = lax.all_gather(tokens, "head", axis=1, tiled=True)
+    full = gathered.shape[1]
+    light_cols = light_input.shape[2]
+    tile = part_width
+    light_heads = pl.pallas_call(
+        light_kernel,
+        grid=(full // tile,),
+        in_specs=[
+            pl.BlockSpec((tok_rows, tile), lambda i: (0, i)),
+            pl.BlockSpec((3, tile, light_cols), lambda i: (0, i, 0)),
+        ],
+        out_specs=pl.BlockSpec((tok_rows, light_cols), lambda i: (0, 0)),
+        out_shape=jax.ShapeDtypeStruct((tok_rows, light_cols), BF),
+        scratch_shapes=[pltpu.VMEM((3, tok_rows, light_cols), F32)],
+        cost_estimate=cost(6 * tok_rows * full * light_cols, 2 * full * (3 * light_cols + tok_rows)),
+    )(gathered, light_input)
+    wide = light_output.shape[1]
+    light_part = pl.pallas_call(
+        light_output_kernel,
+        grid=(wide // own_width,),
+        in_specs=[
+            pl.BlockSpec((tok_rows, light_cols), lambda i: (0, 0)),
+            pl.BlockSpec((light_cols, own_width), lambda i: (0, i)),
+        ],
+        out_specs=pl.BlockSpec((tok_rows, own_width), lambda i: (0, i)),
+        out_shape=jax.ShapeDtypeStruct((tok_rows, wide), BF),
+        cost_estimate=cost(2 * tok_rows * light_cols * wide, 2 * wide * (light_cols + tok_rows)),
+    )(light_heads, light_output)
+    light = lax.psum_scatter(light_part, "head", scatter_dimension=1, tiled=True)
+
+    keep, send = pl.pallas_call(
+        pick_kernel,
+        in_specs=[SMEM, VMEM, VMEM, VMEM],
+        out_specs=[VMEM, VMEM],
+        out_shape=[jax.ShapeDtypeStruct((slots, own_width), BF)] * 2,
+        cost_estimate=cost(4 * slots * tok_rows * own_width, 2 * tok_rows * own_width),
+    )(where, tokens, query_tokens, context_tokens)
+    got = lax.ppermute(send, "head", pair)
+    spread = pl.pallas_call(
+        spread_kernel,
+        in_specs=[SMEM, VMEM, VMEM],
+        out_specs=VMEM,
+        out_shape=jax.ShapeDtypeStruct((seq_count, slots, part_width), BF),
+        cost_estimate=cost(0, 4 * seq_count * slots * part_width),
+    )(where, keep, got)
+    spread = lax.all_to_all(spread, "seq", split_axis=0, concat_axis=0, tiled=True)
+    mine = pl.pallas_call(
+        compact_kernel,
+        in_specs=[SMEM, VMEM, VMEM, VMEM],
+        out_specs=VMEM,
+        out_shape=jax.ShapeDtypeStruct((routed, part_width), BF),
+        cost_estimate=cost(0, 4 * seq_count * slots * part_width),
+    )(where, spread, flat_q, flat_s)
+    holds = [
+        (s * head_count + h, s * head_count + (h ^ 2))
+        for s in range(seq_count)
+        for h in range(head_count)
+        if s // half == h // 2
+    ]
+    crossed = lax.ppermute(mine, ("seq", "head"), holds)
+    mine = jnp.where(seq_index // half == head_index // 2, mine, crossed)
+    other = lax.ppermute(mine, "head", pair)
+    group = 2
+    parts = pl.pallas_call(
+        project_kernel,
+        grid=(head_cols // (group * HD),),
+        in_specs=[
+            SMEM,
+            pl.BlockSpec((routed, part_width), lambda i: (0, 0)),
+            pl.BlockSpec((routed, part_width), lambda i: (0, 0)),
+            pl.BlockSpec((3, part_width, group * HD), lambda i: (0, 0, i)),
+        ],
+        out_specs=pl.BlockSpec((group, 3, routed, HD), lambda i: (i, 0, 0, 0)),
+        out_shape=jax.ShapeDtypeStruct((seq_count, 3, routed, HD), BF),
+        cost_estimate=cost(6 * routed * part_width * head_cols, 6 * part_width * head_cols),
+    )(where, mine, other, heavy_input)
+    parts = lax.all_to_all(parts, "seq", split_axis=0, concat_axis=0, tiled=True)
+    heads = pl.pallas_call(
+        heavy_attend_kernel,
+        in_specs=[VMEM],
+        out_specs=VMEM,
+        out_shape=jax.ShapeDtypeStruct((seq_count, routed, HD), BF),
+        cost_estimate=cost(0, 8 * seq_count * routed * HD),
+    )(parts)
+    heads = lax.all_to_all(heads, "seq", split_axis=0, concat_axis=0, tiled=True)
+    outgoing = pl.pallas_call(
+        heavy_output_kernel,
+        in_specs=[VMEM, VMEM, VMEM],
+        out_specs=VMEM,
+        out_shape=jax.ShapeDtypeStruct((seq_count, slots, out_cols), BF),
+        cost_estimate=cost(2 * routed * head_cols * out_cols, 2 * head_cols * out_cols),
+    )(heads, heavy_output, flat_q)
+    returned = lax.all_to_all(outgoing, "seq", split_axis=0, concat_axis=0, tiled=True)
+    per = seq_count // head_count
+    view = returned.reshape(head_count // 2, 2, per, slots, out_cols)
+    odd = head_index % 2
+    give = lax.dynamic_index_in_dim(view, 1 - odd, 1, keepdims=False)
+    got_pair = lax.ppermute(give, "head", pair)
+    far = 1 - head_index // 2
+    give = (
+        lax.dynamic_index_in_dim(
+            lax.dynamic_index_in_dim(view, far, 0, keepdims=False), odd, 0, keepdims=False
+        ).astype(F32)
+        + lax.dynamic_index_in_dim(got_pair, far, 0, keepdims=False).astype(F32)
+    ).astype(BF)
+    last = lax.ppermute(give, "head", across)
+    return pl.pallas_call(
+        finish_kernel,
+        in_specs=[SMEM] + [VMEM] * 6,
+        out_specs=VMEM,
+        out_shape=jax.ShapeDtypeStruct((tok_rows, own_width), BF),
+        cost_estimate=cost(0, 4 * tok_rows * own_width),
+    )(
+        where,
+        light,
+        returned,
+        got_pair.reshape(-1, slots, out_cols),
+        last,
+        query_tokens,
+        query_gate,
+    )
+
+
 def solution(mesh):
     placed = (
         P("seq", "head"),
@@ -117,6 +423,13 @@
         P(),
         P("seq", None),
     )
+
+    def per_device(*args):
+        seq_count, head_count = mesh.shape["seq"], mesh.shape["head"]
+        local_heads = args[3].shape[2] // HD
+        fits = head_count // 2 == 2 and seq_count % head_count == 0 and local_heads == seq_count
+        return (one_head_a_device if fits else general)(*args)
+
     return jax.shard_map(
         per_device, mesh=mesh, in_specs=placed, out_specs=P("seq", "head"), check_vma=False
     )

time: 188 us -> 146 us (0.78)
  Pallas kernels: 0 us -> 30 us
  other arithmetic: 22.4 us -> 1.52 us
  blocking collectives: 45.5 us -> 28.7 us
  matrix products: 15.5 us -> 0 us
  local copies, waits for them, and re-layouts: 18.6 us -> 3.9 us
  starting transfers between devices: 15.5 us -> 12.7 us
    psum x1 -> x0, blocking collectives: 45.5 us -> none  [per_device(): lax.psum(project(query_rows, source_rows, heavy_input), 'seq')]
    reduce_scatter x1, waiting for transfers between devices: 31 us -> 0.01 us  [one_head_a_device(): lax.psum_scatter(light_part, 'head', scatter_dimension=1, tiled=True)]
    pallas_call x0 -> x9, Pallas kernels: none -> 30 us  [the longest x1 8.81 us: one_head_a_device(): pl.pallas_call(light_kernel, grid=(full // tile,), in_specs=[pl.BlockSpec...]
    all_to_all x0 -> x2, blocking collectives: none -> 28.7 us  [the longest x1 17.4 us: one_head_a_device(): lax.all_to_all(parts, 'seq', split_axis=0, concat_axis=0, tiled=True)]
    dot_general x8 -> x0, matrix products: 15.5 us -> none  [the longest x1 5.25 us: per_device(): jnp.einsum('td,cdw->ctw', gathered, light_input, preferred_element_type=j...]
    all_to_all x3 -> x2, waiting for transfers between devices: 4.34 us -> 16.1 us  [the longest x1 8.14 us: one_head_a_device(): lax.all_to_all(outgoing, 'seq', split_axis=0, concat_axis=0, tiled=True)]
    ppermute x0 -> x5, waiting for transfers between devices: none -> 10.6 us  [the longest x1 3.42 us: one_head_a_device(): crossed = lax.ppermute(mine, ('seq', 'head'), holds)]
    gather x5 -> x0, local copies, waits for them, and re-layouts: 9.99 us -> none  [the longest x2 6.33 us: pick_rows(): chosen = jnp.take(gathered, jnp.maximum(own_list, 0), axis=0)]
  transfers between devices with their start and end apart: 5 -> 9, of which waited for: 4 -> 8; matrix products, arithmetic and copies ran while one was open for 19% -> 2% of each run, Pallas kernels for 0% -> 10%
where the time goes in v2:
time: 146 us; the launch traced here: 145 us
  waiting for transfers between devices  54.4 us (37%)
  Pallas kernels  30 us (21%)
  blocking collectives  28.7 us (20%)
  between operations  13.5 us (9%)
  starting transfers between devices  12.7 us (9%)
  local copies, waits for them, and re-layouts  3.9 us (3%)
  other arithmetic  1.52 us (1%)
    all_gather x1, waiting for transfers between devices, one_head_a_device(): gathered = lax.all_gather(tokens, 'head', axis=1, tiled=True)  26.9 us
    all_to_all x1, blocking collectives, one_head_a_device(): lax.all_to_all(parts, 'seq', split_axis=0, concat_axis=0, tiled=True)  17.4 us
    all_to_all x1, blocking collectives, one_head_a_device(): lax.all_to_all(heads, 'seq', split_axis=0, concat_axis=0, tiled=True)  11.3 us
    pallas_call x1, Pallas kernels, one_head_a_device(): pl.pallas_call(light_kernel, grid=(full // tile,), in_specs=[pl.BlockSpec...  8.81 us
    all_to_all x1, waiting for transfers between devices, one_head_a_device(): lax.all_to_all(outgoing, 'seq', split_axis=0, concat_axis=0, tiled=True)  8.14 us
    all_to_all x1, waiting for transfers between devices, one_head_a_device(): lax.all_to_all(spread, 'seq', split_axis=0, concat_axis=0, tiled=True)  8 us
    all_to_all x1, starting transfers between devices, one_head_a_device(): lax.all_to_all(spread, 'seq', split_axis=0, concat_axis=0, tiled=True)  5.46 us
    pallas_call x1, Pallas kernels, one_head_a_device(): pl.pallas_call(light_output_kernel, grid=(wide // own_width,), in_specs=[...  4.41 us
  transfers between devices with their start and end apart: 9, of which 8 were waited for; matrix products, arithmetic and copies ran while one was open for 2% of the time, Pallas kernels for 10%

profile of v2, /device:TPU:0, one launch (start us, length us, event | category | flops | bytes accessed | tf_op | source)
XLA Modules:
  0.0 144.7 jit_solution(16895186094251084997)
XLA Ops:
  6.5 0.0 all-gather.2.cloned.1.call-start
  6.5 0.7 all-gather.2.cloned.1.call-update
  7.3 0.0 reduce-scatter.2.cloned.1.call-start
  7.3 26.9 %all-gather.2.cloned.1.call-done.tok_ref = bf16[256,4096]{1,0:T(8,128)(2,1)} async-done(((bf16[256,1024]{1,0:T(8,128)(2,1)}), bf16[256,4096]{1,0:T(8,128)(2,1)}) %all-gather.2.cloned.1.call-update) | async-done | bytes 2097168 | tf_op jit(solution)/shard_map/all_gather | solution.py:292
  34.2 8.8 %shard_map.82.heads_ref = bf16[256,256]{1,0:T(8,128)(2,1)} custom-call(bf16[256,4096]{1,0:T(8,128)(2,1)} %all-gather.2.cloned.1.call-done.tok_ref, bf16[3,4096,256]{2,1,0:T(8,128)(2,1)} %weight_ref.4), custom_call_target="tpu_custom_call" | custom-call | flops 1610612736 | bytes 8388608 | tf_op jit(solution)/shard_map/pallas_call | solution.py:296
  43.0 4.4 %shard_map.83 = bf16[256,4096]{1,0:T(8,128)(2,1)} custom-call(bf16[256,256]{1,0:T(8,128)(2,1)} %shard_map.82.heads_ref, bf16[256,4096]{1,0:T(8,128)(2,1)} %weight_ref.5), custom_call_target="tpu_custom_call" | custom-call | flops 536870912 | bytes 4194304 | tf_op jit(solution)/shard_map/pallas_call | solution.py:309
  47.5 0.0 copy-start.7
  47.5 0.0 copy-start.8
  47.5 0.0 reduce-scatter.2.cloned.1.call-update
  47.5 0.7 pad_add_fusion.where_ref
  48.1 2.0 %shard_map.84 = (bf16[32,1024]{1,0:T(8,128)(2,1)}, bf16[32,1024]{1,0:T(8,128)(2,1)}) custom-call(s32[2]{0:T(128)} %pad_add_fusion.where_ref, bf16[256,1024]{1,0:T(8,128)(2,1)} %tok_ref.1, s32[8,32]{1,0:T(8,128)} %query_ref.3, s32[8,32]{1,0:T(8,128)} %source_ref.1), custom_call_target="tpu_custom_call" | custom-call | flops 33554432 | bytes 524288 | tf_op jit(solution)/shard_map/pallas_call | solution.py:322
  50.2 0.2 collective-permute-start
  50.4 1.2 collective-permute-done.got_ref
  51.6 0.0 copy-start.6
  51.6 0.6 copy-done.6
  52.3 1.7 %shard_map.85 = bf16[8,32,512]{2,1,0:T(8,128)(2,1)} custom-call(s32[2]{0:T(128)} %pad_add_fusion.where_ref, bf16[32,1024]{1,0:T(8,128)(2,1)} %get-tuple-element.7.keep_ref, bf16[32,1024]{1,0:T(8,128)(2,1)} %copy-done.6), custom_call_target="tpu_custom_call" | custom-call | bytes 524288 | tf_op jit(solution)/shard_map/pallas_call | solution.py:330
  53.9 5.5 %all-to-all-start = ((bf16[8,32,512]{2,1,0:T(8,128)(2,1)}), bf16[8,32,512]{2,1,0:T(8,128)(2,1)S(1)}, u32[]{:S(2)}, u32[]{:S(2)}) async-start(bf16[8,32,512]{2,1,0:T(8,128)(2,1)} %shard_map.85), calls=%async_computation.1 | async-start | bytes 524288 | tf_op jit(solution)/shard_map/all_to_all | solution.py:337
  59.4 0.0 copy-done.7
  59.4 0.6 reshape.18.query_ref
  60.0 0.0 copy-done.8
  60.0 0.7 reshape.19.source_ref
  60.7 8.0 %all-to-all-done.slots_ref = bf16[8,32,512]{2,1,0:T(8,128)(2,1)S(1)} async-done(((bf16[8,32,512]{2,1,0:T(8,128)(2,1)}), bf16[8,32,512]{2,1,0:T(8,128)(2,1)S(1)}, u32[]{:S(2)}, u32[]{:S(2)}) %all-to-all-start) | async-done | bytes 262176 | tf_op jit(solution)/shard_map/all_to_all | solution.py:337
  68.7 0.0 copy-start.1
  68.7 0.7 copy-done.1
  69.4 1.9 %shard_map.86 = bf16[64,512]{1,0:T(8,128)(2,1)} custom-call(s32[2]{0:T(128)} %pad_add_fusion.where_ref, bf16[8,32,512]{2,1,0:T(8,128)(2,1)} %copy-done.1, s32[1,256]{1,0:T(1,128)} %reshape.18.query_ref, s32[1,256]{1,0:T(1,128)} %reshape.19.source_ref), custom_call_target="tpu_custom_call" | custom-call | bytes 524288 | tf_op jit(solution)/shard_map/pallas_call | solution.py:338
  71.3 2.4 %collective-permute-start.1 = (bf16[64,512]{1,0:T(8,128)(2,1)}, bf16[64,512]{1,0:T(8,128)(2,1)S(1)}, u32[]{:S(2)}, u32[]{:S(2)}) collective-permute-start(bf16[64,512]{1,0:T(8,128)(2,1)} %shard_map.86), channel_id=1, source_target_pairs={{0,2},{1,3},{4,6},{5,7},{8,10},{9,11},{12,14},{13,15},{18,16},{19,... | collective-permute-start | bytes 196616 | tf_op jit(solution)/shard_map/ppermute | solution.py:351
  73.8 3.4 %collective-permute-done.1 = bf16[64,512]{1,0:T(8,128)(2,1)S(1)} collective-permute-done((bf16[64,512]{1,0:T(8,128)(2,1)}, bf16[64,512]{1,0:T(8,128)(2,1)S(1)}, u32[]{:S(2)}, u32[]{:S(2)}) %collective-permute-start.1) | collective-permute-done | bytes 65568 | tf_op jit(solution)/shard_map/ppermute | solution.py:351
  77.2 0.8 broadcast_select_fusion.mine_ref
  78.1 0.0 copy-start.3
  78.1 0.1 collective-permute-start.2
  78.2 1.2 collective-permute-done.2.other_ref
  79.4 0.0 copy-done.3
  79.4 0.6 copy-done.4
  80.0 4.2 %shard_map.87 = bf16[8,3,64,128]{3,2,1,0:T(8,128)(2,1)} custom-call(s32[2]{0:T(128)} %pad_add_fusion.where_ref, bf16[64,512]{1,0:T(8,128)(2,1)} %copy-done.3, bf16[64,512]{1,0:T(8,128)(2,1)} %copy-done.4, bf16[3,512,1024]{2,1,0:T(8,128)(2,1)} %weight_ref.6), custom_call_target="tpu_custom_call" | custom-call | flops 201326592 | bytes 3145728 | tf_op jit(solution)/shard_map/pallas_call | solution.py:355
  84.2 17.4 %all_to_all.20.parts_ref = bf16[8,3,64,128]{3,2,1,0:T(8,128)(2,1)} all-to-all(bf16[8,3,64,128]{3,2,1,0:T(8,128)(2,1)} %shard_map.87), channel_id=1, replica_groups=mesh['seq'=8,'head'=4] {'seq'}, dimensions={0} | all-to-all | bytes 786432 | tf_op jit(solution)/shard_map/all_to_all | solution.py:368
  101.6 2.0 %shard_map.88 = bf16[8,64,128]{2,1,0:T(8,128)(2,1)} custom-call(bf16[8,3,64,128]{3,2,1,0:T(8,128)(2,1)} %all_to_all.20.parts_ref), custom_call_target="tpu_custom_call" | custom-call | bytes 524288 | tf_op jit(solution)/shard_map/pallas_call | solution.py:369
  103.6 11.3 %all_to_all.21.heads_ref = bf16[8,64,128]{2,1,0:T(8,128)(2,1)} all-to-all(bf16[8,64,128]{2,1,0:T(8,128)(2,1)} %shard_map.88), channel_id=1, replica_groups=mesh['seq'=8,'head'=4] {'seq'}, dimensions={0} | all-to-all | bytes 262144 | tf_op jit(solution)/shard_map/all_to_all | solution.py:376
  114.9 2.5 %shard_map.89 = bf16[8,32,512]{2,1,0:T(8,128)(2,1)} custom-call(bf16[8,64,128]{2,1,0:T(8,128)(2,1)} %all_to_all.21.heads_ref, bf16[1024,512]{1,0:T(8,128)(2,1)} %weight_ref.7, s32[1,256]{1,0:T(1,128)} %reshape.18.query_ref), custom_call_target="tpu_custom_call" | custom-call | flops 67108864 | bytes 1048576 | tf_op jit(solution)/shard_map/pallas_call | solution.py:377
  117.4 3.4 %all-to-all-start.3 = ((bf16[8,32,512]{2,1,0:T(8,128)(2,1)}), bf16[8,32,512]{2,1,0:T(8,128)(2,1)S(1)}, u32[]{:S(2)}, u32[]{:S(2)}) async-start(bf16[8,32,512]{2,1,0:T(8,128)(2,1)} %shard_map.89), calls=%async_computation.4 | async-start | bytes 524288 | tf_op jit(solution)/shard_map/all_to_all | solution.py:384
  120.9 8.1 %all-to-all-done.3.mine_ref = bf16[8,32,512]{2,1,0:T(8,128)(2,1)S(1)} async-done(((bf16[8,32,512]{2,1,0:T(8,128)(2,1)}), bf16[8,32,512]{2,1,0:T(8,128)(2,1)S(1)}, u32[]{:S(2)}, u32[]{:S(2)}) %all-to-all-start.3) | async-done | bytes 262176 | tf_op jit(solution)/shard_map/all_to_all | solution.py:384
  129.0 0.1 collective-permute-start.3
  129.1 1.3 collective-permute-done.3
  130.5 1.0 collective-permute-start.4
  131.4 3.4 %collective-permute-done.4.last_ref = bf16[2,32,512]{2,1,0:T(8,128)(2,1)S(1)} collective-permute-done((bf16[2,32,512]{2,1,0:T(8,128)(2,1)S(1)}, bf16[2,32,512]{2,1,0:T(8,128)(2,1)S(1)}, u32[]{:S(2)}, u32[]{:S(2)}) %collective-permute-start.4) | collective-permute-done | bytes 65568 | tf_op jit(solution)/shard_map/ppermute | solution.py:397
  134.8 0.0 copy-done
  134.8 0.0 copy-done.2
  134.8 0.6 copy-done.5
  135.4 2.5 %shard_map.90 = bf16[256,1024]{1,0:T(8,128)(2,1)} custom-call(s32[2]{0:T(128)} %pad_add_fusion.where_ref, bf16[256,1024]{1,0:T(8,128)(2,1)} %reduce-scatter.2.cloned.1.call-done.light_ref, bf16[8,32,512]{2,1,0:T(8,128)(2,1)} %copy-done, bf16[4,32,512]{2,1,0:T(8,128)(2,1)} %bitcast.14, bf16[2,32,512]{2,1,0:T(8,128)(2,1)} %copy-done.5, s32[8,32]{1,0:T(8,128)} %query_ref.3, ...), custom_call_target="tpu_custom_call" | custom-call | bytes 1048576 | tf_op jit(solution)/shard_map/pallas_call | solution.py:398
  (7 shorter events, 0.0 us)
Async XLA Ops:
  6.5 27.7 %all-gather.2.cloned.1.call-start = ((), (), s32[]{:S(2)}) async-start(), calls=%async_computation.5 | async-start | bytes 2621440 | tf_op jit(solution)/shard_map/all_gather | solution.py:292
  7.3 127.5 %reduce-scatter.2.cloned.1.call-start = ((), (), s32[]{:S(2)}) async-start(), calls=%async_computation.6 | async-start | bytes 2621440 | tf_op jit(solution)/shard_map/reduce_scatter | solution.py:320
  47.5 11.9 %copy-start.7 = (s32[8,32]{1,0:T(8,128)S(1)}, s32[8,32]{1,0:T(8,128)}, u32[]{:S(2)}) copy-start(s32[8,32]{1,0:T(8,128)} %query_ref.3) | copy-start | bytes 3076
  47.5 12.6 %copy-start.8 = (s32[8,32]{1,0:T(8,128)S(1)}, s32[8,32]{1,0:T(8,128)}, u32[]{:S(2)}) copy-start(s32[8,32]{1,0:T(8,128)} %source_ref.1) | copy-start | bytes 3076
  50.2 1.5 %collective-permute-start = (bf16[32,1024]{1,0:T(8,128)(2,1)}, bf16[32,1024]{1,0:T(8,128)(2,1)S(1)}, u32[]{:S(2)}, u32[]{:S(2)}) collective-permute-start(bf16[32,1024]{1,0:T(8,128)(2,1)} %get-tuple-element.8), channel_id=1, source_target_pairs={{0,1},{1,0},{2,3},{3,2},{4,5},{5,4},{6,7},{7,6},{8,9},{9,8},{10,11... | collective-permute-start | bytes 196616 | tf_op jit(solution)/shard_map/ppermute | solution.py:329
  51.6 0.6 copy-start.6
  53.9 14.8 %all-to-all-start = ((bf16[8,32,512]{2,1,0:T(8,128)(2,1)}), bf16[8,32,512]{2,1,0:T(8,128)(2,1)S(1)}, u32[]{:S(2)}, u32[]{:S(2)}) async-start(bf16[8,32,512]{2,1,0:T(8,128)(2,1)} %shard_map.85), calls=%async_computation.1 | async-start | bytes 524288 | tf_op jit(solution)/shard_map/all_to_all | solution.py:337
  68.7 0.7 copy-start.1
  71.3 5.9 %collective-permute-start.1 = (bf16[64,512]{1,0:T(8,128)(2,1)}, bf16[64,512]{1,0:T(8,128)(2,1)S(1)}, u32[]{:S(2)}, u32[]{:S(2)}) collective-permute-start(bf16[64,512]{1,0:T(8,128)(2,1)} %shard_map.86), channel_id=1, source_target_pairs={{0,2},{1,3},{4,6},{5,7},{8,10},{9,11},{12,14},{13,15},{18,16},{19,... | collective-permute-start | bytes 196616 | tf_op jit(solution)/shard_map/ppermute | solution.py:351
  78.1 1.3 copy-start.3
  78.1 1.3 collective-permute-start.2
  79.4 0.6 copy-start.4
  117.4 11.6 %all-to-all-start.3 = ((bf16[8,32,512]{2,1,0:T(8,128)(2,1)}), bf16[8,32,512]{2,1,0:T(8,128)(2,1)S(1)}, u32[]{:S(2)}, u32[]{:S(2)}) async-start(bf16[8,32,512]{2,1,0:T(8,128)(2,1)} %shard_map.89), calls=%async_computation.4 | async-start | bytes 524288 | tf_op jit(solution)/shard_map/all_to_all | solution.py:384
  129.0 5.8 %copy-start = (bf16[8,32,512]{2,1,0:T(8,128)(2,1)}, bf16[8,32,512]{2,1,0:T(8,128)(2,1)S(1)}, u32[]{:S(2)}) copy-start(bf16[8,32,512]{2,1,0:T(8,128)(2,1)S(1)} %all-to-all-done.3.mine_ref) | copy-start | bytes 786436
  129.0 1.4 collective-permute-start.3
  130.4 4.4 %copy-start.2 = (bf16[2,2,32,512]{3,2,1,0:T(8,128)(2,1)}, bf16[2,2,32,512]{3,2,1,0:T(8,128)(2,1)S(1)}, u32[]{:S(2)}) copy-start(bf16[2,2,32,512]{3,2,1,0:T(8,128)(2,1)S(1)} %collective-permute-done.3) | copy-start | bytes 393220
  130.5 4.3 %collective-permute-start.4 = (bf16[2,32,512]{2,1,0:T(8,128)(2,1)S(1)}, bf16[2,32,512]{2,1,0:T(8,128)(2,1)S(1)}, u32[]{:S(2)}, u32[]{:S(2)}) collective-permute-start(bf16[2,32,512]{2,1,0:T(8,128)(2,1)S(1)} %fusion), channel_id=1, source_target_pairs={{0,2},{1,3},{2,0},{3,1},{4,6},{5,7},{6,4},{7,5},{8,10},{9,11},{10,... | collective-permute-start | bytes 196616 | tf_op jit(solution)/shard_map/ppermute | solution.py:397
  134.8 0.6 copy-start.5
Sparse Core Ops, SparseCore 0:
  8.9 25.2 all-gather.1
  47.6 31.4 reduce-scatter.1

commit v3 on v2

--- a/solution.py
+++ b/solution.py
@@ -290,34 +290,6 @@
     half = seq_count // (head_count // 2)
 
     gathered = lax.all_gather(tokens, "head", axis=1, tiled=True)
-    full = gathered.shape[1]
-    light_cols = light_input.shape[2]
-    tile = part_width
-    light_heads = pl.pallas_call(
-        light_kernel,
-        grid=(full // tile,),
-        in_specs=[
-            pl.BlockSpec((tok_rows, tile), lambda i: (0, i)),
-            pl.BlockSpec((3, tile, light_cols), lambda i: (0, i, 0)),
-        ],
-        out_specs=pl.BlockSpec((tok_rows, light_cols), lambda i: (0, 0)),
-        out_shape=jax.ShapeDtypeStruct((tok_rows, light_cols), BF),
-        scratch_shapes=[pltpu.VMEM((3, tok_rows, light_cols), F32)],
-        cost_estimate=cost(6 * tok_rows * full * light_cols, 2 * full * (3 * light_cols + tok_rows)),
-    )(gathered, light_input)
-    wide = light_output.shape[1]
-    light_part = pl.pallas_call(
-        light_output_kernel,
-        grid=(wide // own_width,),
-        in_specs=[
-            pl.BlockSpec((tok_rows, light_cols), lambda i: (0, 0)),
-            pl.BlockSpec((light_cols, own_width), lambda i: (0, i)),
-        ],
-        out_specs=pl.BlockSpec((tok_rows, own_width), lambda i: (0, i)),
-        out_shape=jax.ShapeDtypeStruct((tok_rows, wide), BF),
-        cost_estimate=cost(2 * tok_rows * light_cols * wide, 2 * wide * (light_cols + tok_rows)),
-    )(light_heads, light_output)
-    light = lax.psum_scatter(light_part, "head", scatter_dimension=1, tiled=True)
 
     keep, send = pl.pallas_call(
         pick_kernel,
@@ -365,7 +337,38 @@
         out_shape=jax.ShapeDtypeStruct((seq_count, 3, routed, HD), BF),
         cost_estimate=cost(6 * routed * part_width * head_cols, 6 * part_width * head_cols),
     )(where, mine, other, heavy_input)
+    gathered, parts = lax.optimization_barrier((gathered, parts))
+    full = gathered.shape[1]
+    light_cols = light_input.shape[2]
+    tile = part_width
+    light_heads = pl.pallas_call(
+        light_kernel,
+        grid=(full // tile,),
+        in_specs=[
+            pl.BlockSpec((tok_rows, tile), lambda i: (0, i)),
+            pl.BlockSpec((3, tile, light_cols), lambda i: (0, i, 0)),
+        ],
+        out_specs=pl.BlockSpec((tok_rows, light_cols), lambda i: (0, 0)),
+        out_shape=jax.ShapeDtypeStruct((tok_rows, light_cols), BF),
+        scratch_shapes=[pltpu.VMEM((3, tok_rows, light_cols), F32)],
+        cost_estimate=cost(6 * tok_rows * full * light_cols, 2 * full * (3 * light_cols + tok_rows)),
+    )(gathered, light_input)
+    wide = light_output.shape[1]
+    light_part = pl.pallas_call(
+        light_output_kernel,
+        grid=(wide // own_width,),
+        in_specs=[
+            pl.BlockSpec((tok_rows, light_cols), lambda i: (0, 0)),
+            pl.BlockSpec((light_cols, own_width), lambda i: (0, i)),
+        ],
+        out_specs=pl.BlockSpec((tok_rows, own_width), lambda i: (0, i)),
+        out_shape=jax.ShapeDtypeStruct((tok_rows, wide), BF),
+        cost_estimate=cost(2 * tok_rows * light_cols * wide, 2 * wide * (light_cols + tok_rows)),
+    )(light_heads, light_output)
+
     parts = lax.all_to_all(parts, "seq", split_axis=0, concat_axis=0, tiled=True)
+    parts, light_part = lax.optimization_barrier((parts, light_part))
+    light = lax.psum_scatter(light_part, "head", scatter_dimension=1, tiled=True)
     heads = pl.pallas_call(
         heavy_attend_kernel,
         in_specs=[VMEM],

time: 146 us -> 109 us (0.75)
  waiting for transfers between devices: 54.4 us -> 24.3 us
  blocking collectives: 28.7 us -> 13.4 us
  starting transfers between devices: 12.7 us -> 19.5 us
  local copies, waits for them, and re-layouts: 3.9 us -> 5.89 us
    all_gather x1, waiting for transfers between devices: 26.9 us -> 0.01 us  [one_head_a_device(): gathered = lax.all_gather(tokens, 'head', axis=1, tiled=True)]
    all_to_all x1 -> x0, blocking collectives: 17.4 us -> none  [one_head_a_device(): lax.all_to_all(parts, 'seq', split_axis=0, concat_axis=0, tiled=True)]
    all_to_all x0 -> x1, starting transfers between devices: none -> 3.52 us  [one_head_a_device(): lax.all_to_all(parts, 'seq', split_axis=0, concat_axis=0, tiled=True)]
    all_to_all x1, blocking collectives: 11.3 us -> 13.4 us  [one_head_a_device(): lax.all_to_all(heads, 'seq', split_axis=0, concat_axis=0, tiled=True)]
    all_to_all x1, starting transfers between devices: 5.46 us -> 7.18 us  [one_head_a_device(): lax.all_to_all(spread, 'seq', split_axis=0, concat_axis=0, tiled=True)]
    unnamed x18 -> x16, local copies, waits for them, and re-layouts: 2.58 us -> 3.28 us
  transfers between devices with their start and end apart: 9 -> 10, of which waited for: 8 -> 7; matrix products, arithmetic and copies ran while one was open for 2% -> 4% of each run, Pallas kernels for 10% -> 25%
where the time goes in v3:
time: 109 us; the launch traced here: 108 us
  Pallas kernels  29.9 us (27%)
  waiting for transfers between devices  24.3 us (22%)
  starting transfers between devices  19.5 us (18%)
  between operations  13.5 us (12%)
  blocking collectives  13.4 us (12%)
  local copies, waits for them, and re-layouts  5.89 us (5%)
  other arithmetic  1.45 us (1%)
    all_to_all x1, blocking collectives, one_head_a_device(): lax.all_to_all(heads, 'seq', split_axis=0, concat_axis=0, tiled=True)  13.4 us
    pallas_call x1, Pallas kernels, one_head_a_device(): pl.pallas_call(light_kernel, grid=(full // tile,), in_specs=[pl.BlockSpec...  8.82 us
    all_to_all x1, waiting for transfers between devices, one_head_a_device(): lax.all_to_all(outgoing, 'seq', split_axis=0, concat_axis=0, tiled=True)  8.15 us
    all_to_all x1, starting transfers between devices, one_head_a_device(): lax.all_to_all(spread, 'seq', split_axis=0, concat_axis=0, tiled=True)  7.18 us
    all_to_all x1, waiting for transfers between devices, one_head_a_device(): lax.all_to_all(spread, 'seq', split_axis=0, concat_axis=0, tiled=True)  6.64 us
    pallas_call x1, Pallas kernels, one_head_a_device(): pl.pallas_call(light_output_kernel, grid=(wide // own_width,), in_specs=[...  4.38 us
    pallas_call x1, Pallas kernels, one_head_a_device(): pl.pallas_call(project_kernel, grid=(head_cols // (group * HD),), in_spec...  4.15 us
    all_to_all x1, starting transfers between devices, one_head_a_device(): lax.all_to_all(parts, 'seq', split_axis=0, concat_axis=0, tiled=True)  3.52 us
  transfers between devices with their start and end apart: 10, of which 7 were waited for; matrix products, arithmetic and copies ran while one was open for 4% of the time, Pallas kernels for 25%

profile of v3, /device:TPU:0, one launch (start us, length us, event | category | flops | bytes accessed | tf_op | source)
XLA Modules:
  0.0 108.0 jit_solution(2391582366724361622)
XLA Ops:
  6.5 0.0 all-gather.2.cloned.1.call-start
  6.5 0.7 all-gather.2.cloned.1.call-update
  7.3 0.6 pad_add_fusion.where_ref
  7.8 2.0 %shard_map.82 = (bf16[32,1024]{1,0:T(8,128)(2,1)}, bf16[32,1024]{1,0:T(8,128)(2,1)}) custom-call(s32[2]{0:T(128)} %pad_add_fusion.where_ref, bf16[256,1024]{1,0:T(8,128)(2,1)} %tok_ref.1, s32[8,32]{1,0:T(8,128)} %query_ref.3, s32[8,32]{1,0:T(8,128)} %source_ref.1), custom_call_target="tpu_custom_call" | custom-call | flops 33554432 | bytes 524288 | tf_op jit(solution)/shard_map/pallas_call | solution.py:294
  9.9 0.5 collective-permute-start
  10.3 1.1 %collective-permute-done.got_ref = bf16[32,1024]{1,0:T(8,128)(2,1)S(1)} collective-permute-done((bf16[32,1024]{1,0:T(8,128)(2,1)}, bf16[32,1024]{1,0:T(8,128)(2,1)S(1)}, u32[]{:S(2)}, u32[]{:S(2)}) %collective-permute-start) | collective-permute-done | bytes 65568 | tf_op jit(solution)/shard_map/ppermute | solution.py:301
  11.4 0.0 copy-start.7
  11.4 0.6 copy-done.7
  12.1 1.6 %shard_map.83 = bf16[8,32,512]{2,1,0:T(8,128)(2,1)} custom-call(s32[2]{0:T(128)} %pad_add_fusion.where_ref, bf16[32,1024]{1,0:T(8,128)(2,1)} %get-tuple-element.11.keep_ref, bf16[32,1024]{1,0:T(8,128)(2,1)} %copy-done.7), custom_call_target="tpu_custom_call" | custom-call | bytes 524288 | tf_op jit(solution)/shard_map/pallas_call | solution.py:302
  13.7 7.2 %all-to-all-start = ((bf16[8,32,512]{2,1,0:T(8,128)(2,1)}), bf16[8,32,512]{2,1,0:T(8,128)(2,1)S(1)}, u32[]{:S(2)}, u32[]{:S(2)}) async-start(bf16[8,32,512]{2,1,0:T(8,128)(2,1)} %shard_map.83), calls=%async_computation | async-start | bytes 524288 | tf_op jit(solution)/shard_map/all_to_all | solution.py:309
  20.8 1.3 %reshape.18.query_ref = s32[1,256]{1,0:T(1,128)} reshape(s32[8,32]{1,0:T(8,128)} %query_ref.3) | data formatting | bytes 2048 | tf_op jit(solution)/shard_map/reshape | solution.py:286
  22.1 1.3 %reshape.19.source_ref = s32[1,256]{1,0:T(1,128)} reshape(s32[8,32]{1,0:T(8,128)} %source_ref.1) | data formatting | bytes 2048 | tf_op jit(solution)/shard_map/reshape | solution.py:287
  23.5 6.6 %all-to-all-done.slots_ref = bf16[8,32,512]{2,1,0:T(8,128)(2,1)S(1)} async-done(((bf16[8,32,512]{2,1,0:T(8,128)(2,1)}), bf16[8,32,512]{2,1,0:T(8,128)(2,1)S(1)}, u32[]{:S(2)}, u32[]{:S(2)}) %all-to-all-start) | async-done | bytes 262176 | tf_op jit(solution)/shard_map/all_to_all | solution.py:309
  30.1 0.0 copy-start.2
  30.1 0.7 copy-done.2
  30.8 1.9 %shard_map.84 = bf16[64,512]{1,0:T(8,128)(2,1)} custom-call(s32[2]{0:T(128)} %pad_add_fusion.where_ref, bf16[8,32,512]{2,1,0:T(8,128)(2,1)} %copy-done.2, s32[1,256]{1,0:T(1,128)} %reshape.18.query_ref, s32[1,256]{1,0:T(1,128)} %reshape.19.source_ref), custom_call_target="tpu_custom_call" | custom-call | bytes 524288 | tf_op jit(solution)/shard_map/pallas_call | solution.py:310
  32.7 3.4 %collective-permute-start.1 = (bf16[64,512]{1,0:T(8,128)(2,1)}, bf16[64,512]{1,0:T(8,128)(2,1)S(1)}, u32[]{:S(2)}, u32[]{:S(2)}) collective-permute-start(bf16[64,512]{1,0:T(8,128)(2,1)} %shard_map.84), channel_id=1, source_target_pairs={{0,2},{1,3},{4,6},{5,7},{8,10},{9,11},{12,14},{13,15},{18,16},{19,... | collective-permute-start | bytes 196616 | tf_op jit(solution)/shard_map/ppermute | solution.py:323
  36.1 2.2 %collective-permute-done.1 = bf16[64,512]{1,0:T(8,128)(2,1)S(1)} collective-permute-done((bf16[64,512]{1,0:T(8,128)(2,1)}, bf16[64,512]{1,0:T(8,128)(2,1)S(1)}, u32[]{:S(2)}, u32[]{:S(2)}) %collective-permute-start.1) | collective-permute-done | bytes 65568 | tf_op jit(solution)/shard_map/ppermute | solution.py:323
  38.3 0.8 broadcast_select_fusion.mine_ref
  39.1 0.0 copy-start.4
  39.1 0.1 collective-permute-start.2
  39.2 1.2 %collective-permute-done.2.other_ref = bf16[64,512]{1,0:T(8,128)(2,1)S(1)} collective-permute-done((bf16[64,512]{1,0:T(8,128)(2,1)S(1)}, bf16[64,512]{1,0:T(8,128)(2,1)S(1)}, u32[]{:S(2)}, u32[]{:S(2)}) %collective-permute-start.2) | collective-permute-done | bytes 65568 | tf_op jit(solution)/shard_map/ppermute | solution.py:325
  40.5 0.0 copy-done.4
  40.5 0.0 copy-start.5
  40.5 0.6 copy-done.5
  41.1 4.1 %shard_map.85 = bf16[8,3,64,128]{3,2,1,0:T(8,128)(2,1)} custom-call(s32[2]{0:T(128)} %pad_add_fusion.where_ref, bf16[64,512]{1,0:T(8,128)(2,1)} %copy-done.4, bf16[64,512]{1,0:T(8,128)(2,1)} %copy-done.5, bf16[3,512,1024]{2,1,0:T(8,128)(2,1)} %weight_ref.4), custom_call_target="tpu_custom_call" | custom-call | flops 201326592 | bytes 3145728 | tf_op jit(solution)/shard_map/pallas_call | solution.py:327
  45.2 0.0 all-gather.2.cloned.1.call-done.tok_ref
  45.2 3.5 %all-to-all-start.1 = ((bf16[8,3,64,128]{3,2,1,0:T(8,128)(2,1)}), bf16[8,3,64,128]{3,2,1,0:T(8,128)(2,1)S(1)}, u32[]{:S(2)}, u32[]{:S(2)}) async-start(bf16[8,3,64,128]{3,2,1,0:T(8,128)(2,1)} %shard_map.85), calls=%async_computation.1 | async-start | bytes 786432 | tf_op jit(solution)/shard_map/all_to_all | solution.py:369
  48.8 0.0 reduce-scatter.2.cloned.1.call-start
  48.8 8.8 %shard_map.86.heads_ref = bf16[256,256]{1,0:T(8,128)(2,1)} custom-call(bf16[256,4096]{1,0:T(8,128)(2,1)} %all-gather.2.cloned.1.call-done.tok_ref, bf16[3,4096,256]{2,1,0:T(8,128)(2,1)} %weight_ref.5), custom_call_target="tpu_custom_call" | custom-call | flops 1610612736 | bytes 8388608 | tf_op jit(solution)/shard_map/pallas_call | solution.py:344
  57.6 4.4 %shard_map.87 = bf16[256,4096]{1,0:T(8,128)(2,1)} custom-call(bf16[256,256]{1,0:T(8,128)(2,1)} %shard_map.86.heads_ref, bf16[256,4096]{1,0:T(8,128)(2,1)} %weight_ref.6), custom_call_target="tpu_custom_call" | custom-call | flops 536870912 | bytes 4194304 | tf_op jit(solution)/shard_map/pallas_call | solution.py:357
  62.0 0.0 all-to-all-done.1.parts_ref
  62.0 0.0 copy-start.1
  62.0 0.0 reduce-scatter.2.cloned.1.call-update
  62.0 0.7 copy-done.1
  62.8 2.0 %shard_map.88 = bf16[8,64,128]{2,1,0:T(8,128)(2,1)} custom-call(bf16[8,3,64,128]{3,2,1,0:T(8,128)(2,1)} %copy-done.1), custom_call_target="tpu_custom_call" | custom-call | bytes 524288 | tf_op jit(solution)/shard_map/pallas_call | solution.py:372
  64.8 13.4 %all_to_all.20.heads_ref = bf16[8,64,128]{2,1,0:T(8,128)(2,1)} all-to-all(bf16[8,64,128]{2,1,0:T(8,128)(2,1)} %shard_map.88), channel_id=1, replica_groups=mesh['seq'=8,'head'=4] {'seq'}, dimensions={0} | all-to-all | bytes 262144 | tf_op jit(solution)/shard_map/all_to_all | solution.py:379
  78.1 2.5 %shard_map.89 = bf16[8,32,512]{2,1,0:T(8,128)(2,1)} custom-call(bf16[8,64,128]{2,1,0:T(8,128)(2,1)} %all_to_all.20.heads_ref, bf16[1024,512]{1,0:T(8,128)(2,1)} %weight_ref.7, s32[1,256]{1,0:T(1,128)} %reshape.18.query_ref), custom_call_target="tpu_custom_call" | custom-call | flops 67108864 | bytes 1048576 | tf_op jit(solution)/shard_map/pallas_call | solution.py:380
  80.7 3.4 %all-to-all-start.3 = ((bf16[8,32,512]{2,1,0:T(8,128)(2,1)}), bf16[8,32,512]{2,1,0:T(8,128)(2,1)S(1)}, u32[]{:S(2)}, u32[]{:S(2)}) async-start(bf16[8,32,512]{2,1,0:T(8,128)(2,1)} %shard_map.89), calls=%async_computation.4 | async-start | bytes 524288 | tf_op jit(solution)/shard_map/all_to_all | solution.py:387
  84.1 8.1 %all-to-all-done.3.mine_ref = bf16[8,32,512]{2,1,0:T(8,128)(2,1)S(1)} async-done(((bf16[8,32,512]{2,1,0:T(8,128)(2,1)}), bf16[8,32,512]{2,1,0:T(8,128)(2,1)S(1)}, u32[]{:S(2)}, u32[]{:S(2)}) %all-to-all-start.3) | async-done | bytes 262176 | tf_op jit(solution)/shard_map/all_to_all | solution.py:387
  92.3 0.1 collective-permute-start.3
  92.4 1.3 %collective-permute-done.3 = bf16[2,2,32,512]{3,2,1,0:T(8,128)(2,1)S(1)} collective-permute-done((bf16[2,2,32,512]{3,2,1,0:T(8,128)(2,1)S(1)}, bf16[2,2,32,512]{3,2,1,0:T(8,128)(2,1)S(1)}, u32[]{:S(2)}, u32[]{:S(2)}) %collective-permute-start.3) | collective-permute-done | bytes 131104 | tf_op jit(solution)/shard_map/ppermute | solution.py:392
  93.7 1.4 %collective-permute-start.4 = (bf16[2,32,512]{2,1,0:T(8,128)(2,1)S(1)}, bf16[2,32,512]{2,1,0:T(8,128)(2,1)S(1)}, u32[]{:S(2)}, u32[]{:S(2)}) collective-permute-start(bf16[2,32,512]{2,1,0:T(8,128)(2,1)S(1)} %fusion), channel_id=1, source_target_pairs={{0,2},{1,3},{2,0},{3,1},{4,6},{5,7},{6,4},{7,5},{8,10},{9,11},{10,... | collective-permute-start | bytes 196616 | tf_op jit(solution)/shard_map/ppermute | solution.py:400
  95.1 3.0 %collective-permute-done.4.last_ref = bf16[2,32,512]{2,1,0:T(8,128)(2,1)S(1)} collective-permute-done((bf16[2,32,512]{2,1,0:T(8,128)(2,1)S(1)}, bf16[2,32,512]{2,1,0:T(8,128)(2,1)S(1)}, u32[]{:S(2)}, u32[]{:S(2)}) %collective-permute-start.4) | collective-permute-done | bytes 65568 | tf_op jit(solution)/shard_map/ppermute | solution.py:400
  98.0 0.0 copy-done
  98.0 0.0 copy-done.3
  98.0 0.6 copy-done.6
  98.7 2.5 %shard_map.90 = bf16[256,1024]{1,0:T(8,128)(2,1)} custom-call(s32[2]{0:T(128)} %pad_add_fusion.where_ref, bf16[256,1024]{1,0:T(8,128)(2,1)} %reduce-scatter.2.cloned.1.call-done.light_ref, bf16[8,32,512]{2,1,0:T(8,128)(2,1)} %copy-done, bf16[4,32,512]{2,1,0:T(8,128)(2,1)} %bitcast.14, bf16[2,32,512]{2,1,0:T(8,128)(2,1)} %copy-done.6, s32[8,32]{1,0:T(8,128)} %query_ref.3, ...), custom_call_target="tpu_custom_call" | custom-call | bytes 1048576 | tf_op jit(solution)/shard_map/pallas_call | solution.py:401
  (6 shorter events, 0.0 us)
Async XLA Ops:
  6.5 38.7 %all-gather.2.cloned.1.call-start = ((), (), s32[]{:S(2)}) async-start(), calls=%async_computation.5 | async-start | bytes 2621440 | tf_op jit(solution)/shard_map/all_gather | solution.py:292
  9.9 1.6 %collective-permute-start = (bf16[32,1024]{1,0:T(8,128)(2,1)}, bf16[32,1024]{1,0:T(8,128)(2,1)S(1)}, u32[]{:S(2)}, u32[]{:S(2)}) collective-permute-start(bf16[32,1024]{1,0:T(8,128)(2,1)} %get-tuple-element.12), channel_id=1, source_target_pairs={{0,1},{1,0},{2,3},{3,2},{4,5},{5,4},{6,7},{7,6},{8,9},{9,8},{10,11... | collective-permute-start | bytes 196616 | tf_op jit(solution)/shard_map/ppermute | solution.py:301
  11.4 0.6 copy-start.7
  13.7 16.4 %all-to-all-start = ((bf16[8,32,512]{2,1,0:T(8,128)(2,1)}), bf16[8,32,512]{2,1,0:T(8,128)(2,1)S(1)}, u32[]{:S(2)}, u32[]{:S(2)}) async-start(bf16[8,32,512]{2,1,0:T(8,128)(2,1)} %shard_map.83), calls=%async_computation | async-start | bytes 524288 | tf_op jit(solution)/shard_map/all_to_all | solution.py:309
  30.1 0.7 copy-start.2
  32.7 5.6 %collective-permute-start.1 = (bf16[64,512]{1,0:T(8,128)(2,1)}, bf16[64,512]{1,0:T(8,128)(2,1)S(1)}, u32[]{:S(2)}, u32[]{:S(2)}) collective-permute-start(bf16[64,512]{1,0:T(8,128)(2,1)} %shard_map.84), channel_id=1, source_target_pairs={{0,2},{1,3},{4,6},{5,7},{8,10},{9,11},{12,14},{13,15},{18,16},{19,... | collective-permute-start | bytes 196616 | tf_op jit(solution)/shard_map/ppermute | solution.py:323
  39.1 1.3 %copy-start.4 = (bf16[64,512]{1,0:T(8,128)(2,1)}, bf16[64,512]{1,0:T(8,128)(2,1)S(1)}, u32[]{:S(2)}) copy-start(bf16[64,512]{1,0:T(8,128)(2,1)S(1)} %broadcast_select_fusion.mine_ref) | copy-start | bytes 196612
  39.1 1.3 %collective-permute-start.2 = (bf16[64,512]{1,0:T(8,128)(2,1)S(1)}, bf16[64,512]{1,0:T(8,128)(2,1)S(1)}, u32[]{:S(2)}, u32[]{:S(2)}) collective-permute-start(bf16[64,512]{1,0:T(8,128)(2,1)S(1)} %broadcast_select_fusion.mine_ref), channel_id=1, source_target_pairs={{0,1},{1,0},{2,3},{3,2},{4,5},{5,4},{6,7},{7,6},{8,9},{9,8},{10,11... | collective-permute-start | bytes 196616 | tf_op jit(solution)/shard_map/ppermute | solution.py:325
  40.5 0.6 copy-start.5
  45.2 16.8 %all-to-all-start.1 = ((bf16[8,3,64,128]{3,2,1,0:T(8,128)(2,1)}), bf16[8,3,64,128]{3,2,1,0:T(8,128)(2,1)S(1)}, u32[]{:S(2)}, u32[]{:S(2)}) async-start(bf16[8,3,64,128]{3,2,1,0:T(8,128)(2,1)} %shard_map.85), calls=%async_computation.1 | async-start | bytes 786432 | tf_op jit(solution)/shard_map/all_to_all | solution.py:369
  48.8 49.3 %reduce-scatter.2.cloned.1.call-start = ((), (), s32[]{:S(2)}) async-start(), calls=%async_computation.6 | async-start | bytes 2621440 | tf_op jit(solution)/shard_map/reduce_scatter | solution.py:371
  62.0 0.7 copy-start.1
  80.7 11.6 %all-to-all-start.3 = ((bf16[8,32,512]{2,1,0:T(8,128)(2,1)}), bf16[8,32,512]{2,1,0:T(8,128)(2,1)S(1)}, u32[]{:S(2)}, u32[]{:S(2)}) async-start(bf16[8,32,512]{2,1,0:T(8,128)(2,1)} %shard_map.89), calls=%async_computation.4 | async-start | bytes 524288 | tf_op jit(solution)/shard_map/all_to_all | solution.py:387
  92.3 5.8 %copy-start = (bf16[8,32,512]{2,1,0:T(8,128)(2,1)}, bf16[8,32,512]{2,1,0:T(8,128)(2,1)S(1)}, u32[]{:S(2)}) copy-start(bf16[8,32,512]{2,1,0:T(8,128)(2,1)S(1)} %all-to-all-done.3.mine_ref) | copy-start | bytes 786436
  92.3 1.4 %collective-permute-start.3 = (bf16[2,2,32,512]{3,2,1,0:T(8,128)(2,1)S(1)}, bf16[2,2,32,512]{3,2,1,0:T(8,128)(2,1)S(1)}, u32[]{:S(2)}, u32[]{:S(2)}) collective-permute-start(bf16[2,2,32,512]{3,2,1,0:T(8,128)(2,1)S(1)} %dynamic-slice_bitcast_fusion), channel_id=1, source_target_pairs={{0,1},{1,0},{2,3},{3,2},{4,5},{5,4},{6,7},{7,6},{8,9},{9,8},{10,11... | collective-permute-start | bytes 393224 | tf_op jit(solution)/shard_map/ppermute | solution.py:392
  93.7 4.4 %copy-start.3 = (bf16[2,2,32,512]{3,2,1,0:T(8,128)(2,1)}, bf16[2,2,32,512]{3,2,1,0:T(8,128)(2,1)S(1)}, u32[]{:S(2)}) copy-start(bf16[2,2,32,512]{3,2,1,0:T(8,128)(2,1)S(1)} %collective-permute-done.3) | copy-start | bytes 393220
  93.7 4.3 %collective-permute-start.4 = (bf16[2,32,512]{2,1,0:T(8,128)(2,1)S(1)}, bf16[2,32,512]{2,1,0:T(8,128)(2,1)S(1)}, u32[]{:S(2)}, u32[]{:S(2)}) collective-permute-start(bf16[2,32,512]{2,1,0:T(8,128)(2,1)S(1)} %fusion), channel_id=1, source_target_pairs={{0,2},{1,3},{2,0},{3,1},{4,6},{5,7},{6,4},{7,5},{8,10},{9,11},{10,... | collective-permute-start | bytes 196616 | tf_op jit(solution)/shard_map/ppermute | solution.py:400
  98.0 0.6 copy-start.6
Sparse Core Ops, SparseCore 0:
  8.9 25.2 all-gather.1
  62.2 32.5 reduce-scatter.1

commit v4 on v1

--- a/solution.py
+++ b/solution.py
@@ -3,11 +3,18 @@
 import jax
 import jax.numpy as jnp
 from jax import lax
+from jax.experimental import pallas as pl
+from jax.experimental.pallas import tpu as pltpu
 from jax.sharding import PartitionSpec as P
 
 HD = 128
 LB = 128
 ROUTE = 32
+BF = jnp.bfloat16
+F32 = jnp.float32
+VMEM = pl.BlockSpec(memory_space=pltpu.VMEM)
+FIRST = (((0,), (0,)), ((), ()))
+LAST = (((1,), (1,)), ((), ()))
 
 
 def attend(queries, key_rows, value_rows):
@@ -50,7 +57,7 @@
     return jnp.where((own_list >= 0)[:, None], chosen, jnp.zeros_like(chosen))
 
 
-def per_device(
+def general(
     tokens,
     light_input,
     light_output,
@@ -106,6 +113,367 @@
     return lax.psum_scatter(combined.astype(jnp.bfloat16), "head", scatter_dimension=1, tiled=True)
 
 
+def in_vmem(*arrays):
+    return tuple(pltpu.with_memory_space_constraint(a, pltpu.VMEM) for a in arrays)
+
+
+def on_chip(kernel, outs, *arrays, hbm=(), scratch=(), flops=0, moved=0, off=False):
+    made = [(jax.ShapeDtypeStruct if off else pltpu.VMEM)(*o) for o in outs]
+    result = pl.pallas_call(
+        kernel,
+        in_specs=[pl.BlockSpec(memory_space=pl.ANY)] * len(hbm) + [VMEM] * len(arrays),
+        scratch_shapes=list(scratch),
+        out_specs=[VMEM] * len(made),
+        out_shape=made,
+        compiler_params=pltpu.CompilerParams(vmem_limit_bytes=(60 if hbm else 8) << 20),
+        cost_estimate=pl.CostEstimate(
+            flops=int(flops), bytes_accessed=int(moved), transcendentals=0
+        ),
+    )(*hbm, *in_vmem(*arrays))
+    return result if len(outs) > 1 else result[0]
+
+
+def own_row(table, index):
+    rows = lax.broadcasted_iota(jnp.int32, table.shape, 0)
+    return jnp.sum(jnp.where(rows == index, table, 0), axis=0, keepdims=True)
+
+
+def onehot(flags):
+    return flags.astype(F32).astype(BF)
+
+
+def compact_onehot(table, out_ref):
+    shards, slots = table.shape
+    live = (table >= 0).astype(jnp.int32)
+    counts = jnp.sum(live, axis=1, keepdims=True)
+    row = lax.broadcasted_iota(jnp.int32, (out_ref.shape[0], slots), 0)
+    place = lax.broadcasted_iota(jnp.int32, (1, slots), 1)
+    for s in range(shards):
+        here = (row == place) & (table[s : s + 1] >= 0)
+        out_ref[:, s * slots : (s + 1) * slots] = onehot(here)
+        place = place + counts[s : s + 1]
+
+
+def pick_kernel(
+    tok_hbm, query_hbm, source_hbm, keep_ref, send_ref, tok_ref, query_ref, source_ref, sems
+):
+    copies = [
+        pltpu.make_async_copy(*ends, sems.at[i])
+        for i, ends in enumerate(
+            ((query_hbm, query_ref), (source_hbm, source_ref), (tok_hbm, tok_ref))
+        )
+    ]
+    for copy in copies:
+        copy.start()
+    seq_index, odd = lax.axis_index("seq"), lax.axis_index("head") % 2
+    copies[0].wait()
+    copies[1].wait()
+    own_q = own_row(query_ref[...], seq_index)
+    own_s = own_row(source_ref[...], seq_index)
+    spot = lax.broadcasted_iota(jnp.int32, (tok_ref.shape[0], own_q.shape[1]), 0)
+    chosen = [onehot(spot == jnp.where(odd == k, own_q, own_s)) for k in range(2)]
+    copies[2].wait()
+    for ref, rows in zip((keep_ref, send_ref), chosen):
+        ref[...] = lax.dot_general(rows, tok_ref[...], FIRST, preferred_element_type=F32).astype(
+            BF
+        )
+
+
+def prepare_kernel(
+    query_ref, source_ref, gate_ref, mine_ref, query_map_ref, own_map_ref, gate_map_ref
+):
+    odd = lax.axis_index("head") % 2
+    query, source = query_ref[...], source_ref[...]
+    compact_onehot(query, query_map_ref)
+    compact_onehot(jnp.where(odd == 0, query, source), mine_ref)
+    own_q = own_row(query, lax.axis_index("seq"))
+    spot = lax.broadcasted_iota(jnp.int32, own_map_ref.shape, 0)
+    own_map_ref[...] = onehot(spot == own_q)
+    slots = own_q.shape[1]
+    diagonal = lax.broadcasted_iota(jnp.int32, (slots, slots), 0) == lax.broadcasted_iota(
+        jnp.int32, (slots, slots), 1
+    )
+    gate = jnp.sum(jnp.where(diagonal, gate_ref[...], 0.0), axis=1, keepdims=True)
+    gate_map_ref[...] = jnp.broadcast_to(gate, gate_map_ref.shape)
+
+
+def spread_kernel(*refs):
+    *pieces, out_ref = refs
+    head = lax.axis_index("head")
+    width = out_ref.shape[2]
+    per = out_ref.shape[0] // len(pieces)
+    for j, piece in enumerate(pieces):
+        owner = head ^ j
+        for i in range(per):
+            out_ref[owner * per + i] = piece[:, i * width : (i + 1) * width]
+
+
+def compact_kernel(slots_ref, chosen_ref, out_ref):
+    rows = slots_ref[...].reshape(-1, slots_ref.shape[2])
+    out_ref[...] = jnp.dot(chosen_ref[...], rows, preferred_element_type=F32).astype(BF)
+
+
+def project_kernel(mine_ref, other_ref, weight_ref, out_ref):
+    odd = lax.axis_index("head") % 2
+    mine, other = mine_ref[...], other_ref[...]
+    query = jnp.where(odd == 0, mine, other)
+    source = jnp.where(odd == 0, other, mine)
+    for c, rows in enumerate((query, source, source)):
+        part = jnp.dot(rows, weight_ref[c], preferred_element_type=F32).astype(BF)
+        for g in range(out_ref.shape[0]):
+            out_ref[g, c] = part[:, g * HD : (g + 1) * HD]
+
+
+def one_head(query, key, value):
+    scores = lax.dot_general(query, key, LAST, preferred_element_type=F32) / math.sqrt(HD)
+    expanded = jnp.exp(scores - jnp.max(scores, axis=-1, keepdims=True))
+    totals = jnp.sum(expanded, axis=-1, keepdims=True)
+    weighted = jnp.dot(expanded.astype(BF), value, preferred_element_type=F32)
+    return (weighted / totals).astype(BF)
+
+
+def heavy_attend_kernel(parts_ref, out_ref):
+    total = parts_ref[0].astype(F32)
+    for s in range(1, parts_ref.shape[0]):
+        total = total + parts_ref[s].astype(F32)
+    total = total.astype(BF)
+    result = one_head(total[0], total[1], total[2])
+    for s in range(out_ref.shape[0]):
+        out_ref[s] = result
+
+
+def heavy_output_kernel(heads_ref, weight_ref, chosen_ref, out_ref):
+    rows = jnp.concatenate([heads_ref[g] for g in range(heads_ref.shape[0])], axis=1)
+    part = jnp.dot(rows, weight_ref[...], preferred_element_type=F32).astype(BF)
+    spread = lax.dot_general(chosen_ref[...], part, FIRST, preferred_element_type=F32).astype(BF)
+    out_ref[...] = spread.reshape(out_ref.shape)
+
+
+def give_kernel(back_ref, out_ref):
+    head = lax.axis_index("head")
+    per = out_ref.shape[1]
+    for i, j in enumerate((1, 3)):
+        out_ref[i] = back_ref[pl.ds((head ^ j) * per, per)]
+
+
+def far_kernel(back_ref, got_ref, out_ref):
+    per = out_ref.shape[0]
+    far = lax.axis_index("head") ^ 2
+    out_ref[...] = (
+        back_ref[pl.ds(far * per, per)].astype(F32) + got_ref[1].astype(F32)
+    ).astype(BF)
+
+
+def finish_kernel(
+    light_ref, light_far_ref, back_ref, got_ref, last_ref, own_map_ref, gate_ref, out_ref
+):
+    head = lax.axis_index("head")
+    per = last_ref.shape[0]
+    heavy = (
+        back_ref[pl.ds(head * per, per)].astype(F32)
+        + got_ref[0].astype(F32)
+        + last_ref[...].astype(F32)
+    )
+    chosen, gate = own_map_ref[...], gate_ref[:, :1]
+    width = heavy.shape[2]
+    for j in range(per):
+        scaled = heavy[j] * gate
+        coarse = scaled.astype(BF)
+        fine = (scaled - coarse.astype(F32)).astype(BF)
+        added = jnp.dot(chosen, coarse, preferred_element_type=F32) + jnp.dot(
+            chosen, fine, preferred_element_type=F32
+        )
+        cols = slice(j * width, (j + 1) * width)
+        light = light_ref[:, cols] + light_far_ref[:, cols].astype(F32)
+        out_ref[:, cols] = (light + added).astype(BF)
+
+
+def light_kernel(*refs):
+    count = len(refs) - 9
+    pieces, (w_in, w_out, heads_ref, give_ref, *held) = refs[:count], refs[count:]
+    tok_ref, in_ref, out_ref, sems, gave_sems = held
+    head = lax.axis_index("head")
+    depth = pieces[0].shape[1]
+    width = give_ref.shape[2]
+
+    def rows(j):
+        return pl.ds(pl.multiple_of((head ^ j) * depth, depth), depth)
+
+    def cols(j):
+        return pl.ds(pl.multiple_of((head ^ j) * width, width), width)
+
+    copies = []
+    for j, piece in enumerate(pieces):
+        copies.append(pltpu.make_async_copy(piece, tok_ref.at[j], sems.at[0, j]))
+        for c in range(3):
+            copies.append(
+                pltpu.make_async_copy(
+                    w_in.at[c, rows(j), :], in_ref.at[c, j], sems.at[1 + c, j]
+                )
+            )
+    late = [
+        pltpu.make_async_copy(w_out.at[:, cols(j)], out_ref.at[i], gave_sems.at[i])
+        for i, j in enumerate((1, 3))
+    ]
+    for copy in copies + late:
+        copy.start()
+    total = [None] * 3
+    for j in range(count):
+        copies[4 * j].wait()
+        for c in range(3):
+            copies[4 * j + 1 + c].wait()
+            part = jnp.dot(tok_ref[j], in_ref[c, j], preferred_element_type=F32)
+            total[c] = part if j == 0 else total[c] + part
+    mapped = [t.astype(BF) for t in total]
+    for b in range(heads_ref.shape[0] // LB):
+        for g in range(heads_ref.shape[1] // HD):
+            at = (slice(b * LB, (b + 1) * LB), slice(g * HD, (g + 1) * HD))
+            heads_ref[at] = one_head(*(m[at] for m in mapped))
+    for i in range(2):
+        late[i].wait()
+        give_ref[i] = jnp.dot(
+            heads_ref[...], out_ref[i], preferred_element_type=F32
+        ).astype(BF)
+
+
+def light_own_kernel(w_out, got, heads_ref, own_ref, far_ref, out_ref, got_ref, sems):
+    head = lax.axis_index("head")
+    width = own_ref.shape[1]
+    copies = []
+    for i, j in enumerate((0, 2)):
+        cols = pl.ds(pl.multiple_of((head ^ j) * width, width), width)
+        copies.append(pltpu.make_async_copy(w_out.at[:, cols], out_ref.at[i], sems.at[0, i]))
+        copies.append(pltpu.make_async_copy(got.at[i], got_ref.at[i], sems.at[1, i]))
+    for copy in copies:
+        copy.start()
+    for i, ref in enumerate((own_ref, far_ref)):
+        copies[2 * i].wait()
+        copies[2 * i + 1].wait()
+        block = jnp.dot(heads_ref[...], out_ref[i], preferred_element_type=F32)
+        ref[...] = (block + got_ref[i].astype(F32)).astype(ref.dtype)
+
+
+def one_head_a_device(
+    tokens,
+    light_input,
+    light_output,
+    heavy_input,
+    heavy_output,
+    query_tokens,
+    context_tokens,
+    query_gate,
+):
+    seq_count, head_count = lax.axis_size("seq"), lax.axis_size("head")
+    tok_rows, own_width = tokens.shape
+    slots = query_tokens.shape[1]
+    routed = seq_count * tok_rows // ROUTE
+    part_width, head_cols = heavy_input.shape[1:]
+    out_cols = heavy_output.shape[1]
+    light_cols = light_input.shape[2]
+    per = seq_count // head_count
+    pair, across, diagonal = (
+        [(i, i ^ j) for i in range(head_count)] for j in (1, 2, 3)
+    )
+
+    def swap(x):
+        return lax.all_to_all(x, "seq", split_axis=0, concat_axis=0, tiled=True)
+
+    keep, send, tokens = on_chip(
+        pick_kernel,
+        [((slots, own_width), BF)] * 2 + [(tokens.shape, BF)],
+        hbm=(tokens, query_tokens, context_tokens),
+        scratch=[pltpu.VMEM(query_tokens.shape, jnp.int32)] * 2 + [pltpu.SemaphoreType.DMA((3,))],
+    )
+    pieces = (
+        keep,
+        lax.ppermute(send, "head", pair),
+        lax.ppermute(keep, "head", across),
+        lax.ppermute(send, "head", diagonal),
+    )
+    spread = on_chip(spread_kernel, [((seq_count, slots, part_width), BF)], *pieces)
+    tables = (query_tokens, context_tokens, query_gate)
+    spread, tables, tokens = lax.optimization_barrier((spread, tables, tokens))
+    mine_map, query_map, own_map, gate_map = on_chip(
+        prepare_kernel,
+        [((routed, seq_count * slots), BF)] * 2 + [((tok_rows, slots), BF), ((slots, HD), F32)],
+        *tables,
+    )
+    token_far = lax.ppermute(tokens, "head", across)
+    token_pair = lax.ppermute(tokens, "head", pair)
+    token_last = lax.ppermute(token_far, "head", pair)
+    spread = swap(spread)
+    spread, mine_map = lax.optimization_barrier((spread, mine_map))
+    mine = on_chip(compact_kernel, [((routed, part_width), BF)], spread, mine_map)
+    other = lax.ppermute(mine, "head", pair)
+    parts = on_chip(
+        project_kernel, [((seq_count, 3, routed, HD), BF)], mine, other, heavy_input
+    )
+
+    parts, token_pieces = lax.optimization_barrier(
+        (parts, (tokens, token_pair, token_far, token_last))
+    )
+    light_heads, light_give = on_chip(
+        light_kernel,
+        [((tok_rows, light_cols), BF), ((2, tok_rows, own_width), BF)],
+        hbm=(*token_pieces, light_input, light_output),
+        scratch=[
+            pltpu.VMEM((head_count, tok_rows, own_width), BF),
+            pltpu.VMEM((3, head_count, own_width, light_cols), BF),
+            pltpu.VMEM((2, light_cols, own_width), BF),
+            pltpu.SemaphoreType.DMA((4, head_count)),
+            pltpu.SemaphoreType.DMA((2,)),
+        ],
+        flops=6 * tok_rows * light_cols * own_width * head_count,
+        off=True,
+    )
+    parts = swap(parts)
+    parts, light_heads, light_give = lax.optimization_barrier((parts, light_heads, light_give))
+    heads = on_chip(heavy_attend_kernel, [((seq_count, routed, HD), BF)], parts)
+    light_got = lax.ppermute(light_give, "head", pair)
+    light_own, light_far = on_chip(
+        light_own_kernel,
+        [((tok_rows, own_width), F32), ((tok_rows, own_width), BF)],
+        light_heads,
+        hbm=(light_output, light_got),
+        scratch=[
+            pltpu.VMEM((2, light_cols, own_width), BF),
+            pltpu.VMEM((2, tok_rows, own_width), BF),
+            pltpu.SemaphoreType.DMA((2, 2)),
+        ],
+        flops=4 * tok_rows * light_cols * own_width,
+        off=True,
+    )
+    heads = swap(heads)
+    heads, light_own, light_far = lax.optimization_barrier((heads, light_own, light_far))
+    light_far = lax.ppermute(light_far, "head", across)
+
+    back = swap(
+        on_chip(
+            heavy_output_kernel,
+            [((seq_count, slots, out_cols), BF)],
+            heads,
+            heavy_output,
+            query_map,
+        )
+    )
+    give = on_chip(give_kernel, [((2, per, slots, out_cols), BF)], back)
+    got = lax.ppermute(give, "head", pair)
+    far = on_chip(far_kernel, [((per, slots, out_cols), BF)], back, got)
+    last = lax.ppermute(far, "head", across)
+    return on_chip(
+        finish_kernel,
+        [((tok_rows, own_width), BF)],
+        light_own,
+        light_far,
+        back,
+        got,
+        last,
+        own_map,
+        gate_map,
+        off=True,
+    )
+
+
 def solution(mesh):
     placed = (
         P("seq", "head"),
@@ -117,6 +485,13 @@
         P(),
         P("seq", None),
     )
+
+    def per_device(*args):
+        seq_count, head_count = mesh.shape["seq"], mesh.shape["head"]
+        local_heads = args[3].shape[2] // HD
+        fits = head_count // 2 == 2 and seq_count % head_count == 0 and local_heads == seq_count
+        return (one_head_a_device if fits else general)(*args)
+
     return jax.shard_map(
         per_device, mesh=mesh, in_specs=placed, out_specs=P("seq", "head"), check_vma=False
     )

time: 188 us -> 82 us (0.44)
  blocking collectives: 45.5 us -> 0 us
  waiting for transfers between devices: 55.4 us -> 30.3 us
  other arithmetic: 22.4 us -> 0 us
  Pallas kernels: 0 us -> 18.6 us
  matrix products: 15.5 us -> 0 us
  between operations: 13.6 us -> 0.17 us
  local copies, waits for them, and re-layouts: 18.6 us -> 5.81 us
  starting transfers between devices: 15.5 us -> 26.4 us
    psum x1 -> x0, blocking collectives: 45.5 us -> none  [per_device(): lax.psum(project(query_rows, source_rows, heavy_input), 'seq')]
    reduce_scatter x1 -> x0, waiting for transfers between devices: 31 us -> none  [per_device(): lax.psum_scatter(combined.astype(jnp.bfloat16), 'head', scatter_dimension...]
    all_gather x1 -> x0, waiting for transfers between devices: 19.3 us -> none  [per_device(): gathered = lax.all_gather(tokens, 'head', axis=1, tiled=True)]
    pallas_call x0 -> x12, Pallas kernels: none -> 18.6 us  [on_chip(): pl.pallas_call(kernel, in_specs=[pl.BlockSpec(memory_space=pl.ANY)] * len...]
    ppermute x0 -> x11, waiting for transfers between devices: none -> 16.4 us  [the longest x1 7.03 us: one_head_a_device(): token_far = lax.ppermute(tokens, 'head', across)]
    dot_general x8 -> x0, matrix products: 15.5 us -> none  [the longest x1 5.25 us: per_device(): jnp.einsum('td,cdw->ctw', gathered, light_input, preferred_element_type=j...]
    gather x5 -> x0, local copies, waits for them, and re-layouts: 9.99 us -> none  [the longest x2 6.33 us: pick_rows(): chosen = jnp.take(gathered, jnp.maximum(own_list, 0), axis=0)]
    all_to_all x3 -> x4, waiting for transfers between devices: 4.34 us -> 13.9 us  [swap(): return lax.all_to_all(x, 'seq', split_axis=0, concat_axis=0, tiled=True)]
  transfers between devices with their start and end apart: 5 -> 15, of which waited for: 4 -> 10; matrix products, arithmetic and copies ran while one was open for 19% -> 0% of each run, Pallas kernels for 0% -> 17%
where the time goes in v4:
time: 82 us; the launch traced here: 81.3 us
  waiting for transfers between devices  30.3 us (37%)
  starting transfers between devices  26.4 us (32%)
  Pallas kernels  18.6 us (23%)
  local copies, waits for them, and re-layouts  5.81 us (7%)
    all_to_all x4, starting transfers between devices, swap(): return lax.all_to_all(x, 'seq', split_axis=0, concat_axis=0, tiled=True)  19.3 us
    pallas_call x12, Pallas kernels, on_chip(): pl.pallas_call(kernel, in_specs=[pl.BlockSpec(memory_space=pl.ANY)] * len...  18.6 us
    all_to_all x4, waiting for transfers between devices, swap(): return lax.all_to_all(x, 'seq', split_axis=0, concat_axis=0, tiled=True)  13.9 us
    ppermute x1, waiting for transfers between devices, one_head_a_device(): token_far = lax.ppermute(tokens, 'head', across)  7.03 us
    unnamed x24, local copies, waits for them, and re-layouts  5.81 us
    ppermute x1, starting transfers between devices, one_head_a_device(): lax.ppermute(keep, 'head', across)  3 us
    ppermute x1, waiting for transfers between devices, one_head_a_device(): light_far = lax.ppermute(light_far, 'head', across)  2.16 us
    ppermute x1, waiting for transfers between devices, one_head_a_device(): lax.ppermute(keep, 'head', across)  2.05 us
  transfers between devices with their start and end apart: 15, of which 10 were waited for; matrix products, arithmetic and copies ran while one was open for 0% of the time, Pallas kernels for 17%

profile of v4, /device:TPU:0, one launch (start us, length us, event | category | flops | bytes accessed | tf_op | source)
XLA Modules:
  0.0 81.3 jit_solution(4138350305254629840)
XLA Ops:
  0.0 1.4 %shard_map.82 = (bf16[32,1024]{1,0:T(8,128)(2,1)S(1)}, bf16[32,1024]{1,0:T(8,128)(2,1)S(1)}, bf16[256,1024]{1,0:T(8,128)(2,1)S(1)}) custom-call(bf16[256,1024]{1,0:T(8,128)(2,1)} %tok_hbm.1, s32[8,32]{1,0:T(8,128)} %query_ref, s32[8,32]{1,0:T(8,128)} %source_ref), custom_call_target="tpu_custom_call" | custom-call | tf_op jit(solution)/shard_map/pallas_call | solution.py:122
  1.4 0.0 copy-start.3
  1.4 3.0 %collective-permute-start.1 = (bf16[32,1024]{1,0:T(8,128)(2,1)S(1)}, bf16[32,1024]{1,0:T(8,128)(2,1)S(1)}, u32[]{:S(2)}, u32[]{:S(2)}) collective-permute-start(bf16[32,1024]{1,0:T(8,128)(2,1)S(1)} %get-tuple-element.34.refs_0_), channel_id=1, source_target_pairs={{0,2},{1,3},{2,0},{3,1},{4,6},{5,7},{6,4},{7,5},{8,10},{9,11},{10,... | collective-permute-start | bytes 196616 | tf_op jit(solution)/shard_map/ppermute | solution.py:390
  4.4 0.0 collective-permute-start.2
  4.4 0.2 collective-permute-start
  4.6 2.1 %collective-permute-done.1.refs_2_ = bf16[32,1024]{1,0:T(8,128)(2,1)S(1)} collective-permute-done((bf16[32,1024]{1,0:T(8,128)(2,1)S(1)}, bf16[32,1024]{1,0:T(8,128)(2,1)S(1)}, u32[]{:S(2)}, u32[]{:S(2)}) %collective-permute-start.1) | collective-permute-done | bytes 65568 | tf_op jit(solution)/shard_map/ppermute | solution.py:390
  6.7 1.9 %collective-permute-done.2.refs_3_ = bf16[32,1024]{1,0:T(8,128)(2,1)S(1)} collective-permute-done((bf16[32,1024]{1,0:T(8,128)(2,1)S(1)}, bf16[32,1024]{1,0:T(8,128)(2,1)S(1)}, u32[]{:S(2)}, u32[]{:S(2)}) %collective-permute-start.2) | collective-permute-done | bytes 65568 | tf_op jit(solution)/shard_map/ppermute | solution.py:391
  8.6 0.0 collective-permute-done.refs_1_
  8.6 0.7 shard_map.83
  9.3 0.4 collective-permute-start.5
  9.7 6.2 %all-to-all-start = ((bf16[8,32,512]{2,1,0:T(8,128)(2,1)}), bf16[8,32,512]{2,1,0:T(8,128)(2,1)S(1)}, u32[]{:S(2)}, u32[]{:S(2)}) async-start(bf16[8,32,512]{2,1,0:T(8,128)(2,1)} %shard_map.83), calls=%async_computation | async-start | bytes 524288 | tf_op jit(solution)/shard_map/all_to_all | solution.py:379
  15.9 0.0 collective-permute-start.4
  15.9 7.0 %collective-permute-done.5.refs_2_ = bf16[256,1024]{1,0:T(8,128)(2,1)S(1)} collective-permute-done((bf16[256,1024]{1,0:T(8,128)(2,1)S(1)}, bf16[256,1024]{1,0:T(8,128)(2,1)S(1)}, u32[]{:S(2)}, u32[]{:S(2)}) %collective-permute-start.5) | collective-permute-done | bytes 524320 | tf_op jit(solution)/shard_map/ppermute | solution.py:401
  23.0 0.0 collective-permute-start.6
  23.0 0.7 copy-done.5
  23.7 0.7 copy-done.6
  24.3 0.7 copy-done.7
  25.0 0.3 shard_map.84
  25.3 0.0 all-to-all-done.slots_ref
  25.3 0.2 shard_map.85.mine_ref
  25.5 0.6 collective-permute-start.3
  26.0 0.9 %collective-permute-done.3.other_ref = bf16[64,512]{1,0:T(8,128)(2,1)S(1)} collective-permute-done((bf16[64,512]{1,0:T(8,128)(2,1)S(1)}, bf16[64,512]{1,0:T(8,128)(2,1)S(1)}, u32[]{:S(2)}, u32[]{:S(2)}) %collective-permute-start.3) | collective-permute-done | bytes 65568 | tf_op jit(solution)/shard_map/ppermute | solution.py:407
  26.9 1.9 %copy-done = bf16[3,512,1024]{2,1,0:T(8,128)(2,1)S(1)} copy-done((bf16[3,512,1024]{2,1,0:T(8,128)(2,1)S(1)}, bf16[3,512,1024]{2,1,0:T(8,128)(2,1)}, u32[]{:S(2)}) %copy-start) | copy-done | bytes 3145752
  28.8 1.4 %shard_map.86 = bf16[8,3,64,128]{3,2,1,0:T(8,128)(2,1)} custom-call(bf16[64,512]{1,0:T(8,128)(2,1)S(1)} %shard_map.85.mine_ref, bf16[64,512]{1,0:T(8,128)(2,1)S(1)} %collective-permute-done.3.other_ref, bf16[3,512,1024]{2,1,0:T(8,128)(2,1)S(1)} %copy-done), custom_call_target="tpu_custom_call" | custom-call | tf_op jit(solution)/shard_map/pallas_call | solution.py:122
  30.2 0.0 collective-permute-done.4.refs_1_
  30.2 0.0 collective-permute-done.6.refs_3_
  30.2 6.0 %all-to-all-start.1 = ((bf16[8,3,64,128]{3,2,1,0:T(8,128)(2,1)}), bf16[8,3,64,128]{3,2,1,0:T(8,128)(2,1)S(1)}, u32[]{:S(2)}, u32[]{:S(2)}) async-start(bf16[8,3,64,128]{3,2,1,0:T(8,128)(2,1)} %shard_map.86), calls=%async_computation.1 | async-start | bytes 786432 | tf_op jit(solution)/shard_map/all_to_all | solution.py:379
  36.2 8.4 %shard_map.87 = (bf16[256,256]{1,0:T(8,128)(2,1)}, bf16[2,256,1024]{2,1,0:T(8,128)(2,1)}) custom-call(bf16[256,1024]{1,0:T(8,128)(2,1)} %copy-done.3, bf16[256,1024]{1,0:T(8,128)(2,1)} %copy-done.10, bf16[256,1024]{1,0:T(8,128)(2,1)} %copy-done.9, bf16[256,1024]{1,0:T(8,128)(2,1)} %copy-done.11, bf16[3,4096,256]{2,1,0:T(8,128)(2,1)} %refs_4_.1, ...), custom_call_target="tpu_custom_call" | custom-call | flops 1610612736 | tf_op jit(solution)/shard_map/pallas_call | solution.py:122
  44.7 0.0 copy-start.1
  44.7 3.7 %all-to-all-done.1.parts_ref = bf16[8,3,64,128]{3,2,1,0:T(8,128)(2,1)S(1)} async-done(((bf16[8,3,64,128]{3,2,1,0:T(8,128)(2,1)}), bf16[8,3,64,128]{3,2,1,0:T(8,128)(2,1)S(1)}, u32[]{:S(2)}, u32[]{:S(2)}) %all-to-all-start.1) | async-done | bytes 393248 | tf_op jit(solution)/shard_map/all_to_all | solution.py:379
  48.4 0.0 collective-permute-start.7
  48.4 1.0 %shard_map.88 = bf16[8,64,128]{2,1,0:T(8,128)(2,1)} custom-call(bf16[8,3,64,128]{3,2,1,0:T(8,128)(2,1)S(1)} %all-to-all-done.1.parts_ref), custom_call_target="tpu_custom_call" | custom-call | tf_op jit(solution)/shard_map/pallas_call | solution.py:122
  49.4 3.7 %all-to-all-start.2 = ((bf16[8,64,128]{2,1,0:T(8,128)(2,1)}), bf16[8,64,128]{2,1,0:T(8,128)(2,1)S(1)}, u32[]{:S(2)}, u32[]{:S(2)}) async-start(bf16[8,64,128]{2,1,0:T(8,128)(2,1)} %shard_map.88), calls=%async_computation.2 | async-start | bytes 262144 | tf_op jit(solution)/shard_map/all_to_all | solution.py:379
  53.1 0.0 collective-permute-done.7.got
  53.1 1.0 %copy-done.8 = bf16[2,256,1024]{2,1,0:T(8,128)(2,1)} copy-done((bf16[2,256,1024]{2,1,0:T(8,128)(2,1)}, bf16[2,256,1024]{2,1,0:T(8,128)(2,1)S(1)}, u32[]{:S(2)}) %copy-start.8) | copy-done | bytes 1048600
  54.1 0.9 %copy-done.4 = bf16[256,256]{1,0:T(8,128)(2,1)S(1)} copy-done((bf16[256,256]{1,0:T(8,128)(2,1)S(1)}, bf16[256,256]{1,0:T(8,128)(2,1)}, u32[]{:S(2)}) %copy-start.4) | copy-done | bytes 131096
  55.0 2.8 %shard_map.89 = (f32[256,1024]{1,0:T(8,128)}, bf16[256,1024]{1,0:T(8,128)(2,1)}) custom-call(bf16[256,4096]{1,0:T(8,128)(2,1)} %w_out.1, bf16[2,256,1024]{2,1,0:T(8,128)(2,1)} %copy-done.8, bf16[256,256]{1,0:T(8,128)(2,1)S(1)} %copy-done.4), custom_call_target="tpu_custom_call" | custom-call | flops 268435456 | tf_op jit(solution)/shard_map/pallas_call | solution.py:122
  57.7 3.0 %all-to-all-done.2.heads_ref = bf16[8,64,128]{2,1,0:T(8,128)(2,1)S(1)} async-done(((bf16[8,64,128]{2,1,0:T(8,128)(2,1)}), bf16[8,64,128]{2,1,0:T(8,128)(2,1)S(1)}, u32[]{:S(2)}, u32[]{:S(2)}) %all-to-all-start.2) | async-done | bytes 131104 | tf_op jit(solution)/shard_map/all_to_all | solution.py:379
  60.7 1.2 %shard_map.90 = bf16[8,32,512]{2,1,0:T(8,128)(2,1)} custom-call(bf16[8,64,128]{2,1,0:T(8,128)(2,1)S(1)} %all-to-all-done.2.heads_ref, bf16[1024,512]{1,0:T(8,128)(2,1)S(1)} %copy-done.1, bf16[64,256]{1,0:T(8,128)(2,1)S(1)} %get-tuple-element.60.chosen_ref), custom_call_target="tpu_custom_call" | custom-call | tf_op jit(solution)/shard_map/pallas_call | solution.py:122
  61.9 3.4 %all-to-all-start.3 = ((bf16[8,32,512]{2,1,0:T(8,128)(2,1)}), bf16[8,32,512]{2,1,0:T(8,128)(2,1)S(1)}, u32[]{:S(2)}, u32[]{:S(2)}) async-start(bf16[8,32,512]{2,1,0:T(8,128)(2,1)} %shard_map.90), calls=%async_computation.3 | async-start | bytes 524288 | tf_op jit(solution)/shard_map/all_to_all | solution.py:379
  65.3 1.4 %collective-permute-start.8 = (bf16[256,1024]{1,0:T(8,128)(2,1)}, bf16[256,1024]{1,0:T(8,128)(2,1)S(1)}, u32[]{:S(2)}, u32[]{:S(2)}) collective-permute-start(bf16[256,1024]{1,0:T(8,128)(2,1)} %get-tuple-element.58), channel_id=1, source_target_pairs={{0,2},{1,3},{2,0},{3,1},{4,6},{5,7},{6,4},{7,5},{8,10},{9,11},{10,... | collective-permute-start | bytes 1572872 | tf_op jit(solution)/shard_map/ppermute | solution.py:448
  66.8 7.2 %all-to-all-done.3.back_ref = bf16[8,32,512]{2,1,0:T(8,128)(2,1)S(1)} async-done(((bf16[8,32,512]{2,1,0:T(8,128)(2,1)}), bf16[8,32,512]{2,1,0:T(8,128)(2,1)S(1)}, u32[]{:S(2)}, u32[]{:S(2)}) %all-to-all-start.3) | async-done | bytes 262176 | tf_op jit(solution)/shard_map/all_to_all | solution.py:379
  74.0 0.1 collective-permute-start.9
  74.1 1.3 %collective-permute-done.9.got_ref = bf16[2,2,32,512]{3,2,1,0:T(8,128)(2,1)S(1)} collective-permute-done((bf16[2,2,32,512]{3,2,1,0:T(8,128)(2,1)S(1)}, bf16[2,2,32,512]{3,2,1,0:T(8,128)(2,1)S(1)}, u32[]{:S(2)}, u32[]{:S(2)}) %collective-permute-start.9) | collective-permute-done | bytes 131104 | tf_op jit(solution)/shard_map/ppermute | solution.py:460
  75.4 1.4 %collective-permute-start.10 = (bf16[2,32,512]{2,1,0:T(8,128)(2,1)S(1)}, bf16[2,32,512]{2,1,0:T(8,128)(2,1)S(1)}, u32[]{:S(2)}, u32[]{:S(2)}) collective-permute-start(bf16[2,32,512]{2,1,0:T(8,128)(2,1)S(1)} %shard_map.92), channel_id=1, source_target_pairs={{0,2},{1,3},{2,0},{3,1},{4,6},{5,7},{6,4},{7,5},{8,10},{9,11},{10,... | collective-permute-start | bytes 196616 | tf_op jit(solution)/shard_map/ppermute | solution.py:462
  76.8 2.2 %collective-permute-done.8.light_far_ref = bf16[256,1024]{1,0:T(8,128)(2,1)S(1)} collective-permute-done((bf16[256,1024]{1,0:T(8,128)(2,1)}, bf16[256,1024]{1,0:T(8,128)(2,1)S(1)}, u32[]{:S(2)}, u32[]{:S(2)}) %collective-permute-start.8) | collective-permute-done | bytes 524320 | tf_op jit(solution)/shard_map/ppermute | solution.py:448
  79.0 1.1 %collective-permute-done.10.last_ref = bf16[2,32,512]{2,1,0:T(8,128)(2,1)S(1)} collective-permute-done((bf16[2,32,512]{2,1,0:T(8,128)(2,1)S(1)}, bf16[2,32,512]{2,1,0:T(8,128)(2,1)S(1)}, u32[]{:S(2)}, u32[]{:S(2)}) %collective-permute-start.10) | collective-permute-done | bytes 65568 | tf_op jit(solution)/shard_map/ppermute | solution.py:462
  80.0 1.3 %shard_map.93 = bf16[256,1024]{1,0:T(8,128)(2,1)} custom-call(f32[256,1024]{1,0:T(8,128)S(1)} %copy-done.2, bf16[256,1024]{1,0:T(8,128)(2,1)S(1)} %collective-permute-done.8.light_far_ref, bf16[8,32,512]{2,1,0:T(8,128)(2,1)S(1)} %all-to-all-done.3.back_ref, bf16[2,2,32,512]{3,2,1,0:T(8,128)(2,1)S(1)} %collective-permute-done.9.got_ref, ...), custom_call_target="tpu_custom_call" | custom-call | tf_op jit(solution)/shard_map/pallas_call | solution.py:122
  (18 shorter events, 0.1 us)
Async XLA Ops:
  1.4 34.8 %copy-start.3 = (bf16[256,1024]{1,0:T(8,128)(2,1)}, bf16[256,1024]{1,0:T(8,128)(2,1)S(1)}, u32[]{:S(2)}) copy-start(bf16[256,1024]{1,0:T(8,128)(2,1)S(1)} %get-tuple-element.46.refs_0_) | copy-start | bytes 1572868
  1.4 5.2 %collective-permute-start.1 = (bf16[32,1024]{1,0:T(8,128)(2,1)S(1)}, bf16[32,1024]{1,0:T(8,128)(2,1)S(1)}, u32[]{:S(2)}, u32[]{:S(2)}) collective-permute-start(bf16[32,1024]{1,0:T(8,128)(2,1)S(1)} %get-tuple-element.34.refs_0_), channel_id=1, source_target_pairs={{0,2},{1,3},{2,0},{3,1},{4,6},{5,7},{6,4},{7,5},{8,10},{9,11},{10,... | collective-permute-start | bytes 196616 | tf_op jit(solution)/shard_map/ppermute | solution.py:390
  4.4 4.1 %collective-permute-start.2 = (bf16[32,1024]{1,0:T(8,128)(2,1)S(1)}, bf16[32,1024]{1,0:T(8,128)(2,1)S(1)}, u32[]{:S(2)}, u32[]{:S(2)}) collective-permute-start(bf16[32,1024]{1,0:T(8,128)(2,1)S(1)} %get-tuple-element.35), channel_id=1, source_target_pairs={{0,3},{1,2},{2,1},{3,0},{4,7},{5,6},{6,5},{7,4},{8,11},{9,10},{10,... | collective-permute-start | bytes 196616 | tf_op jit(solution)/shard_map/ppermute | solution.py:391
  4.4 4.1 %collective-permute-start = (bf16[32,1024]{1,0:T(8,128)(2,1)S(1)}, bf16[32,1024]{1,0:T(8,128)(2,1)S(1)}, u32[]{:S(2)}, u32[]{:S(2)}) collective-permute-start(bf16[32,1024]{1,0:T(8,128)(2,1)S(1)} %get-tuple-element.35), channel_id=1, source_target_pairs={{0,1},{1,0},{2,3},{3,2},{4,5},{5,4},{6,7},{7,6},{8,9},{9,8},{10,11... | collective-permute-start | bytes 196616 | tf_op jit(solution)/shard_map/ppermute | solution.py:389
  9.3 13.7 %collective-permute-start.5 = (bf16[256,1024]{1,0:T(8,128)(2,1)S(1)}, bf16[256,1024]{1,0:T(8,128)(2,1)S(1)}, u32[]{:S(2)}, u32[]{:S(2)}) collective-permute-start(bf16[256,1024]{1,0:T(8,128)(2,1)S(1)} %get-tuple-element.46.refs_0_), channel_id=1, source_target_pairs={{0,2},{1,3},{2,0},{3,1},{4,6},{5,7},{6,4},{7,5},{8,10},{9,11},{10,... | collective-permute-start | bytes 1572872 | tf_op jit(solution)/shard_map/ppermute | solution.py:401
  9.7 15.6 %all-to-all-start = ((bf16[8,32,512]{2,1,0:T(8,128)(2,1)}), bf16[8,32,512]{2,1,0:T(8,128)(2,1)S(1)}, u32[]{:S(2)}, u32[]{:S(2)}) async-start(bf16[8,32,512]{2,1,0:T(8,128)(2,1)} %shard_map.83), calls=%async_computation | async-start | bytes 524288 | tf_op jit(solution)/shard_map/all_to_all | solution.py:379
  15.9 14.3 %collective-permute-start.4 = (bf16[256,1024]{1,0:T(8,128)(2,1)S(1)}, bf16[256,1024]{1,0:T(8,128)(2,1)S(1)}, u32[]{:S(2)}, u32[]{:S(2)}) collective-permute-start(bf16[256,1024]{1,0:T(8,128)(2,1)S(1)} %get-tuple-element.46.refs_0_), channel_id=1, source_target_pairs={{0,1},{1,0},{2,3},{3,2},{4,5},{5,4},{6,7},{7,6},{8,9},{9,8},{10,11... | collective-permute-start | bytes 1572872 | tf_op jit(solution)/shard_map/ppermute | solution.py:402
  23.0 13.3 %copy-start.9 = (bf16[256,1024]{1,0:T(8,128)(2,1)}, bf16[256,1024]{1,0:T(8,128)(2,1)S(1)}, u32[]{:S(2)}) copy-start(bf16[256,1024]{1,0:T(8,128)(2,1)S(1)} %collective-permute-done.5.refs_2_) | copy-start | bytes 1572868
  23.0 7.3 %collective-permute-start.6 = (bf16[256,1024]{1,0:T(8,128)(2,1)S(1)}, bf16[256,1024]{1,0:T(8,128)(2,1)S(1)}, u32[]{:S(2)}, u32[]{:S(2)}) collective-permute-start(bf16[256,1024]{1,0:T(8,128)(2,1)S(1)} %collective-permute-done.5.refs_2_), channel_id=1, source_target_pairs={{0,1},{1,0},{2,3},{3,2},{4,5},{5,4},{6,7},{7,6},{8,9},{9,8},{10,11... | collective-permute-start | bytes 1572872 | tf_op jit(solution)/shard_map/ppermute | solution.py:403
  23.0 0.7 copy-start.5
  23.7 0.7 copy-start.6
  24.3 0.7 copy-start.7
  25.5 1.5 %collective-permute-start.3 = (bf16[64,512]{1,0:T(8,128)(2,1)S(1)}, bf16[64,512]{1,0:T(8,128)(2,1)S(1)}, u32[]{:S(2)}, u32[]{:S(2)}) collective-permute-start(bf16[64,512]{1,0:T(8,128)(2,1)S(1)} %shard_map.85.mine_ref), channel_id=1, source_target_pairs={{0,1},{1,0},{2,3},{3,2},{4,5},{5,4},{6,7},{7,6},{8,9},{9,8},{10,11... | collective-permute-start | bytes 196616 | tf_op jit(solution)/shard_map/ppermute | solution.py:407
  26.9 1.9 %copy-start = (bf16[3,512,1024]{2,1,0:T(8,128)(2,1)S(1)}, bf16[3,512,1024]{2,1,0:T(8,128)(2,1)}, u32[]{:S(2)}) copy-start(bf16[3,512,1024]{2,1,0:T(8,128)(2,1)} %weight_ref.2) | copy-start | bytes 9437188
  30.2 6.0 %copy-start.10 = (bf16[256,1024]{1,0:T(8,128)(2,1)}, bf16[256,1024]{1,0:T(8,128)(2,1)S(1)}, u32[]{:S(2)}) copy-start(bf16[256,1024]{1,0:T(8,128)(2,1)S(1)} %collective-permute-done.4.refs_1_) | copy-start | bytes 1572868
  30.2 6.0 %copy-start.11 = (bf16[256,1024]{1,0:T(8,128)(2,1)}, bf16[256,1024]{1,0:T(8,128)(2,1)S(1)}, u32[]{:S(2)}) copy-start(bf16[256,1024]{1,0:T(8,128)(2,1)S(1)} %collective-permute-done.6.refs_3_) | copy-start | bytes 1572868
  30.2 18.2 %all-to-all-start.1 = ((bf16[8,3,64,128]{3,2,1,0:T(8,128)(2,1)}), bf16[8,3,64,128]{3,2,1,0:T(8,128)(2,1)S(1)}, u32[]{:S(2)}, u32[]{:S(2)}) async-start(bf16[8,3,64,128]{3,2,1,0:T(8,128)(2,1)} %shard_map.86), calls=%async_computation.1 | async-start | bytes 786432 | tf_op jit(solution)/shard_map/all_to_all | solution.py:379
  44.7 16.1 %copy-start.1 = (bf16[1024,512]{1,0:T(8,128)(2,1)S(1)}, bf16[1024,512]{1,0:T(8,128)(2,1)}, u32[]{:S(2)}) copy-start(bf16[1024,512]{1,0:T(8,128)(2,1)} %weight_ref.3) | copy-start | bytes 3145732
  48.4 4.7 %collective-permute-start.7 = (bf16[2,256,1024]{2,1,0:T(8,128)(2,1)}, bf16[2,256,1024]{2,1,0:T(8,128)(2,1)S(1)}, u32[]{:S(2)}, u32[]{:S(2)}) collective-permute-start(bf16[2,256,1024]{2,1,0:T(8,128)(2,1)} %get-tuple-element.53), channel_id=1, source_target_pairs={{0,1},{1,0},{2,3},{3,2},{4,5},{5,4},{6,7},{7,6},{8,9},{9,8},{10,11... | collective-permute-start | bytes 3145736 | tf_op jit(solution)/shard_map/ppermute | solution.py:432
  49.4 11.3 %all-to-all-start.2 = ((bf16[8,64,128]{2,1,0:T(8,128)(2,1)}), bf16[8,64,128]{2,1,0:T(8,128)(2,1)S(1)}, u32[]{:S(2)}, u32[]{:S(2)}) async-start(bf16[8,64,128]{2,1,0:T(8,128)(2,1)} %shard_map.88), calls=%async_computation.2 | async-start | bytes 262144 | tf_op jit(solution)/shard_map/all_to_all | solution.py:379
  53.1 1.0 %copy-start.8 = (bf16[2,256,1024]{2,1,0:T(8,128)(2,1)}, bf16[2,256,1024]{2,1,0:T(8,128)(2,1)S(1)}, u32[]{:S(2)}) copy-start(bf16[2,256,1024]{2,1,0:T(8,128)(2,1)S(1)} %collective-permute-done.7.got) | copy-start | bytes 3145732
  54.1 0.9 %copy-start.4 = (bf16[256,256]{1,0:T(8,128)(2,1)S(1)}, bf16[256,256]{1,0:T(8,128)(2,1)}, u32[]{:S(2)}) copy-start(bf16[256,256]{1,0:T(8,128)(2,1)} %get-tuple-element.54.heads_ref) | copy-start | bytes 393220
  57.7 22.3 %copy-start.2 = (f32[256,1024]{1,0:T(8,128)S(1)}, f32[256,1024]{1,0:T(8,128)}, u32[]{:S(2)}) copy-start(f32[256,1024]{1,0:T(8,128)} %get-tuple-element.57.light_ref) | copy-start | bytes 3145732
  61.9 12.1 %all-to-all-start.3 = ((bf16[8,32,512]{2,1,0:T(8,128)(2,1)}), bf16[8,32,512]{2,1,0:T(8,128)(2,1)S(1)}, u32[]{:S(2)}, u32[]{:S(2)}) async-start(bf16[8,32,512]{2,1,0:T(8,128)(2,1)} %shard_map.90), calls=%async_computation.3 | async-start | bytes 524288 | tf_op jit(solution)/shard_map/all_to_all | solution.py:379
  65.3 13.7 %collective-permute-start.8 = (bf16[256,1024]{1,0:T(8,128)(2,1)}, bf16[256,1024]{1,0:T(8,128)(2,1)S(1)}, u32[]{:S(2)}, u32[]{:S(2)}) collective-permute-start(bf16[256,1024]{1,0:T(8,128)(2,1)} %get-tuple-element.58), channel_id=1, source_target_pairs={{0,2},{1,3},{2,0},{3,1},{4,6},{5,7},{6,4},{7,5},{8,10},{9,11},{10,... | collective-permute-start | bytes 1572872 | tf_op jit(solution)/shard_map/ppermute | solution.py:448
  74.0 1.4 %collective-permute-start.9 = (bf16[2,2,32,512]{3,2,1,0:T(8,128)(2,1)S(1)}, bf16[2,2,32,512]{3,2,1,0:T(8,128)(2,1)S(1)}, u32[]{:S(2)}, u32[]{:S(2)}) collective-permute-start(bf16[2,2,32,512]{3,2,1,0:T(8,128)(2,1)S(1)} %shard_map.91), channel_id=1, source_target_pairs={{0,1},{1,0},{2,3},{3,2},{4,5},{5,4},{6,7},{7,6},{8,9},{9,8},{10,11... | collective-permute-start | bytes 393224 | tf_op jit(solution)/shard_map/ppermute | solution.py:460
  75.4 4.6 %collective-permute-start.10 = (bf16[2,32,512]{2,1,0:T(8,128)(2,1)S(1)}, bf16[2,32,512]{2,1,0:T(8,128)(2,1)S(1)}, u32[]{:S(2)}, u32[]{:S(2)}) collective-permute-start(bf16[2,32,512]{2,1,0:T(8,128)(2,1)S(1)} %shard_map.92), channel_id=1, source_target_pairs={{0,2},{1,3},{2,0},{3,1},{4,6},{5,7},{6,4},{7,5},{8,10},{9,11},{10,... | collective-permute-start | bytes 196616 | tf_op jit(solution)/shard_map/ppermute | solution.py:462

commit v5 on v4

--- a/solution.py
+++ b/solution.py
@@ -1,3 +1,4 @@
+import functools
 import math
 
 import jax
@@ -155,62 +156,75 @@
 
 
 def pick_kernel(
-    tok_hbm, query_hbm, source_hbm, keep_ref, send_ref, tok_ref, query_ref, source_ref, sems
+    tok_hbm,
+    query_hbm,
+    source_hbm,
+    gate_hbm,
+    keep_ref,
+    send_ref,
+    mine_ref,
+    query_map_ref,
+    own_map_ref,
+    gate_map_ref,
+    tok_ref,
+    query_ref,
+    source_ref,
+    gate_ref,
+    sems,
 ):
-    copies = [
-        pltpu.make_async_copy(*ends, sems.at[i])
-        for i, ends in enumerate(
-            ((query_hbm, query_ref), (source_hbm, source_ref), (tok_hbm, tok_ref))
-        )
-    ]
+    ends = (
+        (query_hbm, query_ref),
+        (source_hbm, source_ref),
+        (gate_hbm, gate_ref),
+        (tok_hbm, tok_ref),
+    )
+    copies = [pltpu.make_async_copy(*e, sems.at[i]) for i, e in enumerate(ends)]
     for copy in copies:
         copy.start()
-    seq_index, odd = lax.axis_index("seq"), lax.axis_index("head") % 2
-    copies[0].wait()
-    copies[1].wait()
-    own_q = own_row(query_ref[...], seq_index)
-    own_s = own_row(source_ref[...], seq_index)
-    spot = lax.broadcasted_iota(jnp.int32, (tok_ref.shape[0], own_q.shape[1]), 0)
+    odd = lax.axis_index("head") % 2
+    for copy in copies[:3]:
+        copy.wait()
+    query, source = query_ref[...], source_ref[...]
+    own_q = own_row(query, lax.axis_index("seq"))
+    own_s = own_row(source, lax.axis_index("seq"))
+    spot = lax.broadcasted_iota(jnp.int32, own_map_ref.shape, 0)
     chosen = [onehot(spot == jnp.where(odd == k, own_q, own_s)) for k in range(2)]
-    copies[2].wait()
+    own_map_ref[...] = onehot(spot == own_q)
+    compact_onehot(query, query_map_ref)
+    compact_onehot(jnp.where(odd == 0, query, source), mine_ref)
+    slots = own_q.shape[1]
+    diagonal = lax.broadcasted_iota(jnp.int32, (slots, slots), 0) == lax.broadcasted_iota(
+        jnp.int32, (slots, slots), 1
+    )
+    gate = jnp.sum(jnp.where(diagonal, gate_ref[...], 0.0), axis=1, keepdims=True)
+    gate_map_ref[...] = jnp.broadcast_to(gate, gate_map_ref.shape)
+    copies[3].wait()
     for ref, rows in zip((keep_ref, send_ref), chosen):
         ref[...] = lax.dot_general(rows, tok_ref[...], FIRST, preferred_element_type=F32).astype(
             BF
         )
 
 
-def prepare_kernel(
-    query_ref, source_ref, gate_ref, mine_ref, query_map_ref, own_map_ref, gate_map_ref
-):
+def spread_kernel(keep_ref, got_ref, out_ref):
     odd = lax.axis_index("head") % 2
-    query, source = query_ref[...], source_ref[...]
-    compact_onehot(query, query_map_ref)
-    compact_onehot(jnp.where(odd == 0, query, source), mine_ref)
-    own_q = own_row(query, lax.axis_index("seq"))
-    spot = lax.broadcasted_iota(jnp.int32, own_map_ref.shape, 0)
-    own_map_ref[...] = onehot(spot == own_q)
-    slots = own_q.shape[1]
-    diagonal = lax.broadcasted_iota(jnp.int32, (slots, slots), 0) == lax.broadcasted_iota(
-        jnp.int32, (slots, slots), 1
-    )
-    gate = jnp.sum(jnp.where(diagonal, gate_ref[...], 0.0), axis=1, keepdims=True)
-    gate_map_ref[...] = jnp.broadcast_to(gate, gate_map_ref.shape)
-
-
-def spread_kernel(*refs):
-    *pieces, out_ref = refs
-    head = lax.axis_index("head")
+    keep, got = keep_ref[...], got_ref[...]
     width = out_ref.shape[2]
-    per = out_ref.shape[0] // len(pieces)
-    for j, piece in enumerate(pieces):
-        owner = head ^ j
+    per = keep.shape[1] // width
+    for part, block in enumerate((jnp.where(odd == 0, keep, got), jnp.where(odd == 0, got, keep))):
         for i in range(per):
-            out_ref[owner * per + i] = piece[:, i * width : (i + 1) * width]
+            for at in range(part * per + i, out_ref.shape[0], 2 * per):
+                out_ref[at] = block[:, i * width : (i + 1) * width]
 
 
 def compact_kernel(slots_ref, chosen_ref, out_ref):
     rows = slots_ref[...].reshape(-1, slots_ref.shape[2])
     out_ref[...] = jnp.dot(chosen_ref[...], rows, preferred_element_type=F32).astype(BF)
+
+
+def choose_kernel(mine_ref, crossed_ref, out_ref):
+    pairs = lax.axis_size("head") // 2
+    holder = lax.axis_index("seq") * pairs // lax.axis_size("seq")
+    out_ref[...] = jnp.where(holder == lax.axis_index("head") // 2, mine_ref[...], crossed_ref[...])
 
 
 def project_kernel(mine_ref, other_ref, weight_ref, out_ref):
@@ -288,69 +302,88 @@
         out_ref[:, cols] = (light + added).astype(BF)
 
 
-def light_kernel(*refs):
-    count = len(refs) - 9
-    pieces, (w_in, w_out, heads_ref, give_ref, *held) = refs[:count], refs[count:]
-    tok_ref, in_ref, out_ref, sems, gave_sems = held
+def light_kernel(flips, last, *refs):
+    count = len(flips)
+    pieces, (w_in, *refs) = refs[:count], refs[count:]
+    if last:
+        before, w_out, heads_ref, give_ref, before_ref, out_ref, *refs = refs
+    else:
+        sum_ref, *refs = refs
+    tok_ref, in_ref, sems = refs[:3]
     head = lax.axis_index("head")
     depth = pieces[0].shape[1]
-    width = give_ref.shape[2]
-
-    def rows(j):
-        return pl.ds(pl.multiple_of((head ^ j) * depth, depth), depth)
-
-    def cols(j):
-        return pl.ds(pl.multiple_of((head ^ j) * width, width), width)
-
     copies = []
-    for j, piece in enumerate(pieces):
-        copies.append(pltpu.make_async_copy(piece, tok_ref.at[j], sems.at[0, j]))
+    for i, (j, piece) in enumerate(zip(flips, pieces)):
+        rows = pl.ds(pl.multiple_of((head ^ j) * depth, depth), depth)
+        copies.append(pltpu.make_async_copy(piece, tok_ref.at[i], sems.at[0, i]))
         for c in range(3):
             copies.append(
-                pltpu.make_async_copy(
-                    w_in.at[c, rows(j), :], in_ref.at[c, j], sems.at[1 + c, j]
-                )
+                pltpu.make_async_copy(w_in.at[c, rows, :], in_ref.at[c, i], sems.at[1 + c, i])
             )
-    late = [
-        pltpu.make_async_copy(w_out.at[:, cols(j)], out_ref.at[i], gave_sems.at[i])
-        for i, j in enumerate((1, 3))
-    ]
+    late = []
+    if last:
+        late_sems = refs[3]
+        width = give_ref.shape[2]
+        late.append(pltpu.make_async_copy(before, before_ref, late_sems.at[2]))
+        for i, j in enumerate((1, 3)):
+            cols = pl.ds(pl.multiple_of((head ^ j) * width, width), width)
+            late.append(pltpu.make_async_copy(w_out.at[:, cols], out_ref.at[i], late_sems.at[i]))
     for copy in copies + late:
         copy.start()
     total = [None] * 3
-    for j in range(count):
-        copies[4 * j].wait()
+    for i in range(count):
+        copies[4 * i].wait()
         for c in range(3):
-            copies[4 * j + 1 + c].wait()
-            part = jnp.dot(tok_ref[j], in_ref[c, j], preferred_element_type=F32)
-            total[c] = part if j == 0 else total[c] + part
-    mapped = [t.astype(BF) for t in total]
+            copies[4 * i + 1 + c].wait()
+            part = jnp.dot(tok_ref[i], in_ref[c, i], preferred_element_type=F32)
+            total[c] = part if i == 0 else total[c] + part
+    if not last:
+        for c in range(3):
+            sum_ref[c] = total[c]
+        return
+    late[0].wait()
+    mapped = [(before_ref[c] + total[c]).astype(BF) for c in range(3)]
     for b in range(heads_ref.shape[0] // LB):
         for g in range(heads_ref.shape[1] // HD):
             at = (slice(b * LB, (b + 1) * LB), slice(g * HD, (g + 1) * HD))
             heads_ref[at] = one_head(*(m[at] for m in mapped))
     for i in range(2):
-        late[i].wait()
-        give_ref[i] = jnp.dot(
-            heads_ref[...], out_ref[i], preferred_element_type=F32
-        ).astype(BF)
-
-
-def light_own_kernel(w_out, got, heads_ref, own_ref, far_ref, out_ref, got_ref, sems):
+        late[1 + i].wait()
+        give_ref[i] = jnp.dot(heads_ref[...], out_ref[i], preferred_element_type=F32).astype(BF)
+
+
+def light_own_kernel(w_out, got_ref, heads_ref, own_ref, far_ref, out_ref, sems):
     head = lax.axis_index("head")
     width = own_ref.shape[1]
     copies = []
     for i, j in enumerate((0, 2)):
         cols = pl.ds(pl.multiple_of((head ^ j) * width, width), width)
-        copies.append(pltpu.make_async_copy(w_out.at[:, cols], out_ref.at[i], sems.at[0, i]))
-        copies.append(pltpu.make_async_copy(got.at[i], got_ref.at[i], sems.at[1, i]))
+        copies.append(pltpu.make_async_copy(w_out.at[:, cols], out_ref.at[i], sems.at[i]))
     for copy in copies:
         copy.start()
     for i, ref in enumerate((own_ref, far_ref)):
-        copies[2 * i].wait()
-        copies[2 * i + 1].wait()
+        copies[i].wait()
         block = jnp.dot(heads_ref[...], out_ref[i], preferred_element_type=F32)
         ref[...] = (block + got_ref[i].astype(F32)).astype(ref.dtype)
+
+
+def light_call(flips, last, outs, pieces, *arrays, scratch=()):
+    count = len(flips)
+    rows, width = pieces[0].shape
+    return on_chip(
+        functools.partial(light_kernel, flips, last),
+        outs,
+        hbm=(*pieces, *arrays),
+        scratch=[
+            *scratch,
+            pltpu.VMEM((count, rows, width), BF),
+            pltpu.VMEM((3, count, width, arrays[0].shape[2]), BF),
+            pltpu.SemaphoreType.DMA((4, count)),
+            pltpu.SemaphoreType.DMA((3,)),
+        ],
+        flops=6 * count * rows * width * arrays[0].shape[2],
+        off=True,
+    )
 
 
 def one_head_a_device(
@@ -371,75 +404,83 @@
     out_cols = heavy_output.shape[1]
     light_cols = light_input.shape[2]
     per = seq_count // head_count
-    pair, across, diagonal = (
-        [(i, i ^ j) for i in range(head_count)] for j in (1, 2, 3)
-    )
+    pair, across = ([(i, i ^ j) for i in range(head_count)] for j in (1, 2))
 
     def swap(x):
         return lax.all_to_all(x, "seq", split_axis=0, concat_axis=0, tiled=True)
 
-    keep, send, tokens = on_chip(
+    routes = (routed, seq_count * slots)
+    keep, send, mine_map, query_map, own_map, gate_map = on_chip(
         pick_kernel,
-        [((slots, own_width), BF)] * 2 + [(tokens.shape, BF)],
-        hbm=(tokens, query_tokens, context_tokens),
-        scratch=[pltpu.VMEM(query_tokens.shape, jnp.int32)] * 2 + [pltpu.SemaphoreType.DMA((3,))],
-    )
-    pieces = (
-        keep,
-        lax.ppermute(send, "head", pair),
-        lax.ppermute(keep, "head", across),
-        lax.ppermute(send, "head", diagonal),
-    )
-    spread = on_chip(spread_kernel, [((seq_count, slots, part_width), BF)], *pieces)
-    tables = (query_tokens, context_tokens, query_gate)
-    spread, tables, tokens = lax.optimization_barrier((spread, tables, tokens))
-    mine_map, query_map, own_map, gate_map = on_chip(
-        prepare_kernel,
-        [((routed, seq_count * slots), BF)] * 2 + [((tok_rows, slots), BF), ((slots, HD), F32)],
-        *tables,
-    )
+        [((slots, own_width), BF)] * 2
+        + [(routes, BF)] * 2
+        + [((tok_rows, slots), BF), ((slots, HD), F32)],
+        hbm=(tokens, query_tokens, context_tokens, query_gate),
+        scratch=[
+            pltpu.VMEM(tokens.shape, BF),
+            pltpu.VMEM(query_tokens.shape, jnp.int32),
+            pltpu.VMEM(context_tokens.shape, jnp.int32),
+            pltpu.VMEM(query_gate.shape, F32),
+            pltpu.SemaphoreType.DMA((4,)),
+        ],
+    )
+    got = lax.ppermute(send, "head", pair)
+    spread = on_chip(spread_kernel, [((seq_count, slots, part_width), BF)], keep, got)
+    spread, tokens = lax.optimization_barrier((spread, tokens))
     token_far = lax.ppermute(tokens, "head", across)
     token_pair = lax.ppermute(tokens, "head", pair)
+    light_sum = light_call(
+        (0, 1),
+        False,
+        [((3, tok_rows, light_cols), F32)],
+        (tokens, token_pair),
+        light_input,
+    )
+    spread = swap(spread)
+    spread, token_far, light_sum = lax.optimization_barrier((spread, token_far, light_sum))
     token_last = lax.ppermute(token_far, "head", pair)
-    spread = swap(spread)
-    spread, mine_map = lax.optimization_barrier((spread, mine_map))
-    mine = on_chip(compact_kernel, [((routed, part_width), BF)], spread, mine_map)
+    mine = on_chip(compact_kernel, [((routed, part_width), BF)], spread, mine_map, moved=20 << 20)
+    half = seq_count * 2 // head_count
+    holds = [
+        (s * head_count + h, s * head_count + (h ^ 2))
+        for s in range(seq_count)
+        for h in range(head_count)
+        if s // half == h // 2
+    ]
+    crossed = lax.ppermute(mine, ("seq", "head"), holds)
+    mine = on_chip(choose_kernel, [((routed, part_width), BF)], mine, crossed)
     other = lax.ppermute(mine, "head", pair)
     parts = on_chip(
         project_kernel, [((seq_count, 3, routed, HD), BF)], mine, other, heavy_input
     )
 
-    parts, token_pieces = lax.optimization_barrier(
-        (parts, (tokens, token_pair, token_far, token_last))
-    )
-    light_heads, light_give = on_chip(
-        light_kernel,
+    parts, light_sum, token_far, token_last = lax.optimization_barrier(
+        (parts, light_sum, token_far, token_last)
+    )
+    light_heads, light_give = light_call(
+        (2, 3),
+        True,
         [((tok_rows, light_cols), BF), ((2, tok_rows, own_width), BF)],
-        hbm=(*token_pieces, light_input, light_output),
+        (token_far, token_last),
+        light_input,
+        light_sum,
+        light_output,
         scratch=[
-            pltpu.VMEM((head_count, tok_rows, own_width), BF),
-            pltpu.VMEM((3, head_count, own_width, light_cols), BF),
+            pltpu.VMEM((3, tok_rows, light_cols), F32),
             pltpu.VMEM((2, light_cols, own_width), BF),
-            pltpu.SemaphoreType.DMA((4, head_count)),
-            pltpu.SemaphoreType.DMA((2,)),
         ],
-        flops=6 * tok_rows * light_cols * own_width * head_count,
-        off=True,
     )
     parts = swap(parts)
     parts, light_heads, light_give = lax.optimization_barrier((parts, light_heads, light_give))
+    light_got = lax.ppermute(light_give, "head", pair)
     heads = on_chip(heavy_attend_kernel, [((seq_count, routed, HD), BF)], parts)
-    light_got = lax.ppermute(light_give, "head", pair)
     light_own, light_far = on_chip(
         light_own_kernel,
         [((tok_rows, own_width), F32), ((tok_rows, own_width), BF)],
+        light_got,
         light_heads,
-        hbm=(light_output, light_got),
-        scratch=[
-            pltpu.VMEM((2, light_cols, own_width), BF),
-            pltpu.VMEM((2, tok_rows, own_width), BF),
-            pltpu.SemaphoreType.DMA((2, 2)),
-        ],
+        hbm=(light_output,),
+        scratch=[pltpu.VMEM((2, light_cols, own_width), BF), pltpu.SemaphoreType.DMA((2,))],
         flops=4 * tok_rows * light_cols * own_width,
         off=True,
     )
@@ -447,15 +488,15 @@
     heads, light_own, light_far = lax.optimization_barrier((heads, light_own, light_far))
     light_far = lax.ppermute(light_far, "head", across)
 
-    back = swap(
-        on_chip(
-            heavy_output_kernel,
-            [((seq_count, slots, out_cols), BF)],
-            heads,
-            heavy_output,
-            query_map,
-        )
-    )
+    back = on_chip(
+        heavy_output_kernel,
+        [((seq_count, slots, out_cols), BF)],
+        heads,
+        heavy_output,
+        query_map,
+    )
+    back = swap(back)
+    back, light_far = lax.optimization_barrier((back, light_far))
     give = on_chip(give_kernel, [((2, per, slots, out_cols), BF)], back)
     got = lax.ppermute(give, "head", pair)
     far = on_chip(far_kernel, [((per, slots, out_cols), BF)], back, got)

time: 82 us -> 79.6 us (0.971)
  blocking collectives: 0 us -> 11.1 us
  waiting for transfers between devices: 30.3 us -> 23.9 us
  local copies, waits for them, and re-layouts: 5.81 us -> 0.91 us
  starting transfers between devices: 26.4 us -> 22.4 us
  Pallas kernels: 18.6 us -> 20.7 us
    all_to_all x0 -> x1, blocking collectives: none -> 11.1 us  [swap(): return lax.all_to_all(x, 'seq', split_axis=0, concat_axis=0, tiled=True)]
    ppermute x1, waiting for transfers between devices: 7.03 us -> 0.01 us  [one_head_a_device(): token_far = lax.ppermute(tokens, 'head', across)]
    unnamed x24 -> x8, local copies, waits for them, and re-layouts: 5.81 us -> 0.91 us
    all_to_all x4 -> x3, starting transfers between devices: 19.3 us -> 15.3 us  [swap(): return lax.all_to_all(x, 'seq', split_axis=0, concat_axis=0, tiled=True)]
    ppermute x1, waiting for transfers between devices: 1.05 us -> 3.63 us  [one_head_a_device(): last = lax.ppermute(far, 'head', across)]
    ppermute x1, starting transfers between devices: 0.41 us -> 2.64 us  [one_head_a_device(): token_far = lax.ppermute(tokens, 'head', across)]
    pallas_call x12 -> x13, Pallas kernels: 18.6 us -> 20.7 us  [on_chip(): pl.pallas_call(kernel, in_specs=[pl.BlockSpec(memory_space=pl.ANY)] * len...]
    ppermute x1, waiting for transfers between devices: 2.16 us -> 1.06 us  [one_head_a_device(): light_far = lax.ppermute(light_far, 'head', across)]
  transfers between devices with their start and end apart: 15 -> 13, of which waited for: 10 -> 9; matrix products, arithmetic and copies ran while one was open for 0% -> 0% of each run, Pallas kernels for 17% -> 22%
where the time goes in v5:
time: 79.6 us; the launch traced here: 79.1 us
  waiting for transfers between devices  23.9 us (30%)
  starting transfers between devices  22.4 us (28%)
  Pallas kernels  20.7 us (26%)
  blocking collectives  11.1 us (14%)
  local copies, waits for them, and re-layouts  0.91 us (1%)
    pallas_call x13, Pallas kernels, on_chip(): pl.pallas_call(kernel, in_specs=[pl.BlockSpec(memory_space=pl.ANY)] * len...  20.7 us
    all_to_all x3, starting transfers between devices, swap(): return lax.all_to_all(x, 'seq', split_axis=0, concat_axis=0, tiled=True)  15.3 us
    all_to_all x3, waiting for transfers between devices, swap(): return lax.all_to_all(x, 'seq', split_axis=0, concat_axis=0, tiled=True)  13.7 us
    all_to_all x1, blocking collectives, swap(): return lax.all_to_all(x, 'seq', split_axis=0, concat_axis=0, tiled=True)  11.1 us
    ppermute x1, waiting for transfers between devices, one_head_a_device(): last = lax.ppermute(far, 'head', across)  3.63 us
    ppermute x1, starting transfers between devices, one_head_a_device(): token_far = lax.ppermute(tokens, 'head', across)  2.64 us
    ppermute x1, starting transfers between devices, one_head_a_device(): crossed = lax.ppermute(mine, ('seq', 'head'), holds)  2.44 us
    ppermute x1, waiting for transfers between devices, one_head_a_device(): crossed = lax.ppermute(mine, ('seq', 'head'), holds)  2 us
  transfers between devices with their start and end apart: 13, of which 9 were waited for; matrix products, arithmetic and copies ran while one was open for 0% of the time, Pallas kernels for 22%

profile of v5, /device:TPU:0, one launch (start us, length us, event | category | flops | bytes accessed | tf_op | source)
XLA Modules:
  0.0 79.1 jit_solution(18444128712921063426)
XLA Ops:
  0.0 1.4 %shard_map.82 = (bf16[32,1024]{1,0:T(8,128)(2,1)S(1)}, bf16[32,1024]{1,0:T(8,128)(2,1)S(1)}, bf16[64,256]{1,0:T(8,128)(2,1)S(1)}, bf16[64,256]{1,0:T(8,128)(2,1)...) custom-call(bf16[256,1024]{1,0:T(8,128)(2,1)} %refs_0_, s32[8,32]{1,0:T(8,128)} %query_hbm.1, ...), custom_call_target="tpu_custom_call" | custom-call | tf_op jit(solution)/shard_map/pallas_call | solution.py:123
  1.4 0.5 collective-permute-start
  2.0 0.9 %collective-permute-done.got_ref = bf16[32,1024]{1,0:T(8,128)(2,1)S(1)} collective-permute-done((bf16[32,1024]{1,0:T(8,128)(2,1)S(1)}, bf16[32,1024]{1,0:T(8,128)(2,1)S(1)}, u32[]{:S(2)}, u32[]{:S(2)}) %collective-permute-start) | collective-permute-done | bytes 65568 | tf_op jit(solution)/shard_map/ppermute | solution.py:427
  2.9 0.7 shard_map.83
  3.6 0.4 collective-permute-start.2
  3.9 2.6 %collective-permute-start.1 = (bf16[256,1024]{1,0:T(8,128)(2,1)}, bf16[256,1024]{1,0:T(8,128)(2,1)}, u32[]{:S(2)}, u32[]{:S(2)}) collective-permute-start(bf16[256,1024]{1,0:T(8,128)(2,1)} %refs_0_), channel_id=1, source_target_pairs={{0,2},{1,3},{2,0},{3,1},{4,6},{5,7},{6,4},{7,5},{8,10},{9,11},{10,... | collective-permute-start | bytes 1572872 | tf_op jit(solution)/shard_map/ppermute | solution.py:430
  6.6 5.8 %all-to-all-start = ((bf16[8,32,512]{2,1,0:T(8,128)(2,1)}), bf16[8,32,512]{2,1,0:T(8,128)(2,1)S(1)}, u32[]{:S(2)}, u32[]{:S(2)}) async-start(bf16[8,32,512]{2,1,0:T(8,128)(2,1)} %shard_map.83), calls=%async_computation | async-start | bytes 524288 | tf_op jit(solution)/shard_map/all_to_all | solution.py:410
  12.4 0.0 copy-start
  12.4 0.0 collective-permute-done.2.refs_1_
  12.4 4.8 %shard_map.84.refs_3_ = f32[3,256,256]{2,1,0:T(8,128)} custom-call(bf16[256,1024]{1,0:T(8,128)(2,1)} %refs_0_, bf16[256,1024]{1,0:T(8,128)(2,1)} %collective-permute-done.2.refs_1_, bf16[3,4096,256]{2,1,0:T(8,128)(2,1)} %refs_2_.3), custom_call_target="tpu_custom_call" | custom-call | flops 805306368 | tf_op jit(solution)/shard_map/pallas_call | solution.py:123
  17.3 4.3 %all-to-all-done.slots_ref = bf16[8,32,512]{2,1,0:T(8,128)(2,1)S(1)} async-done(((bf16[8,32,512]{2,1,0:T(8,128)(2,1)}), bf16[8,32,512]{2,1,0:T(8,128)(2,1)S(1)}, u32[]{:S(2)}, u32[]{:S(2)}) %all-to-all-start) | async-done | bytes 262176 | tf_op jit(solution)/shard_map/all_to_all | solution.py:410
  21.6 0.0 collective-permute-done.1.refs_0_
  21.6 0.0 collective-permute-start.5
  21.6 0.2 shard_map.85.mine_ref
  21.7 2.4 %collective-permute-start.3 = (bf16[64,512]{1,0:T(8,128)(2,1)S(1)}, bf16[64,512]{1,0:T(8,128)(2,1)S(1)}, u32[]{:S(2)}, u32[]{:S(2)}) collective-permute-start(bf16[64,512]{1,0:T(8,128)(2,1)S(1)} %shard_map.85.mine_ref), channel_id=1, source_target_pairs={{0,2},{1,3},{4,6},{5,7},{8,10},{9,11},{12,14},{13,15},{18,16},{19,... | collective-permute-start | bytes 196616 | tf_op jit(solution)/shard_map/ppermute | solution.py:450
  24.2 2.0 %collective-permute-done.3.crossed_ref = bf16[64,512]{1,0:T(8,128)(2,1)S(1)} collective-permute-done((bf16[64,512]{1,0:T(8,128)(2,1)S(1)}, bf16[64,512]{1,0:T(8,128)(2,1)S(1)}, u32[]{:S(2)}, u32[]{:S(2)}) %collective-permute-start.3) | collective-permute-done | bytes 65568 | tf_op jit(solution)/shard_map/ppermute | solution.py:450
  26.2 0.1 collective-permute-start.4
  26.3 1.2 %collective-permute-done.4.other_ref = bf16[64,512]{1,0:T(8,128)(2,1)S(1)} collective-permute-done((bf16[64,512]{1,0:T(8,128)(2,1)S(1)}, bf16[64,512]{1,0:T(8,128)(2,1)S(1)}, u32[]{:S(2)}, u32[]{:S(2)}) %collective-permute-start.4) | collective-permute-done | bytes 65568 | tf_op jit(solution)/shard_map/ppermute | solution.py:452
  27.5 0.0 copy-done
  27.5 1.4 %shard_map.87 = bf16[8,3,64,128]{3,2,1,0:T(8,128)(2,1)} custom-call(bf16[64,512]{1,0:T(8,128)(2,1)S(1)} %shard_map.86.mine_ref, bf16[64,512]{1,0:T(8,128)(2,1)S(1)} %collective-permute-done.4.other_ref, bf16[3,512,1024]{2,1,0:T(8,128)(2,1)S(1)} %copy-done), custom_call_target="tpu_custom_call" | custom-call | tf_op jit(solution)/shard_map/pallas_call | solution.py:123
  28.9 0.0 collective-permute-done.5.refs_1_
  29.0 5.8 %all-to-all-start.1 = ((bf16[8,3,64,128]{3,2,1,0:T(8,128)(2,1)}), bf16[8,3,64,128]{3,2,1,0:T(8,128)(2,1)S(1)}, u32[]{:S(2)}, u32[]{:S(2)}) async-start(bf16[8,3,64,128]{3,2,1,0:T(8,128)(2,1)} %shard_map.87), calls=%async_computation.1 | async-start | bytes 786432 | tf_op jit(solution)/shard_map/all_to_all | solution.py:410
  34.7 6.8 %shard_map.88 = (bf16[256,256]{1,0:T(8,128)(2,1)}, bf16[2,256,1024]{2,1,0:T(8,128)(2,1)}) custom-call(bf16[256,1024]{1,0:T(8,128)(2,1)} %collective-permute-done.1.refs_0_, bf16[256,1024]{1,0:T(8,128)(2,1)} %collective-permute-done.5.refs_1_, bf16[3,4096,256]{2,1,0:T(8,128)(2,1)} %refs_2_.3, f32[3,256,256]{2,1,0:T(8,128)} %shard_map.84.refs_3_, ...), custom_call_target="tpu_custom_call" | custom-call | flops 805306368 | tf_op jit(solution)/shard_map/pallas_call | solution.py:123
  41.5 0.0 copy-start.1
  41.5 5.2 %all-to-all-done.1.parts_ref = bf16[8,3,64,128]{3,2,1,0:T(8,128)(2,1)S(1)} async-done(((bf16[8,3,64,128]{3,2,1,0:T(8,128)(2,1)}), bf16[8,3,64,128]{3,2,1,0:T(8,128)(2,1)S(1)}, u32[]{:S(2)}, u32[]{:S(2)}) %all-to-all-start.1) | async-done | bytes 393248 | tf_op jit(solution)/shard_map/all_to_all | solution.py:410
  46.7 0.0 collective-permute-start.6
  46.7 1.0 %shard_map.89 = bf16[8,64,128]{2,1,0:T(8,128)(2,1)} custom-call(bf16[8,3,64,128]{3,2,1,0:T(8,128)(2,1)S(1)} %all-to-all-done.1.parts_ref), custom_call_target="tpu_custom_call" | custom-call | tf_op jit(solution)/shard_map/pallas_call | solution.py:123
  47.8 3.6 %all-to-all-start.2 = ((bf16[8,64,128]{2,1,0:T(8,128)(2,1)}), bf16[8,64,128]{2,1,0:T(8,128)(2,1)S(1)}, u32[]{:S(2)}, u32[]{:S(2)}) async-start(bf16[8,64,128]{2,1,0:T(8,128)(2,1)} %shard_map.89), calls=%async_computation.2 | async-start | bytes 262144 | tf_op jit(solution)/shard_map/all_to_all | solution.py:410
  51.4 0.0 collective-permute-done.6.got_ref
  51.4 0.0 copy-start.3
  51.4 0.9 %copy-done.3 = bf16[256,256]{1,0:T(8,128)(2,1)S(1)} copy-done((bf16[256,256]{1,0:T(8,128)(2,1)S(1)}, bf16[256,256]{1,0:T(8,128)(2,1)}, u32[]{:S(2)}) %copy-start.3) | copy-done | bytes 131096
  52.3 2.5 %shard_map.90 = (f32[256,1024]{1,0:T(8,128)}, bf16[256,1024]{1,0:T(8,128)(2,1)}) custom-call(bf16[256,4096]{1,0:T(8,128)(2,1)} %w_out.1, bf16[2,256,1024]{2,1,0:T(8,128)(2,1)S(1)} %collective-permute-done.6.got_ref, bf16[256,256]{1,0:T(8,128)(2,1)S(1)} %copy-done.3), custom_call_target="tpu_custom_call" | custom-call | flops 268435456 | tf_op jit(solution)/shard_map/pallas_call | solution.py:123
  54.8 0.0 copy-start.2
  54.9 4.2 %all-to-all-done.2.heads_ref = bf16[8,64,128]{2,1,0:T(8,128)(2,1)S(1)} async-done(((bf16[8,64,128]{2,1,0:T(8,128)(2,1)}), bf16[8,64,128]{2,1,0:T(8,128)(2,1)S(1)}, u32[]{:S(2)}, u32[]{:S(2)}) %all-to-all-start.2) | async-done | bytes 131104 | tf_op jit(solution)/shard_map/all_to_all | solution.py:410
  59.1 0.3 collective-permute-start.7
  59.4 0.0 copy-done.1
  59.4 0.5 shard_map.91
  59.9 11.1 %all_to_all.20.back_ref = bf16[8,32,512]{2,1,0:T(8,128)(2,1)S(1)} all-to-all(bf16[8,32,512]{2,1,0:T(8,128)(2,1)S(1)} %shard_map.91), channel_id=1, replica_groups=mesh['seq'=8,'head'=4] {'seq'}, dimensions={0} | all-to-all | bytes 524288 | tf_op jit(solution)/shard_map/all_to_all | solution.py:410
  71.0 1.1 %collective-permute-done.7.light_far_ref = bf16[256,1024]{1,0:T(8,128)(2,1)S(1)} collective-permute-done((bf16[256,1024]{1,0:T(8,128)(2,1)}, bf16[256,1024]{1,0:T(8,128)(2,1)S(1)}, u32[]{:S(2)}, u32[]{:S(2)}) %collective-permute-start.7) | collective-permute-done | bytes 524320 | tf_op jit(solution)/shard_map/ppermute | solution.py:489
  72.0 0.1 collective-permute-start.8
  72.1 1.3 %collective-permute-done.8.got_ref = bf16[2,2,32,512]{3,2,1,0:T(8,128)(2,1)S(1)} collective-permute-done((bf16[2,2,32,512]{3,2,1,0:T(8,128)(2,1)S(1)}, bf16[2,2,32,512]{3,2,1,0:T(8,128)(2,1)S(1)}, u32[]{:S(2)}, u32[]{:S(2)}) %collective-permute-start.8) | collective-permute-done | bytes 131104 | tf_op jit(solution)/shard_map/ppermute | solution.py:501
  73.5 0.7 collective-permute-start.9
  74.2 3.6 %collective-permute-done.9.last_ref = bf16[2,32,512]{2,1,0:T(8,128)(2,1)S(1)} collective-permute-done((bf16[2,32,512]{2,1,0:T(8,128)(2,1)S(1)}, bf16[2,32,512]{2,1,0:T(8,128)(2,1)S(1)}, u32[]{:S(2)}, u32[]{:S(2)}) %collective-permute-start.9) | collective-permute-done | bytes 65568 | tf_op jit(solution)/shard_map/ppermute | solution.py:503
  77.8 0.0 copy-done.2
  77.8 1.3 %shard_map.94 = bf16[256,1024]{1,0:T(8,128)(2,1)} custom-call(f32[256,1024]{1,0:T(8,128)S(1)} %copy-done.2, bf16[256,1024]{1,0:T(8,128)(2,1)S(1)} %collective-permute-done.7.light_far_ref, bf16[8,32,512]{2,1,0:T(8,128)(2,1)S(1)} %all_to_all.20.back_ref, bf16[2,2,32,512]{3,2,1,0:T(8,128)(2,1)S(1)} %collective-permute-done.8.got_ref, ...), custom_call_target="tpu_custom_call" | custom-call | tf_op jit(solution)/shard_map/pallas_call | solution.py:123
  (3 shorter events, 0.0 us)
Async XLA Ops:
  1.4 1.4 %collective-permute-start = (bf16[32,1024]{1,0:T(8,128)(2,1)S(1)}, bf16[32,1024]{1,0:T(8,128)(2,1)S(1)}, u32[]{:S(2)}, u32[]{:S(2)}) collective-permute-start(bf16[32,1024]{1,0:T(8,128)(2,1)S(1)} %get-tuple-element.33), channel_id=1, source_target_pairs={{0,1},{1,0},{2,3},{3,2},{4,5},{5,4},{6,7},{7,6},{8,9},{9,8},{10,11... | collective-permute-start | bytes 196616 | tf_op jit(solution)/shard_map/ppermute | solution.py:427
  3.6 8.8 %collective-permute-start.2 = (bf16[256,1024]{1,0:T(8,128)(2,1)}, bf16[256,1024]{1,0:T(8,128)(2,1)}, u32[]{:S(2)}, u32[]{:S(2)}) collective-permute-start(bf16[256,1024]{1,0:T(8,128)(2,1)} %refs_0_), channel_id=1, source_target_pairs={{0,1},{1,0},{2,3},{3,2},{4,5},{5,4},{6,7},{7,6},{8,9},{9,8},{10,11... | collective-permute-start | bytes 1572872 | tf_op jit(solution)/shard_map/ppermute | solution.py:431
  3.9 17.6 %collective-permute-start.1 = (bf16[256,1024]{1,0:T(8,128)(2,1)}, bf16[256,1024]{1,0:T(8,128)(2,1)}, u32[]{:S(2)}, u32[]{:S(2)}) collective-permute-start(bf16[256,1024]{1,0:T(8,128)(2,1)} %refs_0_), channel_id=1, source_target_pairs={{0,2},{1,3},{2,0},{3,1},{4,6},{5,7},{6,4},{7,5},{8,10},{9,11},{10,... | collective-permute-start | bytes 1572872 | tf_op jit(solution)/shard_map/ppermute | solution.py:430
  6.6 15.0 %all-to-all-start = ((bf16[8,32,512]{2,1,0:T(8,128)(2,1)}), bf16[8,32,512]{2,1,0:T(8,128)(2,1)S(1)}, u32[]{:S(2)}, u32[]{:S(2)}) async-start(bf16[8,32,512]{2,1,0:T(8,128)(2,1)} %shard_map.83), calls=%async_computation | async-start | bytes 524288 | tf_op jit(solution)/shard_map/all_to_all | solution.py:410
  12.4 15.1 %copy-start = (bf16[3,512,1024]{2,1,0:T(8,128)(2,1)S(1)}, bf16[3,512,1024]{2,1,0:T(8,128)(2,1)}, u32[]{:S(2)}) copy-start(bf16[3,512,1024]{2,1,0:T(8,128)(2,1)} %weight_ref.2) | copy-start | bytes 9437188
  21.6 7.4 %collective-permute-start.5 = (bf16[256,1024]{1,0:T(8,128)(2,1)}, bf16[256,1024]{1,0:T(8,128)(2,1)}, u32[]{:S(2)}, u32[]{:S(2)}) collective-permute-start(bf16[256,1024]{1,0:T(8,128)(2,1)} %collective-permute-done.1.refs_0_), channel_id=1, source_target_pairs={{0,1},{1,0},{2,3},{3,2},{4,5},{5,4},{6,7},{7,6},{8,9},{9,8},{10,11... | collective-permute-start | bytes 1572872 | tf_op jit(solution)/shard_map/ppermute | solution.py:441
  21.7 4.5 %collective-permute-start.3 = (bf16[64,512]{1,0:T(8,128)(2,1)S(1)}, bf16[64,512]{1,0:T(8,128)(2,1)S(1)}, u32[]{:S(2)}, u32[]{:S(2)}) collective-permute-start(bf16[64,512]{1,0:T(8,128)(2,1)S(1)} %shard_map.85.mine_ref), channel_id=1, source_target_pairs={{0,2},{1,3},{4,6},{5,7},{8,10},{9,11},{12,14},{13,15},{18,16},{19,... | collective-permute-start | bytes 196616 | tf_op jit(solution)/shard_map/ppermute | solution.py:450
  26.2 1.3 %collective-permute-start.4 = (bf16[64,512]{1,0:T(8,128)(2,1)S(1)}, bf16[64,512]{1,0:T(8,128)(2,1)S(1)}, u32[]{:S(2)}, u32[]{:S(2)}) collective-permute-start(bf16[64,512]{1,0:T(8,128)(2,1)S(1)} %shard_map.86.mine_ref), channel_id=1, source_target_pairs={{0,1},{1,0},{2,3},{3,2},{4,5},{5,4},{6,7},{7,6},{8,9},{9,8},{10,11... | collective-permute-start | bytes 196616 | tf_op jit(solution)/shard_map/ppermute | solution.py:452
  29.0 17.8 %all-to-all-start.1 = ((bf16[8,3,64,128]{3,2,1,0:T(8,128)(2,1)}), bf16[8,3,64,128]{3,2,1,0:T(8,128)(2,1)S(1)}, u32[]{:S(2)}, u32[]{:S(2)}) async-start(bf16[8,3,64,128]{3,2,1,0:T(8,128)(2,1)} %shard_map.87), calls=%async_computation.1 | async-start | bytes 786432 | tf_op jit(solution)/shard_map/all_to_all | solution.py:410
  41.5 17.9 %copy-start.1 = (bf16[1024,512]{1,0:T(8,128)(2,1)S(1)}, bf16[1024,512]{1,0:T(8,128)(2,1)}, u32[]{:S(2)}) copy-start(bf16[1024,512]{1,0:T(8,128)(2,1)} %weight_ref.3) | copy-start | bytes 3145732
  46.7 4.7 %collective-permute-start.6 = (bf16[2,256,1024]{2,1,0:T(8,128)(2,1)}, bf16[2,256,1024]{2,1,0:T(8,128)(2,1)S(1)}, u32[]{:S(2)}, u32[]{:S(2)}) collective-permute-start(bf16[2,256,1024]{2,1,0:T(8,128)(2,1)} %get-tuple-element.47), channel_id=1, source_target_pairs={{0,1},{1,0},{2,3},{3,2},{4,5},{5,4},{6,7},{7,6},{8,9},{9,8},{10,11... | collective-permute-start | bytes 3145736 | tf_op jit(solution)/shard_map/ppermute | solution.py:475
  47.8 11.3 %all-to-all-start.2 = ((bf16[8,64,128]{2,1,0:T(8,128)(2,1)}), bf16[8,64,128]{2,1,0:T(8,128)(2,1)S(1)}, u32[]{:S(2)}, u32[]{:S(2)}) async-start(bf16[8,64,128]{2,1,0:T(8,128)(2,1)} %shard_map.89), calls=%async_computation.2 | async-start | bytes 262144 | tf_op jit(solution)/shard_map/all_to_all | solution.py:410
  51.4 0.9 %copy-start.3 = (bf16[256,256]{1,0:T(8,128)(2,1)S(1)}, bf16[256,256]{1,0:T(8,128)(2,1)}, u32[]{:S(2)}) copy-start(bf16[256,256]{1,0:T(8,128)(2,1)} %get-tuple-element.48.heads_ref) | copy-start | bytes 393220
  54.8 23.0 %copy-start.2 = (f32[256,1024]{1,0:T(8,128)S(1)}, f32[256,1024]{1,0:T(8,128)}, u32[]{:S(2)}) copy-start(f32[256,1024]{1,0:T(8,128)} %get-tuple-element.51.light_ref) | copy-start | bytes 3145732
  59.1 13.0 %collective-permute-start.7 = (bf16[256,1024]{1,0:T(8,128)(2,1)}, bf16[256,1024]{1,0:T(8,128)(2,1)S(1)}, u32[]{:S(2)}, u32[]{:S(2)}) collective-permute-start(bf16[256,1024]{1,0:T(8,128)(2,1)} %get-tuple-element.54), channel_id=1, source_target_pairs={{0,2},{1,3},{2,0},{3,1},{4,6},{5,7},{6,4},{7,5},{8,10},{9,11},{10,... | collective-permute-start | bytes 1572872 | tf_op jit(solution)/shard_map/ppermute | solution.py:489
  72.0 1.4 %collective-permute-start.8 = (bf16[2,2,32,512]{3,2,1,0:T(8,128)(2,1)S(1)}, bf16[2,2,32,512]{3,2,1,0:T(8,128)(2,1)S(1)}, u32[]{:S(2)}, u32[]{:S(2)}) collective-permute-start(bf16[2,2,32,512]{3,2,1,0:T(8,128)(2,1)S(1)} %shard_map.92), channel_id=1, source_target_pairs={{0,1},{1,0},{2,3},{3,2},{4,5},{5,4},{6,7},{7,6},{8,9},{9,8},{10,11... | collective-permute-start | bytes 393224 | tf_op jit(solution)/shard_map/ppermute | solution.py:501
  73.5 4.3 %collective-permute-start.9 = (bf16[2,32,512]{2,1,0:T(8,128)(2,1)S(1)}, bf16[2,32,512]{2,1,0:T(8,128)(2,1)S(1)}, u32[]{:S(2)}, u32[]{:S(2)}) collective-permute-start(bf16[2,32,512]{2,1,0:T(8,128)(2,1)S(1)} %shard_map.93), channel_id=1, source_target_pairs={{0,2},{1,3},{2,0},{3,1},{4,6},{5,7},{6,4},{7,5},{8,10},{9,11},{10,... | collective-permute-start | bytes 196616 | tf_op jit(solution)/shard_map/ppermute | solution.py:503

commit v6 on v5

--- a/solution.py
+++ b/solution.py
@@ -134,6 +134,23 @@
     return result if len(outs) > 1 else result[0]
 
 
+def listed(count):
+    inner = sorted(range(count), key=lambda i: 2 * abs(2 * i + 1 - count) // count)
+    return [i ^ 1 for i in inner]
+
+
+def spots(count):
+    order = listed(count)
+    return [order.index(i) for i in range(count)]
+
+
+def look_up(values, index):
+    found = jnp.int32(values[0])
+    for i, value in enumerate(values[1:], 1):
+        found = jnp.where(index == i, value, found)
+    return found
+
+
 def own_row(table, index):
     rows = lax.broadcasted_iota(jnp.int32, table.shape, 0)
     return jnp.sum(jnp.where(rows == index, table, 0), axis=0, keepdims=True)
@@ -145,13 +162,14 @@
 
 def compact_onehot(table, out_ref):
     shards, slots = table.shape
+    spot = spots(shards)
     live = (table >= 0).astype(jnp.int32)
     counts = jnp.sum(live, axis=1, keepdims=True)
     row = lax.broadcasted_iota(jnp.int32, (out_ref.shape[0], slots), 0)
     place = lax.broadcasted_iota(jnp.int32, (1, slots), 1)
     for s in range(shards):
         here = (row == place) & (table[s : s + 1] >= 0)
-        out_ref[:, s * slots : (s + 1) * slots] = onehot(here)
+        out_ref[:, spot[s] * slots : (spot[s] + 1) * slots] = onehot(here)
         place = place + counts[s : s + 1]
 
 
@@ -210,10 +228,11 @@
     keep, got = keep_ref[...], got_ref[...]
     width = out_ref.shape[2]
     per = keep.shape[1] // width
+    spot = spots(out_ref.shape[0])
     for part, block in enumerate((jnp.where(odd == 0, keep, got), jnp.where(odd == 0, got, keep))):
         for i in range(per):
             for at in range(part * per + i, out_ref.shape[0], 2 * per):
-                out_ref[at] = block[:, i * width : (i + 1) * width]
+                out_ref[spot[at]] = block[:, i * width : (i + 1) * width]
 
 
 def compact_kernel(slots_ref, chosen_ref, out_ref):
@@ -232,10 +251,11 @@
     mine, other = mine_ref[...], other_ref[...]
     query = jnp.where(odd == 0, mine, other)
     source = jnp.where(odd == 0, other, mine)
+    spot = spots(out_ref.shape[0])
     for c, rows in enumerate((query, source, source)):
         part = jnp.dot(rows, weight_ref[c], preferred_element_type=F32).astype(BF)
         for g in range(out_ref.shape[0]):
-            out_ref[g, c] = part[:, g * HD : (g + 1) * HD]
+            out_ref[spot[g], c] = part[:, g * HD : (g + 1) * HD]
 
 
 def one_head(query, key, value):
@@ -257,25 +277,31 @@
 
 
 def heavy_output_kernel(heads_ref, weight_ref, chosen_ref, out_ref):
-    rows = jnp.concatenate([heads_ref[g] for g in range(heads_ref.shape[0])], axis=1)
+    rows = jnp.concatenate([heads_ref[i] for i in spots(heads_ref.shape[0])], axis=1)
     part = jnp.dot(rows, weight_ref[...], preferred_element_type=F32).astype(BF)
     spread = lax.dot_general(chosen_ref[...], part, FIRST, preferred_element_type=F32).astype(BF)
     out_ref[...] = spread.reshape(out_ref.shape)
 
 
+def block_of(back_ref, head, per, i):
+    spot = spots(back_ref.shape[0])
+    return back_ref[look_up(spot[i::per], head)]
+
+
 def give_kernel(back_ref, out_ref):
     head = lax.axis_index("head")
     per = out_ref.shape[1]
-    for i, j in enumerate((1, 3)):
-        out_ref[i] = back_ref[pl.ds((head ^ j) * per, per)]
+    for k, j in enumerate((1, 3)):
+        for i in range(per):
+            out_ref[k, i] = block_of(back_ref, head ^ j, per, i)
 
 
 def far_kernel(back_ref, got_ref, out_ref):
     per = out_ref.shape[0]
-    far = lax.axis_index("head") ^ 2
-    out_ref[...] = (
-        back_ref[pl.ds(far * per, per)].astype(F32) + got_ref[1].astype(F32)
-    ).astype(BF)
+    head = lax.axis_index("head")
+    for i in range(per):
+        mine = block_of(back_ref, head ^ 2, per, i).astype(F32)
+        out_ref[i] = (mine + got_ref[1, i].astype(F32)).astype(BF)
 
 
 def finish_kernel(
@@ -283,15 +309,11 @@
 ):
     head = lax.axis_index("head")
     per = last_ref.shape[0]
-    heavy = (
-        back_ref[pl.ds(head * per, per)].astype(F32)
-        + got_ref[0].astype(F32)
-        + last_ref[...].astype(F32)
-    )
     chosen, gate = own_map_ref[...], gate_ref[:, :1]
-    width = heavy.shape[2]
+    width = last_ref.shape[2]
     for j in range(per):
-        scaled = heavy[j] * gate
+        mine = block_of(back_ref, head, per, j).astype(F32)
+        scaled = (mine + got_ref[0, j].astype(F32) + last_ref[j].astype(F32)) * gate
         coarse = scaled.astype(BF)
         fine = (scaled - coarse.astype(F32)).astype(BF)
         added = jnp.dot(chosen, coarse, preferred_element_type=F32) + jnp.dot(
@@ -407,7 +429,14 @@
     pair, across = ([(i, i ^ j) for i in range(head_count)] for j in (1, 2))
 
     def swap(x):
-        return lax.all_to_all(x, "seq", split_axis=0, concat_axis=0, tiled=True)
+        return lax.all_to_all(
+            x,
+            "seq",
+            split_axis=0,
+            concat_axis=0,
+            tiled=True,
+            axis_index_groups=[listed(seq_count)],
+        )
 
     routes = (routed, seq_count * slots)
     keep, send, mine_map, query_map, own_map, gate_map = on_chip(
@@ -426,9 +455,9 @@
     )
     got = lax.ppermute(send, "head", pair)
     spread = on_chip(spread_kernel, [((seq_count, slots, part_width), BF)], keep, got)
-    spread, tokens = lax.optimization_barrier((spread, tokens))
     token_far = lax.ppermute(tokens, "head", across)
     token_pair = lax.ppermute(tokens, "head", pair)
+    spread, tokens, token_pair = lax.optimization_barrier((spread, tokens, token_pair))
     light_sum = light_call(
         (0, 1),
         False,
@@ -496,10 +525,10 @@
         query_map,
     )
     back = swap(back)
-    back, light_far = lax.optimization_barrier((back, light_far))
     give = on_chip(give_kernel, [((2, per, slots, out_cols), BF)], back)
     got = lax.ppermute(give, "head", pair)
     far = on_chip(far_kernel, [((per, slots, out_cols), BF)], back, got)
+    far, light_far = lax.optimization_barrier((far, light_far))
     last = lax.ppermute(far, "head", across)
     return on_chip(
         finish_kernel,

time: 79.6 us -> 79.9 us (level)
  starting transfers between devices: 22.4 us -> 33.8 us
  blocking collectives: 11.1 us -> 0 us
    all_to_all x1 -> x0, blocking collectives: 11.1 us -> none  [swap(): return lax.all_to_all(x, 'seq', split_axis=0, concat_axis=0, tiled=True)]
    all_to_all x3 -> x4, starting transfers between devices: 15.3 us -> 23.6 us  [swap(): lax.all_to_all(x, 'seq', split_axis=0, concat_axis=0, tiled=True, axis_in...]
    ppermute x1, waiting for transfers between devices: 1.06 us -> 5.18 us  [one_head_a_device(): light_far = lax.ppermute(light_far, 'head', across)]
    all_to_all x3 -> x4, waiting for transfers between devices: 13.7 us -> 10.3 us  [swap(): lax.all_to_all(x, 'seq', split_axis=0, concat_axis=0, tiled=True, axis_in...]
    ppermute x1, starting transfers between devices: 0.33 us -> 1.6 us  [one_head_a_device(): light_far = lax.ppermute(light_far, 'head', across)]
    ppermute x1, waiting for transfers between devices: 3.63 us -> 2.67 us  [one_head_a_device(): last = lax.ppermute(far, 'head', across)]
    ppermute x1, starting transfers between devices: 2.44 us -> 3.36 us  [one_head_a_device(): crossed = lax.ppermute(mine, ('seq', 'head'), holds)]
    ppermute x1, waiting for transfers between devices: 0.9 us -> 0.01 us  [one_head_a_device(): got = lax.ppermute(send, 'head', pair)]
  transfers between devices with their start and end apart: 13 -> 14, of which waited for: 9 -> 10; matrix products, arithmetic and copies ran while one was open for 0% -> 0% of each run, Pallas kernels for 22% -> 24%
where the time goes in v6:
time: 79.9 us; the launch traced here: 79.4 us
  starting transfers between devices  33.8 us (42%)
  waiting for transfers between devices  23.2 us (29%)
  Pallas kernels  21.3 us (27%)
  local copies, waits for them, and re-layouts  0.92 us (1%)
    all_to_all x4, starting transfers between devices, swap(): lax.all_to_all(x, 'seq', split_axis=0, concat_axis=0, tiled=True, axis_in...  23.6 us
    pallas_call x13, Pallas kernels, on_chip(): pl.pallas_call(kernel, in_specs=[pl.BlockSpec(memory_space=pl.ANY)] * len...  21.3 us
    all_to_all x4, waiting for transfers between devices, swap(): lax.all_to_all(x, 'seq', split_axis=0, concat_axis=0, tiled=True, axis_in...  10.3 us
    ppermute x1, waiting for transfers between devices, one_head_a_device(): light_far = lax.ppermute(light_far, 'head', across)  5.18 us
    ppermute x1, starting transfers between devices, one_head_a_device(): crossed = lax.ppermute(mine, ('seq', 'head'), holds)  3.36 us
    ppermute x1, starting transfers between devices, one_head_a_device(): token_far = lax.ppermute(tokens, 'head', across)  2.94 us
    ppermute x1, waiting for transfers between devices, one_head_a_device(): last = lax.ppermute(far, 'head', across)  2.67 us
    ppermute x1, waiting for transfers between devices, one_head_a_device(): crossed = lax.ppermute(mine, ('seq', 'head'), holds)  2 us
  transfers between devices with their start and end apart: 14, of which 10 were waited for; matrix products, arithmetic and copies ran while one was open for 0% of the time, Pallas kernels for 24%

profile of v6, /device:TPU:0, one launch (start us, length us, event | category | flops | bytes accessed | tf_op | source)
XLA Modules:
  0.0 79.4 jit_solution(17993213611466398399)
XLA Ops:
  0.0 0.5 collective-permute-start.1
  0.5 1.4 %shard_map.82 = (bf16[32,1024]{1,0:T(8,128)(2,1)S(1)}, bf16[32,1024]{1,0:T(8,128)(2,1)S(1)}, bf16[64,256]{1,0:T(8,128)(2,1)S(1)}, bf16[64,256]{1,0:T(8,128)(2,1)...) custom-call(bf16[256,1024]{1,0:T(8,128)(2,1)} %refs_0_, s32[8,32]{1,0:T(8,128)} %query_hbm.1, ...), custom_call_target="tpu_custom_call" | custom-call | tf_op jit(solution)/shard_map/pallas_call | solution.py:123
  1.9 0.1 collective-permute-start
  2.0 2.9 %collective-permute-start.2 = (bf16[256,1024]{1,0:T(8,128)(2,1)}, bf16[256,1024]{1,0:T(8,128)(2,1)}, u32[]{:S(2)}, u32[]{:S(2)}) collective-permute-start(bf16[256,1024]{1,0:T(8,128)(2,1)} %refs_0_), channel_id=1, source_target_pairs={{0,2},{1,3},{2,0},{3,1},{4,6},{5,7},{6,4},{7,5},{8,10},{9,11},{10,... | collective-permute-start | bytes 1572872 | tf_op jit(solution)/shard_map/ppermute | solution.py:458
  5.0 0.0 collective-permute-done.got_ref
  5.0 0.7 shard_map.83
  5.7 0.0 collective-permute-done.1.refs_1_
  5.7 6.4 %all-to-all-start = ((bf16[8,32,512]{2,1,0:T(8,128)(2,1)}), bf16[8,32,512]{2,1,0:T(8,128)(2,1)S(1)}, u32[]{:S(2)}, u32[]{:S(2)}) async-start(bf16[8,32,512]{2,1,0:T(8,128)(2,1)} %shard_map.83), calls=%async_computation | async-start | bytes 524288 | tf_op jit(solution)/shard_map/all_to_all | solution.py:432
  12.1 0.0 copy-start
  12.1 4.8 %shard_map.84.refs_3_ = f32[3,256,256]{2,1,0:T(8,128)} custom-call(bf16[256,1024]{1,0:T(8,128)(2,1)} %refs_0_, bf16[256,1024]{1,0:T(8,128)(2,1)} %collective-permute-done.1.refs_1_, bf16[3,4096,256]{2,1,0:T(8,128)(2,1)} %refs_2_.3), custom_call_target="tpu_custom_call" | custom-call | flops 805306368 | tf_op jit(solution)/shard_map/pallas_call | solution.py:123
  16.9 0.5 collective-permute-done.2.refs_0_
  17.4 1.3 %all-to-all-done.slots_ref = bf16[8,32,512]{2,1,0:T(8,128)(2,1)S(1)} async-done(((bf16[8,32,512]{2,1,0:T(8,128)(2,1)}), bf16[8,32,512]{2,1,0:T(8,128)(2,1)S(1)}, u32[]{:S(2)}, u32[]{:S(2)}) %all-to-all-start) | async-done | bytes 262176 | tf_op jit(solution)/shard_map/all_to_all | solution.py:432
  18.8 0.0 collective-permute-start.5
  18.8 0.2 shard_map.85.mine_ref
  18.9 3.4 %collective-permute-start.3 = (bf16[64,512]{1,0:T(8,128)(2,1)S(1)}, bf16[64,512]{1,0:T(8,128)(2,1)S(1)}, u32[]{:S(2)}, u32[]{:S(2)}) collective-permute-start(bf16[64,512]{1,0:T(8,128)(2,1)S(1)} %shard_map.85.mine_ref), channel_id=1, source_target_pairs={{0,2},{1,3},{4,6},{5,7},{8,10},{9,11},{12,14},{13,15},{18,16},{19,... | collective-permute-start | bytes 196616 | tf_op jit(solution)/shard_map/ppermute | solution.py:479
  22.3 2.0 %collective-permute-done.3.crossed_ref = bf16[64,512]{1,0:T(8,128)(2,1)S(1)} collective-permute-done((bf16[64,512]{1,0:T(8,128)(2,1)S(1)}, bf16[64,512]{1,0:T(8,128)(2,1)S(1)}, u32[]{:S(2)}, u32[]{:S(2)}) %collective-permute-start.3) | collective-permute-done | bytes 65568 | tf_op jit(solution)/shard_map/ppermute | solution.py:479
  24.3 0.1 collective-permute-start.4
  24.4 1.2 %collective-permute-done.4.other_ref = bf16[64,512]{1,0:T(8,128)(2,1)S(1)} collective-permute-done((bf16[64,512]{1,0:T(8,128)(2,1)S(1)}, bf16[64,512]{1,0:T(8,128)(2,1)S(1)}, u32[]{:S(2)}, u32[]{:S(2)}) %collective-permute-start.4) | collective-permute-done | bytes 65568 | tf_op jit(solution)/shard_map/ppermute | solution.py:481
  25.6 0.0 copy-done
  25.6 1.4 %shard_map.87 = bf16[8,3,64,128]{3,2,1,0:T(8,128)(2,1)} custom-call(bf16[64,512]{1,0:T(8,128)(2,1)S(1)} %shard_map.86.mine_ref, bf16[64,512]{1,0:T(8,128)(2,1)S(1)} %collective-permute-done.4.other_ref, bf16[3,512,1024]{2,1,0:T(8,128)(2,1)S(1)} %copy-done), custom_call_target="tpu_custom_call" | custom-call | tf_op jit(solution)/shard_map/pallas_call | solution.py:123
  27.0 0.0 collective-permute-done.5.refs_1_
  27.0 6.4 %all-to-all-start.1 = ((bf16[8,3,64,128]{3,2,1,0:T(8,128)(2,1)}), bf16[8,3,64,128]{3,2,1,0:T(8,128)(2,1)S(1)}, u32[]{:S(2)}, u32[]{:S(2)}) async-start(bf16[8,3,64,128]{3,2,1,0:T(8,128)(2,1)} %shard_map.87), calls=%async_computation.1 | async-start | bytes 786432 | tf_op jit(solution)/shard_map/all_to_all | solution.py:432
  33.4 6.8 %shard_map.88 = (bf16[256,256]{1,0:T(8,128)(2,1)}, bf16[2,256,1024]{2,1,0:T(8,128)(2,1)}) custom-call(bf16[256,1024]{1,0:T(8,128)(2,1)} %collective-permute-done.2.refs_0_, bf16[256,1024]{1,0:T(8,128)(2,1)} %collective-permute-done.5.refs_1_, bf16[3,4096,256]{2,1,0:T(8,128)(2,1)} %refs_2_.3, f32[3,256,256]{2,1,0:T(8,128)} %shard_map.84.refs_3_, ...), custom_call_target="tpu_custom_call" | custom-call | flops 805306368 | tf_op jit(solution)/shard_map/pallas_call | solution.py:123
  40.2 0.0 copy-start.1
  40.2 2.7 %all-to-all-done.1.parts_ref = bf16[8,3,64,128]{3,2,1,0:T(8,128)(2,1)S(1)} async-done(((bf16[8,3,64,128]{3,2,1,0:T(8,128)(2,1)}), bf16[8,3,64,128]{3,2,1,0:T(8,128)(2,1)S(1)}, u32[]{:S(2)}, u32[]{:S(2)}) %all-to-all-start.1) | async-done | bytes 393248 | tf_op jit(solution)/shard_map/all_to_all | solution.py:432
  42.9 0.0 collective-permute-start.6
  42.9 1.0 %shard_map.89 = bf16[8,64,128]{2,1,0:T(8,128)(2,1)} custom-call(bf16[8,3,64,128]{3,2,1,0:T(8,128)(2,1)S(1)} %all-to-all-done.1.parts_ref), custom_call_target="tpu_custom_call" | custom-call | tf_op jit(solution)/shard_map/pallas_call | solution.py:123
  43.9 5.3 %all-to-all-start.2 = ((bf16[8,64,128]{2,1,0:T(8,128)(2,1)}), bf16[8,64,128]{2,1,0:T(8,128)(2,1)S(1)}, u32[]{:S(2)}, u32[]{:S(2)}) async-start(bf16[8,64,128]{2,1,0:T(8,128)(2,1)} %shard_map.89), calls=%async_computation.2 | async-start | bytes 262144 | tf_op jit(solution)/shard_map/all_to_all | solution.py:432
  49.2 0.0 collective-permute-done.6.got_ref
  49.2 0.0 copy-start.3
  49.2 0.9 %copy-done.3 = bf16[256,256]{1,0:T(8,128)(2,1)S(1)} copy-done((bf16[256,256]{1,0:T(8,128)(2,1)S(1)}, bf16[256,256]{1,0:T(8,128)(2,1)}, u32[]{:S(2)}) %copy-start.3) | copy-done | bytes 131096
  50.1 2.5 %shard_map.90 = (f32[256,1024]{1,0:T(8,128)}, bf16[256,1024]{1,0:T(8,128)(2,1)}) custom-call(bf16[256,4096]{1,0:T(8,128)(2,1)} %w_out.1, bf16[2,256,1024]{2,1,0:T(8,128)(2,1)S(1)} %collective-permute-done.6.got_ref, bf16[256,256]{1,0:T(8,128)(2,1)S(1)} %copy-done.3), custom_call_target="tpu_custom_call" | custom-call | flops 268435456 | tf_op jit(solution)/shard_map/pallas_call | solution.py:123
  52.6 0.0 copy-start.2
  52.6 1.4 %all-to-all-done.2.heads_ref = bf16[8,64,128]{2,1,0:T(8,128)(2,1)S(1)} async-done(((bf16[8,64,128]{2,1,0:T(8,128)(2,1)}), bf16[8,64,128]{2,1,0:T(8,128)(2,1)S(1)}, u32[]{:S(2)}, u32[]{:S(2)}) %all-to-all-start.2) | async-done | bytes 131104 | tf_op jit(solution)/shard_map/all_to_all | solution.py:432
  54.1 0.0 copy-done.1
  54.1 1.2 %shard_map.91 = bf16[8,32,512]{2,1,0:T(8,128)(2,1)} custom-call(bf16[8,64,128]{2,1,0:T(8,128)(2,1)S(1)} %all-to-all-done.2.heads_ref, bf16[1024,512]{1,0:T(8,128)(2,1)S(1)} %copy-done.1, bf16[64,256]{1,0:T(8,128)(2,1)S(1)} %get-tuple-element.55.chosen_ref), custom_call_target="tpu_custom_call" | custom-call | tf_op jit(solution)/shard_map/pallas_call | solution.py:123
  55.3 5.5 %all-to-all-start.3 = ((bf16[8,32,512]{2,1,0:T(8,128)(2,1)}), bf16[8,32,512]{2,1,0:T(8,128)(2,1)S(1)}, u32[]{:S(2)}, u32[]{:S(2)}) async-start(bf16[8,32,512]{2,1,0:T(8,128)(2,1)} %shard_map.91), calls=%async_computation.3 | async-start | bytes 524288 | tf_op jit(solution)/shard_map/all_to_all | solution.py:432
  60.8 1.6 %collective-permute-start.8 = (bf16[256,1024]{1,0:T(8,128)(2,1)}, bf16[256,1024]{1,0:T(8,128)(2,1)S(1)}, u32[]{:S(2)}, u32[]{:S(2)}) collective-permute-start(bf16[256,1024]{1,0:T(8,128)(2,1)} %get-tuple-element.56), channel_id=1, source_target_pairs={{0,2},{1,3},{2,0},{3,1},{4,6},{5,7},{6,4},{7,5},{8,10},{9,11},{10,... | collective-permute-start | bytes 1572872 | tf_op jit(solution)/shard_map/ppermute | solution.py:518
  62.4 4.8 %all-to-all-done.3.back_ref = bf16[8,32,512]{2,1,0:T(8,128)(2,1)S(1)} async-done(((bf16[8,32,512]{2,1,0:T(8,128)(2,1)}), bf16[8,32,512]{2,1,0:T(8,128)(2,1)S(1)}, u32[]{:S(2)}, u32[]{:S(2)}) %all-to-all-start.3) | async-done | bytes 262176 | tf_op jit(solution)/shard_map/all_to_all | solution.py:432
  67.2 0.1 collective-permute-start.7
  67.3 1.3 %collective-permute-done.7.got_ref = bf16[2,2,32,512]{3,2,1,0:T(8,128)(2,1)S(1)} collective-permute-done((bf16[2,2,32,512]{3,2,1,0:T(8,128)(2,1)S(1)}, bf16[2,2,32,512]{3,2,1,0:T(8,128)(2,1)S(1)}, u32[]{:S(2)}, u32[]{:S(2)}) %collective-permute-start.7) | collective-permute-done | bytes 131104 | tf_op jit(solution)/shard_map/ppermute | solution.py:529
  68.6 5.2 %collective-permute-done.8.light_far_ref = bf16[256,1024]{1,0:T(8,128)(2,1)S(1)} collective-permute-done((bf16[256,1024]{1,0:T(8,128)(2,1)}, bf16[256,1024]{1,0:T(8,128)(2,1)S(1)}, u32[]{:S(2)}, u32[]{:S(2)}) %collective-permute-start.8) | collective-permute-done | bytes 524320 | tf_op jit(solution)/shard_map/ppermute | solution.py:518
  73.8 1.6 %collective-permute-start.9 = (bf16[2,32,512]{2,1,0:T(8,128)(2,1)S(1)}, bf16[2,32,512]{2,1,0:T(8,128)(2,1)S(1)}, u32[]{:S(2)}, u32[]{:S(2)}) collective-permute-start(bf16[2,32,512]{2,1,0:T(8,128)(2,1)S(1)} %shard_map.93), channel_id=1, source_target_pairs={{0,2},{1,3},{2,0},{3,1},{4,6},{5,7},{6,4},{7,5},{8,10},{9,11},{10,... | collective-permute-start | bytes 196616 | tf_op jit(solution)/shard_map/ppermute | solution.py:532
  75.4 2.7 %collective-permute-done.9.last_ref = bf16[2,32,512]{2,1,0:T(8,128)(2,1)S(1)} collective-permute-done((bf16[2,32,512]{2,1,0:T(8,128)(2,1)S(1)}, bf16[2,32,512]{2,1,0:T(8,128)(2,1)S(1)}, u32[]{:S(2)}, u32[]{:S(2)}) %collective-permute-start.9) | collective-permute-done | bytes 65568 | tf_op jit(solution)/shard_map/ppermute | solution.py:532
  78.1 0.0 copy-done.2
  78.1 1.3 %shard_map.94 = bf16[256,1024]{1,0:T(8,128)(2,1)} custom-call(f32[256,1024]{1,0:T(8,128)S(1)} %copy-done.2, bf16[256,1024]{1,0:T(8,128)(2,1)S(1)} %collective-permute-done.8.light_far_ref, bf16[8,32,512]{2,1,0:T(8,128)(2,1)S(1)} %all-to-all-done.3.back_ref, bf16[2,2,32,512]{3,2,1,0:T(8,128)(2,1)S(1)} %collective-permute-done.7.got_ref, ...), custom_call_target="tpu_custom_call" | custom-call | tf_op jit(solution)/shard_map/pallas_call | solution.py:123
  (3 shorter events, 0.0 us)
Async XLA Ops:
  0.0 5.7 %collective-permute-start.1 = (bf16[256,1024]{1,0:T(8,128)(2,1)}, bf16[256,1024]{1,0:T(8,128)(2,1)}, u32[]{:S(2)}, u32[]{:S(2)}) collective-permute-start(bf16[256,1024]{1,0:T(8,128)(2,1)} %refs_0_), channel_id=1, source_target_pairs={{0,1},{1,0},{2,3},{3,2},{4,5},{5,4},{6,7},{7,6},{8,9},{9,8},{10,11... | collective-permute-start | bytes 1572872 | tf_op jit(solution)/shard_map/ppermute | solution.py:459
  1.9 3.1 %collective-permute-start = (bf16[32,1024]{1,0:T(8,128)(2,1)S(1)}, bf16[32,1024]{1,0:T(8,128)(2,1)S(1)}, u32[]{:S(2)}, u32[]{:S(2)}) collective-permute-start(bf16[32,1024]{1,0:T(8,128)(2,1)S(1)} %get-tuple-element.34), channel_id=1, source_target_pairs={{0,1},{1,0},{2,3},{3,2},{4,5},{5,4},{6,7},{7,6},{8,9},{9,8},{10,11... | collective-permute-start | bytes 196616 | tf_op jit(solution)/shard_map/ppermute | solution.py:456
  2.0 15.4 %collective-permute-start.2 = (bf16[256,1024]{1,0:T(8,128)(2,1)}, bf16[256,1024]{1,0:T(8,128)(2,1)}, u32[]{:S(2)}, u32[]{:S(2)}) collective-permute-start(bf16[256,1024]{1,0:T(8,128)(2,1)} %refs_0_), channel_id=1, source_target_pairs={{0,2},{1,3},{2,0},{3,1},{4,6},{5,7},{6,4},{7,5},{8,10},{9,11},{10,... | collective-permute-start | bytes 1572872 | tf_op jit(solution)/shard_map/ppermute | solution.py:458
  5.7 13.1 %all-to-all-start = ((bf16[8,32,512]{2,1,0:T(8,128)(2,1)}), bf16[8,32,512]{2,1,0:T(8,128)(2,1)S(1)}, u32[]{:S(2)}, u32[]{:S(2)}) async-start(bf16[8,32,512]{2,1,0:T(8,128)(2,1)} %shard_map.83), calls=%async_computation | async-start | bytes 524288 | tf_op jit(solution)/shard_map/all_to_all | solution.py:432
  12.1 13.5 %copy-start = (bf16[3,512,1024]{2,1,0:T(8,128)(2,1)S(1)}, bf16[3,512,1024]{2,1,0:T(8,128)(2,1)}, u32[]{:S(2)}) copy-start(bf16[3,512,1024]{2,1,0:T(8,128)(2,1)} %weight_ref.2) | copy-start | bytes 9437188
  18.8 8.3 %collective-permute-start.5 = (bf16[256,1024]{1,0:T(8,128)(2,1)}, bf16[256,1024]{1,0:T(8,128)(2,1)}, u32[]{:S(2)}, u32[]{:S(2)}) collective-permute-start(bf16[256,1024]{1,0:T(8,128)(2,1)} %collective-permute-done.2.refs_0_), channel_id=1, source_target_pairs={{0,1},{1,0},{2,3},{3,2},{4,5},{5,4},{6,7},{7,6},{8,9},{9,8},{10,11... | collective-permute-start | bytes 1572872 | tf_op jit(solution)/shard_map/ppermute | solution.py:470
  18.9 5.4 %collective-permute-start.3 = (bf16[64,512]{1,0:T(8,128)(2,1)S(1)}, bf16[64,512]{1,0:T(8,128)(2,1)S(1)}, u32[]{:S(2)}, u32[]{:S(2)}) collective-permute-start(bf16[64,512]{1,0:T(8,128)(2,1)S(1)} %shard_map.85.mine_ref), channel_id=1, source_target_pairs={{0,2},{1,3},{4,6},{5,7},{8,10},{9,11},{12,14},{13,15},{18,16},{19,... | collective-permute-start | bytes 196616 | tf_op jit(solution)/shard_map/ppermute | solution.py:479
  24.3 1.3 %collective-permute-start.4 = (bf16[64,512]{1,0:T(8,128)(2,1)S(1)}, bf16[64,512]{1,0:T(8,128)(2,1)S(1)}, u32[]{:S(2)}, u32[]{:S(2)}) collective-permute-start(bf16[64,512]{1,0:T(8,128)(2,1)S(1)} %shard_map.86.mine_ref), channel_id=1, source_target_pairs={{0,1},{1,0},{2,3},{3,2},{4,5},{5,4},{6,7},{7,6},{8,9},{9,8},{10,11... | collective-permute-start | bytes 196616 | tf_op jit(solution)/shard_map/ppermute | solution.py:481
  27.0 15.8 %all-to-all-start.1 = ((bf16[8,3,64,128]{3,2,1,0:T(8,128)(2,1)}), bf16[8,3,64,128]{3,2,1,0:T(8,128)(2,1)S(1)}, u32[]{:S(2)}, u32[]{:S(2)}) async-start(bf16[8,3,64,128]{3,2,1,0:T(8,128)(2,1)} %shard_map.87), calls=%async_computation.1 | async-start | bytes 786432 | tf_op jit(solution)/shard_map/all_to_all | solution.py:432
  40.2 13.9 %copy-start.1 = (bf16[1024,512]{1,0:T(8,128)(2,1)S(1)}, bf16[1024,512]{1,0:T(8,128)(2,1)}, u32[]{:S(2)}) copy-start(bf16[1024,512]{1,0:T(8,128)(2,1)} %weight_ref.3) | copy-start | bytes 3145732
  42.9 6.3 %collective-permute-start.6 = (bf16[2,256,1024]{2,1,0:T(8,128)(2,1)}, bf16[2,256,1024]{2,1,0:T(8,128)(2,1)S(1)}, u32[]{:S(2)}, u32[]{:S(2)}) collective-permute-start(bf16[2,256,1024]{2,1,0:T(8,128)(2,1)} %get-tuple-element.49), channel_id=1, source_target_pairs={{0,1},{1,0},{2,3},{3,2},{4,5},{5,4},{6,7},{7,6},{8,9},{9,8},{10,11... | collective-permute-start | bytes 3145736 | tf_op jit(solution)/shard_map/ppermute | solution.py:504
  43.9 10.2 %all-to-all-start.2 = ((bf16[8,64,128]{2,1,0:T(8,128)(2,1)}), bf16[8,64,128]{2,1,0:T(8,128)(2,1)S(1)}, u32[]{:S(2)}, u32[]{:S(2)}) async-start(bf16[8,64,128]{2,1,0:T(8,128)(2,1)} %shard_map.89), calls=%async_computation.2 | async-start | bytes 262144 | tf_op jit(solution)/shard_map/all_to_all | solution.py:432
  49.2 0.9 %copy-start.3 = (bf16[256,256]{1,0:T(8,128)(2,1)S(1)}, bf16[256,256]{1,0:T(8,128)(2,1)}, u32[]{:S(2)}) copy-start(bf16[256,256]{1,0:T(8,128)(2,1)} %get-tuple-element.50.heads_ref) | copy-start | bytes 393220
  52.6 25.5 %copy-start.2 = (f32[256,1024]{1,0:T(8,128)S(1)}, f32[256,1024]{1,0:T(8,128)}, u32[]{:S(2)}) copy-start(f32[256,1024]{1,0:T(8,128)} %get-tuple-element.53.light_ref) | copy-start | bytes 3145732
  55.3 11.9 %all-to-all-start.3 = ((bf16[8,32,512]{2,1,0:T(8,128)(2,1)}), bf16[8,32,512]{2,1,0:T(8,128)(2,1)S(1)}, u32[]{:S(2)}, u32[]{:S(2)}) async-start(bf16[8,32,512]{2,1,0:T(8,128)(2,1)} %shard_map.91), calls=%async_computation.3 | async-start | bytes 524288 | tf_op jit(solution)/shard_map/all_to_all | solution.py:432
  60.8 13.0 %collective-permute-start.8 = (bf16[256,1024]{1,0:T(8,128)(2,1)}, bf16[256,1024]{1,0:T(8,128)(2,1)S(1)}, u32[]{:S(2)}, u32[]{:S(2)}) collective-permute-start(bf16[256,1024]{1,0:T(8,128)(2,1)} %get-tuple-element.56), channel_id=1, source_target_pairs={{0,2},{1,3},{2,0},{3,1},{4,6},{5,7},{6,4},{7,5},{8,10},{9,11},{10,... | collective-permute-start | bytes 1572872 | tf_op jit(solution)/shard_map/ppermute | solution.py:518
  67.2 1.4 %collective-permute-start.7 = (bf16[2,2,32,512]{3,2,1,0:T(8,128)(2,1)S(1)}, bf16[2,2,32,512]{3,2,1,0:T(8,128)(2,1)S(1)}, u32[]{:S(2)}, u32[]{:S(2)}) collective-permute-start(bf16[2,2,32,512]{3,2,1,0:T(8,128)(2,1)S(1)} %shard_map.92), channel_id=1, source_target_pairs={{0,1},{1,0},{2,3},{3,2},{4,5},{5,4},{6,7},{7,6},{8,9},{9,8},{10,11... | collective-permute-start | bytes 393224 | tf_op jit(solution)/shard_map/ppermute | solution.py:529
  73.8 4.3 %collective-permute-start.9 = (bf16[2,32,512]{2,1,0:T(8,128)(2,1)S(1)}, bf16[2,32,512]{2,1,0:T(8,128)(2,1)S(1)}, u32[]{:S(2)}, u32[]{:S(2)}) collective-permute-start(bf16[2,32,512]{2,1,0:T(8,128)(2,1)S(1)} %shard_map.93), channel_id=1, source_target_pairs={{0,2},{1,3},{2,0},{3,1},{4,6},{5,7},{6,4},{7,5},{8,10},{9,11},{10,... | collective-permute-start | bytes 196616 | tf_op jit(solution)/shard_map/ppermute | solution.py:532

commit v7 on v6

--- a/solution.py
+++ b/solution.py
@@ -525,10 +525,10 @@
         query_map,
     )
     back = swap(back)
+    back, light_far = lax.optimization_barrier((back, light_far))
     give = on_chip(give_kernel, [((2, per, slots, out_cols), BF)], back)
     got = lax.ppermute(give, "head", pair)
     far = on_chip(far_kernel, [((per, slots, out_cols), BF)], back, got)
-    far, light_far = lax.optimization_barrier((far, light_far))
     last = lax.ppermute(far, "head", across)
     return on_chip(
         finish_kernel,

time: 79.9 us -> 74.9 us (0.937)
  blocking collectives: 0 us -> 10.7 us
  waiting for transfers between devices: 23.2 us -> 13.7 us
  starting transfers between devices: 33.8 us -> 28.3 us
    all_to_all x0 -> x1, blocking collectives: none -> 10.7 us  [swap(): lax.all_to_all(x, 'seq', split_axis=0, concat_axis=0, tiled=True, axis_in...]
    all_to_all x4 -> x3, starting transfers between devices: 23.6 us -> 18 us  [swap(): lax.all_to_all(x, 'seq', split_axis=0, concat_axis=0, tiled=True, axis_in...]
    all_to_all x4 -> x3, waiting for transfers between devices: 10.3 us -> 5.46 us  [swap(): lax.all_to_all(x, 'seq', split_axis=0, concat_axis=0, tiled=True, axis_in...]
    ppermute x1, waiting for transfers between devices: 5.18 us -> 0.5 us  [one_head_a_device(): light_far = lax.ppermute(light_far, 'head', across)]
  transfers between devices with their start and end apart: 14 -> 13, of which waited for: 10 -> 9; matrix products, arithmetic and copies ran while one was open for 0% -> 0% of each run, Pallas kernels for 24% -> 26%
where the time goes in v7:
time: 74.9 us; the launch traced here: 74.4 us
  starting transfers between devices  28.3 us (38%)
  Pallas kernels  20.7 us (28%)
  waiting for transfers between devices  13.7 us (18%)
  blocking collectives  10.7 us (14%)
  local copies, waits for them, and re-layouts  0.92 us (1%)
    pallas_call x13, Pallas kernels, on_chip(): pl.pallas_call(kernel, in_specs=[pl.BlockSpec(memory_space=pl.ANY)] * len...  20.7 us
    all_to_all x3, starting transfers between devices, swap(): lax.all_to_all(x, 'seq', split_axis=0, concat_axis=0, tiled=True, axis_in...  18 us
    all_to_all x1, blocking collectives, swap(): lax.all_to_all(x, 'seq', split_axis=0, concat_axis=0, tiled=True, axis_in...  10.7 us
    all_to_all x3, waiting for transfers between devices, swap(): lax.all_to_all(x, 'seq', split_axis=0, concat_axis=0, tiled=True, axis_in...  5.46 us
    ppermute x1, starting transfers between devices, one_head_a_device(): crossed = lax.ppermute(mine, ('seq', 'head'), holds)  3.36 us
    ppermute x1, starting transfers between devices, one_head_a_device(): token_far = lax.ppermute(tokens, 'head', across)  2.94 us
    ppermute x1, waiting for transfers between devices, one_head_a_device(): last = lax.ppermute(far, 'head', across)  2.68 us
    ppermute x1, waiting for transfers between devices, one_head_a_device(): crossed = lax.ppermute(mine, ('seq', 'head'), holds)  2 us
  transfers between devices with their start and end apart: 13, of which 9 were waited for; matrix products, arithmetic and copies ran while one was open for 0% of the time, Pallas kernels for 26%

profile of v7, /device:TPU:0, one launch (start us, length us, event | category | flops | bytes accessed | tf_op | source)
XLA Modules:
  0.0 74.4 jit_solution(6992243146046350204)
XLA Ops:
  0.0 0.5 collective-permute-start.1
  0.5 1.4 %shard_map.82 = (bf16[32,1024]{1,0:T(8,128)(2,1)S(1)}, bf16[32,1024]{1,0:T(8,128)(2,1)S(1)}, bf16[64,256]{1,0:T(8,128)(2,1)S(1)}, bf16[64,256]{1,0:T(8,128)(2,1)...) custom-call(bf16[256,1024]{1,0:T(8,128)(2,1)} %refs_0_, s32[8,32]{1,0:T(8,128)} %query_hbm.1, ...), custom_call_target="tpu_custom_call" | custom-call | tf_op jit(solution)/shard_map/pallas_call | solution.py:123
  1.9 0.1 collective-permute-start
  2.0 2.9 %collective-permute-start.2 = (bf16[256,1024]{1,0:T(8,128)(2,1)}, bf16[256,1024]{1,0:T(8,128)(2,1)}, u32[]{:S(2)}, u32[]{:S(2)}) collective-permute-start(bf16[256,1024]{1,0:T(8,128)(2,1)} %refs_0_), channel_id=1, source_target_pairs={{0,2},{1,3},{2,0},{3,1},{4,6},{5,7},{6,4},{7,5},{8,10},{9,11},{10,... | collective-permute-start | bytes 1572872 | tf_op jit(solution)/shard_map/ppermute | solution.py:458
  5.0 0.0 collective-permute-done.got_ref
  5.0 0.7 shard_map.83
  5.7 0.0 collective-permute-done.1.refs_1_
  5.7 6.4 %all-to-all-start = ((bf16[8,32,512]{2,1,0:T(8,128)(2,1)}), bf16[8,32,512]{2,1,0:T(8,128)(2,1)S(1)}, u32[]{:S(2)}, u32[]{:S(2)}) async-start(bf16[8,32,512]{2,1,0:T(8,128)(2,1)} %shard_map.83), calls=%async_computation | async-start | bytes 524288 | tf_op jit(solution)/shard_map/all_to_all | solution.py:432
  12.1 0.0 copy-start
  12.1 4.8 %shard_map.84.refs_3_ = f32[3,256,256]{2,1,0:T(8,128)} custom-call(bf16[256,1024]{1,0:T(8,128)(2,1)} %refs_0_, bf16[256,1024]{1,0:T(8,128)(2,1)} %collective-permute-done.1.refs_1_, bf16[3,4096,256]{2,1,0:T(8,128)(2,1)} %refs_2_.3), custom_call_target="tpu_custom_call" | custom-call | flops 805306368 | tf_op jit(solution)/shard_map/pallas_call | solution.py:123
  16.9 0.5 collective-permute-done.2.refs_0_
  17.4 1.3 %all-to-all-done.slots_ref = bf16[8,32,512]{2,1,0:T(8,128)(2,1)S(1)} async-done(((bf16[8,32,512]{2,1,0:T(8,128)(2,1)}), bf16[8,32,512]{2,1,0:T(8,128)(2,1)S(1)}, u32[]{:S(2)}, u32[]{:S(2)}) %all-to-all-start) | async-done | bytes 262176 | tf_op jit(solution)/shard_map/all_to_all | solution.py:432
  18.8 0.0 collective-permute-start.5
  18.8 0.2 shard_map.85.mine_ref
  18.9 3.4 %collective-permute-start.3 = (bf16[64,512]{1,0:T(8,128)(2,1)S(1)}, bf16[64,512]{1,0:T(8,128)(2,1)S(1)}, u32[]{:S(2)}, u32[]{:S(2)}) collective-permute-start(bf16[64,512]{1,0:T(8,128)(2,1)S(1)} %shard_map.85.mine_ref), channel_id=1, source_target_pairs={{0,2},{1,3},{4,6},{5,7},{8,10},{9,11},{12,14},{13,15},{18,16},{19,... | collective-permute-start | bytes 196616 | tf_op jit(solution)/shard_map/ppermute | solution.py:479
  22.3 2.0 %collective-permute-done.3.crossed_ref = bf16[64,512]{1,0:T(8,128)(2,1)S(1)} collective-permute-done((bf16[64,512]{1,0:T(8,128)(2,1)S(1)}, bf16[64,512]{1,0:T(8,128)(2,1)S(1)}, u32[]{:S(2)}, u32[]{:S(2)}) %collective-permute-start.3) | collective-permute-done | bytes 65568 | tf_op jit(solution)/shard_map/ppermute | solution.py:479
  24.3 0.1 collective-permute-start.4
  24.4 1.2 %collective-permute-done.4.other_ref = bf16[64,512]{1,0:T(8,128)(2,1)S(1)} collective-permute-done((bf16[64,512]{1,0:T(8,128)(2,1)S(1)}, bf16[64,512]{1,0:T(8,128)(2,1)S(1)}, u32[]{:S(2)}, u32[]{:S(2)}) %collective-permute-start.4) | collective-permute-done | bytes 65568 | tf_op jit(solution)/shard_map/ppermute | solution.py:481
  25.6 0.0 copy-done
  25.6 1.4 %shard_map.87 = bf16[8,3,64,128]{3,2,1,0:T(8,128)(2,1)} custom-call(bf16[64,512]{1,0:T(8,128)(2,1)S(1)} %shard_map.86.mine_ref, bf16[64,512]{1,0:T(8,128)(2,1)S(1)} %collective-permute-done.4.other_ref, bf16[3,512,1024]{2,1,0:T(8,128)(2,1)S(1)} %copy-done), custom_call_target="tpu_custom_call" | custom-call | tf_op jit(solution)/shard_map/pallas_call | solution.py:123
  27.0 0.0 collective-permute-done.5.refs_1_
  27.0 6.4 %all-to-all-start.1 = ((bf16[8,3,64,128]{3,2,1,0:T(8,128)(2,1)}), bf16[8,3,64,128]{3,2,1,0:T(8,128)(2,1)S(1)}, u32[]{:S(2)}, u32[]{:S(2)}) async-start(bf16[8,3,64,128]{3,2,1,0:T(8,128)(2,1)} %shard_map.87), calls=%async_computation.1 | async-start | bytes 786432 | tf_op jit(solution)/shard_map/all_to_all | solution.py:432
  33.4 6.8 %shard_map.88 = (bf16[256,256]{1,0:T(8,128)(2,1)}, bf16[2,256,1024]{2,1,0:T(8,128)(2,1)}) custom-call(bf16[256,1024]{1,0:T(8,128)(2,1)} %collective-permute-done.2.refs_0_, bf16[256,1024]{1,0:T(8,128)(2,1)} %collective-permute-done.5.refs_1_, bf16[3,4096,256]{2,1,0:T(8,128)(2,1)} %refs_2_.3, f32[3,256,256]{2,1,0:T(8,128)} %shard_map.84.refs_3_, ...), custom_call_target="tpu_custom_call" | custom-call | flops 805306368 | tf_op jit(solution)/shard_map/pallas_call | solution.py:123
  40.2 0.0 copy-start.1
  40.2 2.7 %all-to-all-done.1.parts_ref = bf16[8,3,64,128]{3,2,1,0:T(8,128)(2,1)S(1)} async-done(((bf16[8,3,64,128]{3,2,1,0:T(8,128)(2,1)}), bf16[8,3,64,128]{3,2,1,0:T(8,128)(2,1)S(1)}, u32[]{:S(2)}, u32[]{:S(2)}) %all-to-all-start.1) | async-done | bytes 393248 | tf_op jit(solution)/shard_map/all_to_all | solution.py:432
  42.9 0.0 collective-permute-start.6
  42.9 1.0 %shard_map.89 = bf16[8,64,128]{2,1,0:T(8,128)(2,1)} custom-call(bf16[8,3,64,128]{3,2,1,0:T(8,128)(2,1)S(1)} %all-to-all-done.1.parts_ref), custom_call_target="tpu_custom_call" | custom-call | tf_op jit(solution)/shard_map/pallas_call | solution.py:123
  43.9 5.3 %all-to-all-start.2 = ((bf16[8,64,128]{2,1,0:T(8,128)(2,1)}), bf16[8,64,128]{2,1,0:T(8,128)(2,1)S(1)}, u32[]{:S(2)}, u32[]{:S(2)}) async-start(bf16[8,64,128]{2,1,0:T(8,128)(2,1)} %shard_map.89), calls=%async_computation.2 | async-start | bytes 262144 | tf_op jit(solution)/shard_map/all_to_all | solution.py:432
  49.2 0.0 collective-permute-done.6.got_ref
  49.2 0.0 copy-start.3
  49.2 0.9 %copy-done.3 = bf16[256,256]{1,0:T(8,128)(2,1)S(1)} copy-done((bf16[256,256]{1,0:T(8,128)(2,1)S(1)}, bf16[256,256]{1,0:T(8,128)(2,1)}, u32[]{:S(2)}) %copy-start.3) | copy-done | bytes 131096
  50.1 2.5 %shard_map.90 = (f32[256,1024]{1,0:T(8,128)}, bf16[256,1024]{1,0:T(8,128)(2,1)}) custom-call(bf16[256,4096]{1,0:T(8,128)(2,1)} %w_out.1, bf16[2,256,1024]{2,1,0:T(8,128)(2,1)S(1)} %collective-permute-done.6.got_ref, bf16[256,256]{1,0:T(8,128)(2,1)S(1)} %copy-done.3), custom_call_target="tpu_custom_call" | custom-call | flops 268435456 | tf_op jit(solution)/shard_map/pallas_call | solution.py:123
  52.6 0.0 copy-start.2
  52.6 1.4 %all-to-all-done.2.heads_ref = bf16[8,64,128]{2,1,0:T(8,128)(2,1)S(1)} async-done(((bf16[8,64,128]{2,1,0:T(8,128)(2,1)}), bf16[8,64,128]{2,1,0:T(8,128)(2,1)S(1)}, u32[]{:S(2)}, u32[]{:S(2)}) %all-to-all-start.2) | async-done | bytes 131104 | tf_op jit(solution)/shard_map/all_to_all | solution.py:432
  54.1 1.6 %collective-permute-start.7 = (bf16[256,1024]{1,0:T(8,128)(2,1)}, bf16[256,1024]{1,0:T(8,128)(2,1)S(1)}, u32[]{:S(2)}, u32[]{:S(2)}) collective-permute-start(bf16[256,1024]{1,0:T(8,128)(2,1)} %get-tuple-element.56), channel_id=1, source_target_pairs={{0,2},{1,3},{2,0},{3,1},{4,6},{5,7},{6,4},{7,5},{8,10},{9,11},{10,... | collective-permute-start | bytes 1572872 | tf_op jit(solution)/shard_map/ppermute | solution.py:518
  55.7 0.0 copy-done.1
  55.7 0.5 shard_map.91
  56.2 10.7 %all_to_all.20.back_ref = bf16[8,32,512]{2,1,0:T(8,128)(2,1)S(1)} all-to-all(bf16[8,32,512]{2,1,0:T(8,128)(2,1)S(1)} %shard_map.91), channel_id=1, replica_groups={{12,8,20,16,4,0,28,24},{13,9,21,17,5,1,29,25},{14,10,22,18,6,2,30,26},{..., dimensions={0} | all-to-all | bytes 524288 | tf_op jit(solution)/shard_map/all_to_all | solution.py:432
  66.9 0.5 collective-permute-done.7.light_far_ref
  67.4 0.1 collective-permute-start.8
  67.5 1.3 %collective-permute-done.8.got_ref = bf16[2,2,32,512]{3,2,1,0:T(8,128)(2,1)S(1)} collective-permute-done((bf16[2,2,32,512]{3,2,1,0:T(8,128)(2,1)S(1)}, bf16[2,2,32,512]{3,2,1,0:T(8,128)(2,1)S(1)}, u32[]{:S(2)}, u32[]{:S(2)}) %collective-permute-start.8) | collective-permute-done | bytes 131104 | tf_op jit(solution)/shard_map/ppermute | solution.py:530
  68.8 1.7 %collective-permute-start.9 = (bf16[2,32,512]{2,1,0:T(8,128)(2,1)S(1)}, bf16[2,32,512]{2,1,0:T(8,128)(2,1)S(1)}, u32[]{:S(2)}, u32[]{:S(2)}) collective-permute-start(bf16[2,32,512]{2,1,0:T(8,128)(2,1)S(1)} %shard_map.93), channel_id=1, source_target_pairs={{0,2},{1,3},{2,0},{3,1},{4,6},{5,7},{6,4},{7,5},{8,10},{9,11},{10,... | collective-permute-start | bytes 196616 | tf_op jit(solution)/shard_map/ppermute | solution.py:532
  70.5 2.7 %collective-permute-done.9.last_ref = bf16[2,32,512]{2,1,0:T(8,128)(2,1)S(1)} collective-permute-done((bf16[2,32,512]{2,1,0:T(8,128)(2,1)S(1)}, bf16[2,32,512]{2,1,0:T(8,128)(2,1)S(1)}, u32[]{:S(2)}, u32[]{:S(2)}) %collective-permute-start.9) | collective-permute-done | bytes 65568 | tf_op jit(solution)/shard_map/ppermute | solution.py:532
  73.2 0.0 copy-done.2
  73.2 1.3 %shard_map.94 = bf16[256,1024]{1,0:T(8,128)(2,1)} custom-call(f32[256,1024]{1,0:T(8,128)S(1)} %copy-done.2, bf16[256,1024]{1,0:T(8,128)(2,1)S(1)} %collective-permute-done.7.light_far_ref, bf16[8,32,512]{2,1,0:T(8,128)(2,1)S(1)} %all_to_all.20.back_ref, bf16[2,2,32,512]{3,2,1,0:T(8,128)(2,1)S(1)} %collective-permute-done.8.got_ref, ...), custom_call_target="tpu_custom_call" | custom-call | tf_op jit(solution)/shard_map/pallas_call | solution.py:123
  (3 shorter events, 0.0 us)
Async XLA Ops:
  0.0 5.7 %collective-permute-start.1 = (bf16[256,1024]{1,0:T(8,128)(2,1)}, bf16[256,1024]{1,0:T(8,128)(2,1)}, u32[]{:S(2)}, u32[]{:S(2)}) collective-permute-start(bf16[256,1024]{1,0:T(8,128)(2,1)} %refs_0_), channel_id=1, source_target_pairs={{0,1},{1,0},{2,3},{3,2},{4,5},{5,4},{6,7},{7,6},{8,9},{9,8},{10,11... | collective-permute-start | bytes 1572872 | tf_op jit(solution)/shard_map/ppermute | solution.py:459
  1.9 3.1 %collective-permute-start = (bf16[32,1024]{1,0:T(8,128)(2,1)S(1)}, bf16[32,1024]{1,0:T(8,128)(2,1)S(1)}, u32[]{:S(2)}, u32[]{:S(2)}) collective-permute-start(bf16[32,1024]{1,0:T(8,128)(2,1)S(1)} %get-tuple-element.34), channel_id=1, source_target_pairs={{0,1},{1,0},{2,3},{3,2},{4,5},{5,4},{6,7},{7,6},{8,9},{9,8},{10,11... | collective-permute-start | bytes 196616 | tf_op jit(solution)/shard_map/ppermute | solution.py:456
  2.0 15.4 %collective-permute-start.2 = (bf16[256,1024]{1,0:T(8,128)(2,1)}, bf16[256,1024]{1,0:T(8,128)(2,1)}, u32[]{:S(2)}, u32[]{:S(2)}) collective-permute-start(bf16[256,1024]{1,0:T(8,128)(2,1)} %refs_0_), channel_id=1, source_target_pairs={{0,2},{1,3},{2,0},{3,1},{4,6},{5,7},{6,4},{7,5},{8,10},{9,11},{10,... | collective-permute-start | bytes 1572872 | tf_op jit(solution)/shard_map/ppermute | solution.py:458
  5.7 13.1 %all-to-all-start = ((bf16[8,32,512]{2,1,0:T(8,128)(2,1)}), bf16[8,32,512]{2,1,0:T(8,128)(2,1)S(1)}, u32[]{:S(2)}, u32[]{:S(2)}) async-start(bf16[8,32,512]{2,1,0:T(8,128)(2,1)} %shard_map.83), calls=%async_computation | async-start | bytes 524288 | tf_op jit(solution)/shard_map/all_to_all | solution.py:432
  12.1 13.5 %copy-start = (bf16[3,512,1024]{2,1,0:T(8,128)(2,1)S(1)}, bf16[3,512,1024]{2,1,0:T(8,128)(2,1)}, u32[]{:S(2)}) copy-start(bf16[3,512,1024]{2,1,0:T(8,128)(2,1)} %weight_ref.2) | copy-start | bytes 9437188
  18.8 8.3 %collective-permute-start.5 = (bf16[256,1024]{1,0:T(8,128)(2,1)}, bf16[256,1024]{1,0:T(8,128)(2,1)}, u32[]{:S(2)}, u32[]{:S(2)}) collective-permute-start(bf16[256,1024]{1,0:T(8,128)(2,1)} %collective-permute-done.2.refs_0_), channel_id=1, source_target_pairs={{0,1},{1,0},{2,3},{3,2},{4,5},{5,4},{6,7},{7,6},{8,9},{9,8},{10,11... | collective-permute-start | bytes 1572872 | tf_op jit(solution)/shard_map/ppermute | solution.py:470
  18.9 5.4 %collective-permute-start.3 = (bf16[64,512]{1,0:T(8,128)(2,1)S(1)}, bf16[64,512]{1,0:T(8,128)(2,1)S(1)}, u32[]{:S(2)}, u32[]{:S(2)}) collective-permute-start(bf16[64,512]{1,0:T(8,128)(2,1)S(1)} %shard_map.85.mine_ref), channel_id=1, source_target_pairs={{0,2},{1,3},{4,6},{5,7},{8,10},{9,11},{12,14},{13,15},{18,16},{19,... | collective-permute-start | bytes 196616 | tf_op jit(solution)/shard_map/ppermute | solution.py:479
  24.3 1.3 %collective-permute-start.4 = (bf16[64,512]{1,0:T(8,128)(2,1)S(1)}, bf16[64,512]{1,0:T(8,128)(2,1)S(1)}, u32[]{:S(2)}, u32[]{:S(2)}) collective-permute-start(bf16[64,512]{1,0:T(8,128)(2,1)S(1)} %shard_map.86.mine_ref), channel_id=1, source_target_pairs={{0,1},{1,0},{2,3},{3,2},{4,5},{5,4},{6,7},{7,6},{8,9},{9,8},{10,11... | collective-permute-start | bytes 196616 | tf_op jit(solution)/shard_map/ppermute | solution.py:481
  27.0 15.8 %all-to-all-start.1 = ((bf16[8,3,64,128]{3,2,1,0:T(8,128)(2,1)}), bf16[8,3,64,128]{3,2,1,0:T(8,128)(2,1)S(1)}, u32[]{:S(2)}, u32[]{:S(2)}) async-start(bf16[8,3,64,128]{3,2,1,0:T(8,128)(2,1)} %shard_map.87), calls=%async_computation.1 | async-start | bytes 786432 | tf_op jit(solution)/shard_map/all_to_all | solution.py:432
  40.2 15.5 %copy-start.1 = (bf16[1024,512]{1,0:T(8,128)(2,1)S(1)}, bf16[1024,512]{1,0:T(8,128)(2,1)}, u32[]{:S(2)}) copy-start(bf16[1024,512]{1,0:T(8,128)(2,1)} %weight_ref.3) | copy-start | bytes 3145732
  42.9 6.3 %collective-permute-start.6 = (bf16[2,256,1024]{2,1,0:T(8,128)(2,1)}, bf16[2,256,1024]{2,1,0:T(8,128)(2,1)S(1)}, u32[]{:S(2)}, u32[]{:S(2)}) collective-permute-start(bf16[2,256,1024]{2,1,0:T(8,128)(2,1)} %get-tuple-element.49), channel_id=1, source_target_pairs={{0,1},{1,0},{2,3},{3,2},{4,5},{5,4},{6,7},{7,6},{8,9},{9,8},{10,11... | collective-permute-start | bytes 3145736 | tf_op jit(solution)/shard_map/ppermute | solution.py:504
  43.9 10.2 %all-to-all-start.2 = ((bf16[8,64,128]{2,1,0:T(8,128)(2,1)}), bf16[8,64,128]{2,1,0:T(8,128)(2,1)S(1)}, u32[]{:S(2)}, u32[]{:S(2)}) async-start(bf16[8,64,128]{2,1,0:T(8,128)(2,1)} %shard_map.89), calls=%async_computation.2 | async-start | bytes 262144 | tf_op jit(solution)/shard_map/all_to_all | solution.py:432
  49.2 0.9 %copy-start.3 = (bf16[256,256]{1,0:T(8,128)(2,1)S(1)}, bf16[256,256]{1,0:T(8,128)(2,1)}, u32[]{:S(2)}) copy-start(bf16[256,256]{1,0:T(8,128)(2,1)} %get-tuple-element.50.heads_ref) | copy-start | bytes 393220
  52.6 20.5 %copy-start.2 = (f32[256,1024]{1,0:T(8,128)S(1)}, f32[256,1024]{1,0:T(8,128)}, u32[]{:S(2)}) copy-start(f32[256,1024]{1,0:T(8,128)} %get-tuple-element.53.light_ref) | copy-start | bytes 3145732
  54.1 13.3 %collective-permute-start.7 = (bf16[256,1024]{1,0:T(8,128)(2,1)}, bf16[256,1024]{1,0:T(8,128)(2,1)S(1)}, u32[]{:S(2)}, u32[]{:S(2)}) collective-permute-start(bf16[256,1024]{1,0:T(8,128)(2,1)} %get-tuple-element.56), channel_id=1, source_target_pairs={{0,2},{1,3},{2,0},{3,1},{4,6},{5,7},{6,4},{7,5},{8,10},{9,11},{10,... | collective-permute-start | bytes 1572872 | tf_op jit(solution)/shard_map/ppermute | solution.py:518
  67.4 1.4 %collective-permute-start.8 = (bf16[2,2,32,512]{3,2,1,0:T(8,128)(2,1)S(1)}, bf16[2,2,32,512]{3,2,1,0:T(8,128)(2,1)S(1)}, u32[]{:S(2)}, u32[]{:S(2)}) collective-permute-start(bf16[2,2,32,512]{3,2,1,0:T(8,128)(2,1)S(1)} %shard_map.92), channel_id=1, source_target_pairs={{0,1},{1,0},{2,3},{3,2},{4,5},{5,4},{6,7},{7,6},{8,9},{9,8},{10,11... | collective-permute-start | bytes 393224 | tf_op jit(solution)/shard_map/ppermute | solution.py:530
  68.8 4.3 %collective-permute-start.9 = (bf16[2,32,512]{2,1,0:T(8,128)(2,1)S(1)}, bf16[2,32,512]{2,1,0:T(8,128)(2,1)S(1)}, u32[]{:S(2)}, u32[]{:S(2)}) collective-permute-start(bf16[2,32,512]{2,1,0:T(8,128)(2,1)S(1)} %shard_map.93), channel_id=1, source_target_pairs={{0,2},{1,3},{2,0},{3,1},{4,6},{5,7},{6,4},{7,5},{8,10},{9,11},{10,... | collective-permute-start | bytes 196616 | tf_op jit(solution)/shard_map/ppermute | solution.py:532

commit v8 on v7

--- a/solution.py
+++ b/solution.py
@@ -276,52 +276,69 @@
         out_ref[s] = result
 
 
-def heavy_output_kernel(heads_ref, weight_ref, chosen_ref, out_ref):
+def heavy_output_kernel(heads_ref, weight_ref, keep_ref, give_ref):
+    odd = lax.axis_index("head") % 2
     rows = jnp.concatenate([heads_ref[i] for i in spots(heads_ref.shape[0])], axis=1)
-    part = jnp.dot(rows, weight_ref[...], preferred_element_type=F32).astype(BF)
-    spread = lax.dot_general(chosen_ref[...], part, FIRST, preferred_element_type=F32).astype(BF)
-    out_ref[...] = spread.reshape(out_ref.shape)
+    part = jnp.dot(rows, weight_ref[...], preferred_element_type=F32)
+    width = keep_ref.shape[1]
+    low, high = part[:, :width], part[:, width:]
+    keep_ref[...] = jnp.where(odd == 0, low, high)
+    give_ref[...] = jnp.where(odd == 0, high, low).astype(BF)
+
+
+def return_kernel(keep_ref, got_ref, chosen_ref, out_ref):
+    rows = (keep_ref[...] + got_ref[...].astype(F32)).astype(BF)
+    spread = lax.dot_general(chosen_ref[...], rows, FIRST, preferred_element_type=F32).astype(BF)
+    shards, pairs, slots = out_ref.shape[:3]
+    for s in range(shards):
+        for k in range(pairs):
+            out_ref[s, k] = spread[s * slots : (s + 1) * slots]
 
 
 def block_of(back_ref, head, per, i):
-    spot = spots(back_ref.shape[0])
-    return back_ref[look_up(spot[i::per], head)]
+    at = look_up(spots(back_ref.shape[0])[i::per], head)
+    total = back_ref[at, 0].astype(F32)
+    for k in range(1, back_ref.shape[1]):
+        total = total + back_ref[at, k].astype(F32)
+    return total
 
 
 def give_kernel(back_ref, out_ref):
     head = lax.axis_index("head")
-    per = out_ref.shape[1]
-    for k, j in enumerate((1, 3)):
-        for i in range(per):
-            out_ref[k, i] = block_of(back_ref, head ^ j, per, i)
-
-
-def far_kernel(back_ref, got_ref, out_ref):
     per = out_ref.shape[0]
+    for i in range(per):
+        out_ref[i] = block_of(back_ref, head ^ 1, per, i).astype(BF)
+
+
+def merge_kernel(own, far, out_ref, far_ref, sems):
+    copies = [
+        pltpu.make_async_copy(own, out_ref, sems.at[0]),
+        pltpu.make_async_copy(far, far_ref, sems.at[1]),
+    ]
+    for copy in copies:
+        copy.start()
+    for copy in copies:
+        copy.wait()
+    out_ref[...] = out_ref[...] + far_ref[...].astype(F32)
+
+
+def finish_kernel(light_ref, back_ref, got_ref, own_map_ref, gate_ref, out_ref):
     head = lax.axis_index("head")
+    per, _, width = got_ref.shape
+    chosen, gate = own_map_ref[...], gate_ref[:, :1]
     for i in range(per):
-        mine = block_of(back_ref, head ^ 2, per, i).astype(F32)
-        out_ref[i] = (mine + got_ref[1, i].astype(F32)).astype(BF)
-
-
-def finish_kernel(
-    light_ref, light_far_ref, back_ref, got_ref, last_ref, own_map_ref, gate_ref, out_ref
-):
-    head = lax.axis_index("head")
-    per = last_ref.shape[0]
-    chosen, gate = own_map_ref[...], gate_ref[:, :1]
-    width = last_ref.shape[2]
-    for j in range(per):
-        mine = block_of(back_ref, head, per, j).astype(F32)
-        scaled = (mine + got_ref[0, j].astype(F32) + last_ref[j].astype(F32)) * gate
-        coarse = scaled.astype(BF)
-        fine = (scaled - coarse.astype(F32)).astype(BF)
-        added = jnp.dot(chosen, coarse, preferred_element_type=F32) + jnp.dot(
-            chosen, fine, preferred_element_type=F32
-        )
-        cols = slice(j * width, (j + 1) * width)
-        light = light_ref[:, cols] + light_far_ref[:, cols].astype(F32)
-        out_ref[:, cols] = (light + added).astype(BF)
+        for half, heavy in (
+            (head % 2, block_of(back_ref, head, per, i)),
+            (1 - head % 2, got_ref[i].astype(F32)),
+        ):
+            scaled = heavy * gate
+            coarse = scaled.astype(BF)
+            fine = (scaled - coarse.astype(F32)).astype(BF)
+            added = jnp.dot(chosen, coarse, preferred_element_type=F32) + jnp.dot(
+                chosen, fine, preferred_element_type=F32
+            )
+            cols = pl.ds(pl.multiple_of((2 * i + half) * width, width), width)
+            out_ref[:, cols] = (light_ref[:, cols] + added).astype(BF)
 
 
 def light_kernel(flips, last, *refs):
@@ -517,27 +534,46 @@
     heads, light_own, light_far = lax.optimization_barrier((heads, light_own, light_far))
     light_far = lax.ppermute(light_far, "head", across)
 
-    back = on_chip(
+    half_cols = out_cols // 2
+    keep, give = on_chip(
         heavy_output_kernel,
-        [((seq_count, slots, out_cols), BF)],
+        [((routed, half_cols), F32), ((routed, half_cols), BF)],
         heads,
         heavy_output,
-        query_map,
-    )
-    back = swap(back)
+    )
+    got = lax.ppermute(give, "head", pair)
+    pairs = head_count // 2
+    back = on_chip(
+        return_kernel, [((seq_count, pairs, slots, half_cols), BF)], keep, got, query_map
+    )
+    groups = [
+        [s * head_count + 2 * k + c for s in listed(seq_count) for k in range(pairs)]
+        for c in range(2)
+    ]
+    back = lax.all_to_all(
+        back.reshape(-1, slots, half_cols),
+        ("seq", "head"),
+        split_axis=0,
+        concat_axis=0,
+        tiled=True,
+        axis_index_groups=groups,
+    ).reshape(back.shape)
     back, light_far = lax.optimization_barrier((back, light_far))
-    give = on_chip(give_kernel, [((2, per, slots, out_cols), BF)], back)
+    give = on_chip(give_kernel, [((per, slots, half_cols), BF)], back)
+    give, light_own, light_far = lax.optimization_barrier((give, light_own, light_far))
     got = lax.ppermute(give, "head", pair)
-    far = on_chip(far_kernel, [((per, slots, out_cols), BF)], back, got)
-    last = lax.ppermute(far, "head", across)
+    light = on_chip(
+        merge_kernel,
+        [((tok_rows, own_width), F32)],
+        hbm=(light_own, light_far),
+        scratch=[pltpu.VMEM((tok_rows, own_width), BF), pltpu.SemaphoreType.DMA((2,))],
+    )
     return on_chip(
         finish_kernel,
         [((tok_rows, own_width), BF)],
-        light_own,
-        light_far,
+        light,
         back,
         got,
-        last,
         own_map,
         gate_map,
         off=True,

time: 74.9 us -> 76.6 us (1.023)
  blocking collectives: 10.7 us -> 0 us
  waiting for transfers between devices: 13.7 us -> 19.8 us
  starting transfers between devices: 28.3 us -> 32.3 us
  Pallas kernels: 20.7 us -> 22.8 us
    all_to_all x1 -> x0, blocking collectives: 10.7 us -> none  [swap(): lax.all_to_all(x, 'seq', split_axis=0, concat_axis=0, tiled=True, axis_in...]
    ppermute x1, waiting for transfers between devices: 0.5 us -> 8.89 us  [one_head_a_device(): light_far = lax.ppermute(light_far, 'head', across)]
    all_to_all x0 -> x1, starting transfers between devices: none -> 5.56 us  [one_head_a_device(): lax.all_to_all(back.reshape(-1, slots, half_cols), ('seq', 'head'), split...]
    ppermute x1 -> x0, waiting for transfers between devices: 2.68 us -> none  [one_head_a_device(): last = lax.ppermute(far, 'head', across)]
    pallas_call x13 -> x14, Pallas kernels: 20.7 us -> 22.8 us  [on_chip(): pl.pallas_call(kernel, in_specs=[pl.BlockSpec(memory_space=pl.ANY)] * len...]
    ppermute x1 -> x0, starting transfers between devices: 1.65 us -> none  [one_head_a_device(): last = lax.ppermute(far, 'head', across)]
    all_to_all x0 -> x1, waiting for transfers between devices: none -> 1.61 us  [one_head_a_device(): lax.all_to_all(back.reshape(-1, slots, half_cols), ('seq', 'head'), split...]
    ppermute x1 -> x2, waiting for transfers between devices: 1.33 us -> 0.01 us  [one_head_a_device(): got = lax.ppermute(give, 'head', pair)]
  transfers between devices with their start and end apart: 13 -> 14, of which waited for: 9 -> 8; matrix products, arithmetic and copies ran while one was open for 0% -> 0% of each run, Pallas kernels for 26% -> 28%
where the time goes in v8:
time: 76.6 us; the launch traced here: 75.9 us
  starting transfers between devices  32.3 us (42%)
  Pallas kernels  22.8 us (30%)
  waiting for transfers between devices  19.8 us (26%)
  local copies, waits for them, and re-layouts  0.92 us (1%)
    pallas_call x14, Pallas kernels, on_chip(): pl.pallas_call(kernel, in_specs=[pl.BlockSpec(memory_space=pl.ANY)] * len...  22.8 us
    all_to_all x3, starting transfers between devices, swap(): lax.all_to_all(x, 'seq', split_axis=0, concat_axis=0, tiled=True, axis_in...  18 us
    ppermute x1, waiting for transfers between devices, one_head_a_device(): light_far = lax.ppermute(light_far, 'head', across)  8.89 us
    all_to_all x1, starting transfers between devices, one_head_a_device(): lax.all_to_all(back.reshape(-1, slots, half_cols), ('seq', 'head'), split...  5.56 us
    all_to_all x3, waiting for transfers between devices, swap(): lax.all_to_all(x, 'seq', split_axis=0, concat_axis=0, tiled=True, axis_in...  5.47 us
    ppermute x1, starting transfers between devices, one_head_a_device(): crossed = lax.ppermute(mine, ('seq', 'head'), holds)  3.36 us
    ppermute x1, starting transfers between devices, one_head_a_device(): token_far = lax.ppermute(tokens, 'head', across)  2.94 us
    ppermute x1, waiting for transfers between devices, one_head_a_device(): crossed = lax.ppermute(mine, ('seq', 'head'), holds)  2 us
  transfers between devices with their start and end apart: 14, of which 8 were waited for; matrix products, arithmetic and copies ran while one was open for 0% of the time, Pallas kernels for 28%

profile of v8, /device:TPU:0, one launch (start us, length us, event | category | flops | bytes accessed | tf_op | source)
XLA Modules:
  0.0 75.9 jit_solution(3693068112677867651)
XLA Ops:
  0.0 0.5 collective-permute-start.1
  0.5 1.4 %shard_map.82 = (bf16[32,1024]{1,0:T(8,128)(2,1)S(1)}, bf16[32,1024]{1,0:T(8,128)(2,1)S(1)}, bf16[64,256]{1,0:T(8,128)(2,1)S(1)}, bf16[64,256]{1,0:T(8,128)(2,1)...) custom-call(bf16[256,1024]{1,0:T(8,128)(2,1)} %refs_0_, s32[8,32]{1,0:T(8,128)} %query_hbm.1, ...), custom_call_target="tpu_custom_call" | custom-call | tf_op jit(solution)/shard_map/pallas_call | solution.py:123
  1.9 0.1 collective-permute-start
  2.0 2.9 %collective-permute-start.2 = (bf16[256,1024]{1,0:T(8,128)(2,1)}, bf16[256,1024]{1,0:T(8,128)(2,1)}, u32[]{:S(2)}, u32[]{:S(2)}) collective-permute-start(bf16[256,1024]{1,0:T(8,128)(2,1)} %refs_0_), channel_id=1, source_target_pairs={{0,2},{1,3},{2,0},{3,1},{4,6},{5,7},{6,4},{7,5},{8,10},{9,11},{10,... | collective-permute-start | bytes 1572872 | tf_op jit(solution)/shard_map/ppermute | solution.py:475
  5.0 0.0 collective-permute-done.got_ref
  5.0 0.7 shard_map.83
  5.7 0.0 collective-permute-done.1.refs_1_
  5.7 6.4 %all-to-all-start = ((bf16[8,32,512]{2,1,0:T(8,128)(2,1)}), bf16[8,32,512]{2,1,0:T(8,128)(2,1)S(1)}, u32[]{:S(2)}, u32[]{:S(2)}) async-start(bf16[8,32,512]{2,1,0:T(8,128)(2,1)} %shard_map.83), calls=%async_computation | async-start | bytes 524288 | tf_op jit(solution)/shard_map/all_to_all | solution.py:449
  12.1 0.0 copy-start
  12.1 4.8 %shard_map.84.refs_3_ = f32[3,256,256]{2,1,0:T(8,128)} custom-call(bf16[256,1024]{1,0:T(8,128)(2,1)} %refs_0_, bf16[256,1024]{1,0:T(8,128)(2,1)} %collective-permute-done.1.refs_1_, bf16[3,4096,256]{2,1,0:T(8,128)(2,1)} %refs_2_.3), custom_call_target="tpu_custom_call" | custom-call | flops 805306368 | tf_op jit(solution)/shard_map/pallas_call | solution.py:123
  16.9 0.5 collective-permute-done.2.refs_0_
  17.4 1.3 %all-to-all-done.slots_ref = bf16[8,32,512]{2,1,0:T(8,128)(2,1)S(1)} async-done(((bf16[8,32,512]{2,1,0:T(8,128)(2,1)}), bf16[8,32,512]{2,1,0:T(8,128)(2,1)S(1)}, u32[]{:S(2)}, u32[]{:S(2)}) %all-to-all-start) | async-done | bytes 262176 | tf_op jit(solution)/shard_map/all_to_all | solution.py:449
  18.8 0.0 collective-permute-start.5
  18.8 0.2 shard_map.85.mine_ref
  18.9 3.4 %collective-permute-start.3 = (bf16[64,512]{1,0:T(8,128)(2,1)S(1)}, bf16[64,512]{1,0:T(8,128)(2,1)S(1)}, u32[]{:S(2)}, u32[]{:S(2)}) collective-permute-start(bf16[64,512]{1,0:T(8,128)(2,1)S(1)} %shard_map.85.mine_ref), channel_id=1, source_target_pairs={{0,2},{1,3},{4,6},{5,7},{8,10},{9,11},{12,14},{13,15},{18,16},{19,... | collective-permute-start | bytes 196616 | tf_op jit(solution)/shard_map/ppermute | solution.py:496
  22.3 2.0 %collective-permute-done.3.crossed_ref = bf16[64,512]{1,0:T(8,128)(2,1)S(1)} collective-permute-done((bf16[64,512]{1,0:T(8,128)(2,1)S(1)}, bf16[64,512]{1,0:T(8,128)(2,1)S(1)}, u32[]{:S(2)}, u32[]{:S(2)}) %collective-permute-start.3) | collective-permute-done | bytes 65568 | tf_op jit(solution)/shard_map/ppermute | solution.py:496
  24.3 0.1 collective-permute-start.4
  24.4 1.2 %collective-permute-done.4.other_ref = bf16[64,512]{1,0:T(8,128)(2,1)S(1)} collective-permute-done((bf16[64,512]{1,0:T(8,128)(2,1)S(1)}, bf16[64,512]{1,0:T(8,128)(2,1)S(1)}, u32[]{:S(2)}, u32[]{:S(2)}) %collective-permute-start.4) | collective-permute-done | bytes 65568 | tf_op jit(solution)/shard_map/ppermute | solution.py:498
  25.6 0.0 copy-done
  25.6 1.4 %shard_map.87 = bf16[8,3,64,128]{3,2,1,0:T(8,128)(2,1)} custom-call(bf16[64,512]{1,0:T(8,128)(2,1)S(1)} %shard_map.86.mine_ref, bf16[64,512]{1,0:T(8,128)(2,1)S(1)} %collective-permute-done.4.other_ref, bf16[3,512,1024]{2,1,0:T(8,128)(2,1)S(1)} %copy-done), custom_call_target="tpu_custom_call" | custom-call | tf_op jit(solution)/shard_map/pallas_call | solution.py:123
  27.0 0.0 collective-permute-done.5.refs_1_
  27.0 6.4 %all-to-all-start.1 = ((bf16[8,3,64,128]{3,2,1,0:T(8,128)(2,1)}), bf16[8,3,64,128]{3,2,1,0:T(8,128)(2,1)S(1)}, u32[]{:S(2)}, u32[]{:S(2)}) async-start(bf16[8,3,64,128]{3,2,1,0:T(8,128)(2,1)} %shard_map.87), calls=%async_computation.1 | async-start | bytes 786432 | tf_op jit(solution)/shard_map/all_to_all | solution.py:449
  33.4 6.8 %shard_map.88 = (bf16[256,256]{1,0:T(8,128)(2,1)}, bf16[2,256,1024]{2,1,0:T(8,128)(2,1)}) custom-call(bf16[256,1024]{1,0:T(8,128)(2,1)} %collective-permute-done.2.refs_0_, bf16[256,1024]{1,0:T(8,128)(2,1)} %collective-permute-done.5.refs_1_, bf16[3,4096,256]{2,1,0:T(8,128)(2,1)} %refs_2_.3, f32[3,256,256]{2,1,0:T(8,128)} %shard_map.84.refs_3_, ...), custom_call_target="tpu_custom_call" | custom-call | flops 805306368 | tf_op jit(solution)/shard_map/pallas_call | solution.py:123
  40.2 0.0 copy-start.1
  40.2 2.7 %all-to-all-done.1.parts_ref = bf16[8,3,64,128]{3,2,1,0:T(8,128)(2,1)S(1)} async-done(((bf16[8,3,64,128]{3,2,1,0:T(8,128)(2,1)}), bf16[8,3,64,128]{3,2,1,0:T(8,128)(2,1)S(1)}, u32[]{:S(2)}, u32[]{:S(2)}) %all-to-all-start.1) | async-done | bytes 393248 | tf_op jit(solution)/shard_map/all_to_all | solution.py:449
  42.9 0.0 collective-permute-start.6
  42.9 1.0 %shard_map.89 = bf16[8,64,128]{2,1,0:T(8,128)(2,1)} custom-call(bf16[8,3,64,128]{3,2,1,0:T(8,128)(2,1)S(1)} %all-to-all-done.1.parts_ref), custom_call_target="tpu_custom_call" | custom-call | tf_op jit(solution)/shard_map/pallas_call | solution.py:123
  43.9 5.3 %all-to-all-start.2 = ((bf16[8,64,128]{2,1,0:T(8,128)(2,1)}), bf16[8,64,128]{2,1,0:T(8,128)(2,1)S(1)}, u32[]{:S(2)}, u32[]{:S(2)}) async-start(bf16[8,64,128]{2,1,0:T(8,128)(2,1)} %shard_map.89), calls=%async_computation.2 | async-start | bytes 262144 | tf_op jit(solution)/shard_map/all_to_all | solution.py:449
  49.2 0.0 collective-permute-done.6.got_ref
  49.2 0.0 copy-start.2
  49.2 0.9 %copy-done.2 = bf16[256,256]{1,0:T(8,128)(2,1)S(1)} copy-done((bf16[256,256]{1,0:T(8,128)(2,1)S(1)}, bf16[256,256]{1,0:T(8,128)(2,1)}, u32[]{:S(2)}) %copy-start.2) | copy-done | bytes 131096
  50.1 2.5 %shard_map.90 = (f32[256,1024]{1,0:T(8,128)}, bf16[256,1024]{1,0:T(8,128)(2,1)}) custom-call(bf16[256,4096]{1,0:T(8,128)(2,1)} %w_out.1, bf16[2,256,1024]{2,1,0:T(8,128)(2,1)S(1)} %collective-permute-done.6.got_ref, bf16[256,256]{1,0:T(8,128)(2,1)S(1)} %copy-done.2), custom_call_target="tpu_custom_call" | custom-call | flops 268435456 | tf_op jit(solution)/shard_map/pallas_call | solution.py:123
  52.6 1.5 %all-to-all-done.2.heads_ref = bf16[8,64,128]{2,1,0:T(8,128)(2,1)S(1)} async-done(((bf16[8,64,128]{2,1,0:T(8,128)(2,1)}), bf16[8,64,128]{2,1,0:T(8,128)(2,1)S(1)}, u32[]{:S(2)}, u32[]{:S(2)}) %all-to-all-start.2) | async-done | bytes 131104 | tf_op jit(solution)/shard_map/all_to_all | solution.py:449
  54.1 0.0 copy-done.1
  54.1 0.3 shard_map.91
  54.4 0.1 collective-permute-start.7
  54.5 1.7 %collective-permute-start.8 = (bf16[256,1024]{1,0:T(8,128)(2,1)}, bf16[256,1024]{1,0:T(8,128)(2,1)S(1)}, u32[]{:S(2)}, u32[]{:S(2)}) collective-permute-start(bf16[256,1024]{1,0:T(8,128)(2,1)} %get-tuple-element.62), channel_id=1, source_target_pairs={{0,2},{1,3},{2,0},{3,1},{4,6},{5,7},{6,4},{7,5},{8,10},{9,11},{10,... | collective-permute-start | bytes 1572872 | tf_op jit(solution)/shard_map/ppermute | solution.py:535
  56.1 0.0 collective-permute-done.7.got_ref
  56.1 0.9 %shard_map.92 = bf16[8,2,32,256]{3,2,1,0:T(8,128)(2,1)} custom-call(f32[64,256]{1,0:T(8,128)S(1)} %get-tuple-element.59.keep_ref, bf16[64,256]{1,0:T(8,128)(2,1)S(1)} %collective-permute-done.7.got_ref, bf16[64,256]{1,0:T(8,128)(2,1)S(1)} %get-tuple-element.61.chosen_ref), custom_call_target="tpu_custom_call" | custom-call | tf_op jit(solution)/shard_map/pallas_call | solution.py:123
  57.0 5.6 %all-to-all-start.3 = ((bf16[16,32,256]{2,1,0:T(8,128)(2,1)}), bf16[16,32,256]{2,1,0:T(8,128)(2,1)S(1)}, u32[]{:S(2)}, u32[]{:S(2)}) async-start(bf16[16,32,256]{2,1,0:T(8,128)(2,1)} %bitcast), calls=%async_computation.3 | async-start | bytes 524288 | tf_op jit(solution)/shard_map/all_to_all | solution.py:553
  62.6 8.9 %collective-permute-done.8.far = bf16[256,1024]{1,0:T(8,128)(2,1)S(1)} collective-permute-done((bf16[256,1024]{1,0:T(8,128)(2,1)}, bf16[256,1024]{1,0:T(8,128)(2,1)S(1)}, u32[]{:S(2)}, u32[]{:S(2)}) %collective-permute-start.8) | collective-permute-done | bytes 524320 | tf_op jit(solution)/shard_map/ppermute | solution.py:535
  71.5 0.0 copy-start.3
  71.5 1.6 %all-to-all-done.3 = bf16[16,32,256]{2,1,0:T(8,128)(2,1)S(1)} async-done(((bf16[16,32,256]{2,1,0:T(8,128)(2,1)}), bf16[16,32,256]{2,1,0:T(8,128)(2,1)S(1)}, u32[]{:S(2)}, u32[]{:S(2)}) %all-to-all-start.3) | async-done | bytes 262176 | tf_op jit(solution)/shard_map/all_to_all | solution.py:553
  73.1 0.1 collective-permute-start.9
  73.2 0.0 copy-done.3
  73.2 1.5 %shard_map.94.light_ref = f32[256,1024]{1,0:T(8,128)S(1)} custom-call(f32[256,1024]{1,0:T(8,128)} %get-tuple-element.66.own, bf16[256,1024]{1,0:T(8,128)(2,1)} %copy-done.3), custom_call_target="tpu_custom_call" | custom-call | tf_op jit(solution)/shard_map/pallas_call | solution.py:123
  74.6 0.0 collective-permute-done.9.got_ref
  74.7 1.3 %shard_map.95 = bf16[256,1024]{1,0:T(8,128)(2,1)} custom-call(f32[256,1024]{1,0:T(8,128)S(1)} %shard_map.94.light_ref, bf16[8,2,32,256]{3,2,1,0:T(8,128)(2,1)S(1)} %bitcast.3, bf16[2,32,256]{2,1,0:T(8,128)(2,1)S(1)} %collective-permute-done.9.got_ref, bf16[256,32]{1,0:T(8,128)(2,1)S(1)} %get-tuple-element.69.own_map_ref, ...), custom_call_target="tpu_custom_call" | custom-call | tf_op jit(solution)/shard_map/pallas_call | solution.py:123
  (2 shorter events, 0.0 us)
Async XLA Ops:
  0.0 5.7 %collective-permute-start.1 = (bf16[256,1024]{1,0:T(8,128)(2,1)}, bf16[256,1024]{1,0:T(8,128)(2,1)}, u32[]{:S(2)}, u32[]{:S(2)}) collective-permute-start(bf16[256,1024]{1,0:T(8,128)(2,1)} %refs_0_), channel_id=1, source_target_pairs={{0,1},{1,0},{2,3},{3,2},{4,5},{5,4},{6,7},{7,6},{8,9},{9,8},{10,11... | collective-permute-start | bytes 1572872 | tf_op jit(solution)/shard_map/ppermute | solution.py:476
  1.9 3.1 %collective-permute-start = (bf16[32,1024]{1,0:T(8,128)(2,1)S(1)}, bf16[32,1024]{1,0:T(8,128)(2,1)S(1)}, u32[]{:S(2)}, u32[]{:S(2)}) collective-permute-start(bf16[32,1024]{1,0:T(8,128)(2,1)S(1)} %get-tuple-element.39), channel_id=1, source_target_pairs={{0,1},{1,0},{2,3},{3,2},{4,5},{5,4},{6,7},{7,6},{8,9},{9,8},{10,11... | collective-permute-start | bytes 196616 | tf_op jit(solution)/shard_map/ppermute | solution.py:473
  2.0 15.4 %collective-permute-start.2 = (bf16[256,1024]{1,0:T(8,128)(2,1)}, bf16[256,1024]{1,0:T(8,128)(2,1)}, u32[]{:S(2)}, u32[]{:S(2)}) collective-permute-start(bf16[256,1024]{1,0:T(8,128)(2,1)} %refs_0_), channel_id=1, source_target_pairs={{0,2},{1,3},{2,0},{3,1},{4,6},{5,7},{6,4},{7,5},{8,10},{9,11},{10,... | collective-permute-start | bytes 1572872 | tf_op jit(solution)/shard_map/ppermute | solution.py:475
  5.7 13.1 %all-to-all-start = ((bf16[8,32,512]{2,1,0:T(8,128)(2,1)}), bf16[8,32,512]{2,1,0:T(8,128)(2,1)S(1)}, u32[]{:S(2)}, u32[]{:S(2)}) async-start(bf16[8,32,512]{2,1,0:T(8,128)(2,1)} %shard_map.83), calls=%async_computation | async-start | bytes 524288 | tf_op jit(solution)/shard_map/all_to_all | solution.py:449
  12.1 13.5 %copy-start = (bf16[3,512,1024]{2,1,0:T(8,128)(2,1)S(1)}, bf16[3,512,1024]{2,1,0:T(8,128)(2,1)}, u32[]{:S(2)}) copy-start(bf16[3,512,1024]{2,1,0:T(8,128)(2,1)} %weight_ref.2) | copy-start | bytes 9437188
  18.8 8.3 %collective-permute-start.5 = (bf16[256,1024]{1,0:T(8,128)(2,1)}, bf16[256,1024]{1,0:T(8,128)(2,1)}, u32[]{:S(2)}, u32[]{:S(2)}) collective-permute-start(bf16[256,1024]{1,0:T(8,128)(2,1)} %collective-permute-done.2.refs_0_), channel_id=1, source_target_pairs={{0,1},{1,0},{2,3},{3,2},{4,5},{5,4},{6,7},{7,6},{8,9},{9,8},{10,11... | collective-permute-start | bytes 1572872 | tf_op jit(solution)/shard_map/ppermute | solution.py:487
  18.9 5.4 %collective-permute-start.3 = (bf16[64,512]{1,0:T(8,128)(2,1)S(1)}, bf16[64,512]{1,0:T(8,128)(2,1)S(1)}, u32[]{:S(2)}, u32[]{:S(2)}) collective-permute-start(bf16[64,512]{1,0:T(8,128)(2,1)S(1)} %shard_map.85.mine_ref), channel_id=1, source_target_pairs={{0,2},{1,3},{4,6},{5,7},{8,10},{9,11},{12,14},{13,15},{18,16},{19,... | collective-permute-start | bytes 196616 | tf_op jit(solution)/shard_map/ppermute | solution.py:496
  24.3 1.3 %collective-permute-start.4 = (bf16[64,512]{1,0:T(8,128)(2,1)S(1)}, bf16[64,512]{1,0:T(8,128)(2,1)S(1)}, u32[]{:S(2)}, u32[]{:S(2)}) collective-permute-start(bf16[64,512]{1,0:T(8,128)(2,1)S(1)} %shard_map.86.mine_ref), channel_id=1, source_target_pairs={{0,1},{1,0},{2,3},{3,2},{4,5},{5,4},{6,7},{7,6},{8,9},{9,8},{10,11... | collective-permute-start | bytes 196616 | tf_op jit(solution)/shard_map/ppermute | solution.py:498
  27.0 15.8 %all-to-all-start.1 = ((bf16[8,3,64,128]{3,2,1,0:T(8,128)(2,1)}), bf16[8,3,64,128]{3,2,1,0:T(8,128)(2,1)S(1)}, u32[]{:S(2)}, u32[]{:S(2)}) async-start(bf16[8,3,64,128]{3,2,1,0:T(8,128)(2,1)} %shard_map.87), calls=%async_computation.1 | async-start | bytes 786432 | tf_op jit(solution)/shard_map/all_to_all | solution.py:449
  40.2 13.9 %copy-start.1 = (bf16[1024,512]{1,0:T(8,128)(2,1)S(1)}, bf16[1024,512]{1,0:T(8,128)(2,1)}, u32[]{:S(2)}) copy-start(bf16[1024,512]{1,0:T(8,128)(2,1)} %weight_ref.3) | copy-start | bytes 3145732
  42.9 6.3 %collective-permute-start.6 = (bf16[2,256,1024]{2,1,0:T(8,128)(2,1)}, bf16[2,256,1024]{2,1,0:T(8,128)(2,1)S(1)}, u32[]{:S(2)}, u32[]{:S(2)}) collective-permute-start(bf16[2,256,1024]{2,1,0:T(8,128)(2,1)} %get-tuple-element.54), channel_id=1, source_target_pairs={{0,1},{1,0},{2,3},{3,2},{4,5},{5,4},{6,7},{7,6},{8,9},{9,8},{10,11... | collective-permute-start | bytes 3145736 | tf_op jit(solution)/shard_map/ppermute | solution.py:521
  43.9 10.2 %all-to-all-start.2 = ((bf16[8,64,128]{2,1,0:T(8,128)(2,1)}), bf16[8,64,128]{2,1,0:T(8,128)(2,1)S(1)}, u32[]{:S(2)}, u32[]{:S(2)}) async-start(bf16[8,64,128]{2,1,0:T(8,128)(2,1)} %shard_map.89), calls=%async_computation.2 | async-start | bytes 262144 | tf_op jit(solution)/shard_map/all_to_all | solution.py:449
  49.2 0.9 %copy-start.2 = (bf16[256,256]{1,0:T(8,128)(2,1)S(1)}, bf16[256,256]{1,0:T(8,128)(2,1)}, u32[]{:S(2)}) copy-start(bf16[256,256]{1,0:T(8,128)(2,1)} %get-tuple-element.55.heads_ref) | copy-start | bytes 393220
  54.4 1.7 %collective-permute-start.7 = (bf16[64,256]{1,0:T(8,128)(2,1)S(1)}, bf16[64,256]{1,0:T(8,128)(2,1)S(1)}, u32[]{:S(2)}, u32[]{:S(2)}) collective-permute-start(bf16[64,256]{1,0:T(8,128)(2,1)S(1)} %get-tuple-element.60), channel_id=1, source_target_pairs={{0,1},{1,0},{2,3},{3,2},{4,5},{5,4},{6,7},{7,6},{8,9},{9,8},{10,11... | collective-permute-start | bytes 98312 | tf_op jit(solution)/shard_map/ppermute | solution.py:544
  54.5 17.0 %collective-permute-start.8 = (bf16[256,1024]{1,0:T(8,128)(2,1)}, bf16[256,1024]{1,0:T(8,128)(2,1)S(1)}, u32[]{:S(2)}, u32[]{:S(2)}) collective-permute-start(bf16[256,1024]{1,0:T(8,128)(2,1)} %get-tuple-element.62), channel_id=1, source_target_pairs={{0,2},{1,3},{2,0},{3,1},{4,6},{5,7},{6,4},{7,5},{8,10},{9,11},{10,... | collective-permute-start | bytes 1572872 | tf_op jit(solution)/shard_map/ppermute | solution.py:535
  57.0 16.1 %all-to-all-start.3 = ((bf16[16,32,256]{2,1,0:T(8,128)(2,1)}), bf16[16,32,256]{2,1,0:T(8,128)(2,1)S(1)}, u32[]{:S(2)}, u32[]{:S(2)}) async-start(bf16[16,32,256]{2,1,0:T(8,128)(2,1)} %bitcast), calls=%async_computation.3 | async-start | bytes 524288 | tf_op jit(solution)/shard_map/all_to_all | solution.py:553
  71.5 1.7 %copy-start.3 = (bf16[256,1024]{1,0:T(8,128)(2,1)}, bf16[256,1024]{1,0:T(8,128)(2,1)S(1)}, u32[]{:S(2)}) copy-start(bf16[256,1024]{1,0:T(8,128)(2,1)S(1)} %collective-permute-done.8.far) | copy-start | bytes 1572868
  73.1 1.6 %collective-permute-start.9 = (bf16[2,32,256]{2,1,0:T(8,128)(2,1)S(1)}, bf16[2,32,256]{2,1,0:T(8,128)(2,1)S(1)}, u32[]{:S(2)}, u32[]{:S(2)}) collective-permute-start(bf16[2,32,256]{2,1,0:T(8,128)(2,1)S(1)} %shard_map.93), channel_id=1, source_target_pairs={{0,1},{1,0},{2,3},{3,2},{4,5},{5,4},{6,7},{7,6},{8,9},{9,8},{10,11... | collective-permute-start | bytes 98312 | tf_op jit(solution)/shard_map/ppermute | solution.py:564

commit v9 on v7

--- a/solution.py
+++ b/solution.py
@@ -118,8 +118,11 @@
     return tuple(pltpu.with_memory_space_constraint(a, pltpu.VMEM) for a in arrays)
 
 
-def on_chip(kernel, outs, *arrays, hbm=(), scratch=(), flops=0, moved=0, off=False):
-    made = [(jax.ShapeDtypeStruct if off else pltpu.VMEM)(*o) for o in outs]
+def on_chip(kernel, outs, *arrays, hbm=(), scratch=(), flops=0, moved=0, off=False, kept=()):
+    made = [
+        (jax.ShapeDtypeStruct if off and i not in kept else pltpu.VMEM)(*o)
+        for i, o in enumerate(outs)
+    ]
     result = pl.pallas_call(
         kernel,
         in_specs=[pl.BlockSpec(memory_space=pl.ANY)] * len(hbm) + [VMEM] * len(arrays),
@@ -405,6 +408,7 @@
         ],
         flops=6 * count * rows * width * arrays[0].shape[2],
         off=True,
+        kept=(0,) if last else (),
     )
 
 
@@ -514,8 +518,9 @@
         off=True,
     )
     heads = swap(heads)
+    far_sent = lax.ppermute(light_far, "head", across)
     heads, light_own, light_far = lax.optimization_barrier((heads, light_own, light_far))
-    light_far = lax.ppermute(light_far, "head", across)
+    light_far = far_sent
 
     back = on_chip(
         heavy_output_kernel,

time: 74.9 us -> 73.6 us (0.983)
  local copies, waits for them, and re-layouts: 0.92 us -> 0.01 us
    unnamed x8 -> x6, local copies, waits for them, and re-layouts: 0.92 us -> 0.01 us
where the time goes in v9:
time: 73.6 us; the launch traced here: 73.1 us
  starting transfers between devices  28.4 us (39%)
  Pallas kernels  20.6 us (28%)
  waiting for transfers between devices  13 us (18%)
  blocking collectives  11 us (15%)
    pallas_call x13, Pallas kernels, on_chip(): pl.pallas_call(kernel, in_specs=[pl.BlockSpec(memory_space=pl.ANY)] * len...  20.6 us
    all_to_all x3, starting transfers between devices, swap(): lax.all_to_all(x, 'seq', split_axis=0, concat_axis=0, tiled=True, axis_in...  18 us
    all_to_all x1, blocking collectives, swap(): lax.all_to_all(x, 'seq', split_axis=0, concat_axis=0, tiled=True, axis_in...  11 us
    all_to_all x3, waiting for transfers between devices, swap(): lax.all_to_all(x, 'seq', split_axis=0, concat_axis=0, tiled=True, axis_in...  4.72 us
    ppermute x1, starting transfers between devices, one_head_a_device(): crossed = lax.ppermute(mine, ('seq', 'head'), holds)  3.36 us
    ppermute x1, starting transfers between devices, one_head_a_device(): token_far = lax.ppermute(tokens, 'head', across)  2.94 us
    ppermute x1, waiting for transfers between devices, one_head_a_device(): last = lax.ppermute(far, 'head', across)  2.68 us
    ppermute x1, waiting for transfers between devices, one_head_a_device(): crossed = lax.ppermute(mine, ('seq', 'head'), holds)  2 us
  transfers between devices with their start and end apart: 13, of which 9 were waited for; matrix products, arithmetic and copies ran while one was open for 0% of the time, Pallas kernels for 26%

profile of v9, /device:TPU:0, one launch (start us, length us, event | category | flops | bytes accessed | tf_op | source)
XLA Modules:
  0.0 73.1 jit_solution(7699487286258894232)
XLA Ops:
  0.0 0.5 collective-permute-start.1
  0.5 1.4 %shard_map.82 = (bf16[32,1024]{1,0:T(8,128)(2,1)S(1)}, bf16[32,1024]{1,0:T(8,128)(2,1)S(1)}, bf16[64,256]{1,0:T(8,128)(2,1)S(1)}, bf16[64,256]{1,0:T(8,128)(2,1)...) custom-call(bf16[256,1024]{1,0:T(8,128)(2,1)} %refs_0_, s32[8,32]{1,0:T(8,128)} %query_hbm.1, ...), custom_call_target="tpu_custom_call" | custom-call | tf_op jit(solution)/shard_map/pallas_call | solution.py:126
  1.9 0.1 collective-permute-start
  2.0 2.9 %collective-permute-start.2 = (bf16[256,1024]{1,0:T(8,128)(2,1)}, bf16[256,1024]{1,0:T(8,128)(2,1)}, u32[]{:S(2)}, u32[]{:S(2)}) collective-permute-start(bf16[256,1024]{1,0:T(8,128)(2,1)} %refs_0_), channel_id=1, source_target_pairs={{0,2},{1,3},{2,0},{3,1},{4,6},{5,7},{6,4},{7,5},{8,10},{9,11},{10,... | collective-permute-start | bytes 1572872 | tf_op jit(solution)/shard_map/ppermute | solution.py:462
  5.0 0.0 collective-permute-done.got_ref
  5.0 0.7 shard_map.83
  5.7 0.0 collective-permute-done.1.refs_1_
  5.7 6.4 %all-to-all-start = ((bf16[8,32,512]{2,1,0:T(8,128)(2,1)}), bf16[8,32,512]{2,1,0:T(8,128)(2,1)S(1)}, u32[]{:S(2)}, u32[]{:S(2)}) async-start(bf16[8,32,512]{2,1,0:T(8,128)(2,1)} %shard_map.83), calls=%async_computation | async-start | bytes 524288 | tf_op jit(solution)/shard_map/all_to_all | solution.py:436
  12.1 0.0 copy-start
  12.1 4.8 %shard_map.84.refs_3_ = f32[3,256,256]{2,1,0:T(8,128)} custom-call(bf16[256,1024]{1,0:T(8,128)(2,1)} %refs_0_, bf16[256,1024]{1,0:T(8,128)(2,1)} %collective-permute-done.1.refs_1_, bf16[3,4096,256]{2,1,0:T(8,128)(2,1)} %refs_2_.3), custom_call_target="tpu_custom_call" | custom-call | flops 805306368 | tf_op jit(solution)/shard_map/pallas_call | solution.py:126
  16.9 0.5 collective-permute-done.2.refs_0_
  17.4 1.3 %all-to-all-done.slots_ref = bf16[8,32,512]{2,1,0:T(8,128)(2,1)S(1)} async-done(((bf16[8,32,512]{2,1,0:T(8,128)(2,1)}), bf16[8,32,512]{2,1,0:T(8,128)(2,1)S(1)}, u32[]{:S(2)}, u32[]{:S(2)}) %all-to-all-start) | async-done | bytes 262176 | tf_op jit(solution)/shard_map/all_to_all | solution.py:436
  18.8 0.0 collective-permute-start.5
  18.8 0.2 shard_map.85.mine_ref
  18.9 3.4 %collective-permute-start.3 = (bf16[64,512]{1,0:T(8,128)(2,1)S(1)}, bf16[64,512]{1,0:T(8,128)(2,1)S(1)}, u32[]{:S(2)}, u32[]{:S(2)}) collective-permute-start(bf16[64,512]{1,0:T(8,128)(2,1)S(1)} %shard_map.85.mine_ref), channel_id=1, source_target_pairs={{0,2},{1,3},{4,6},{5,7},{8,10},{9,11},{12,14},{13,15},{18,16},{19,... | collective-permute-start | bytes 196616 | tf_op jit(solution)/shard_map/ppermute | solution.py:483
  22.3 2.0 %collective-permute-done.3.crossed_ref = bf16[64,512]{1,0:T(8,128)(2,1)S(1)} collective-permute-done((bf16[64,512]{1,0:T(8,128)(2,1)S(1)}, bf16[64,512]{1,0:T(8,128)(2,1)S(1)}, u32[]{:S(2)}, u32[]{:S(2)}) %collective-permute-start.3) | collective-permute-done | bytes 65568 | tf_op jit(solution)/shard_map/ppermute | solution.py:483
  24.3 0.1 collective-permute-start.4
  24.4 1.2 %collective-permute-done.4.other_ref = bf16[64,512]{1,0:T(8,128)(2,1)S(1)} collective-permute-done((bf16[64,512]{1,0:T(8,128)(2,1)S(1)}, bf16[64,512]{1,0:T(8,128)(2,1)S(1)}, u32[]{:S(2)}, u32[]{:S(2)}) %collective-permute-start.4) | collective-permute-done | bytes 65568 | tf_op jit(solution)/shard_map/ppermute | solution.py:485
  25.6 0.0 copy-done
  25.6 1.4 %shard_map.87 = bf16[8,3,64,128]{3,2,1,0:T(8,128)(2,1)} custom-call(bf16[64,512]{1,0:T(8,128)(2,1)S(1)} %shard_map.86.mine_ref, bf16[64,512]{1,0:T(8,128)(2,1)S(1)} %collective-permute-done.4.other_ref, bf16[3,512,1024]{2,1,0:T(8,128)(2,1)S(1)} %copy-done), custom_call_target="tpu_custom_call" | custom-call | tf_op jit(solution)/shard_map/pallas_call | solution.py:126
  27.0 0.0 collective-permute-done.5.refs_1_
  27.0 6.4 %all-to-all-start.1 = ((bf16[8,3,64,128]{3,2,1,0:T(8,128)(2,1)}), bf16[8,3,64,128]{3,2,1,0:T(8,128)(2,1)S(1)}, u32[]{:S(2)}, u32[]{:S(2)}) async-start(bf16[8,3,64,128]{3,2,1,0:T(8,128)(2,1)} %shard_map.87), calls=%async_computation.1 | async-start | bytes 786432 | tf_op jit(solution)/shard_map/all_to_all | solution.py:436
  33.4 6.8 %shard_map.88 = (bf16[256,256]{1,0:T(8,128)(2,1)S(1)}, bf16[2,256,1024]{2,1,0:T(8,128)(2,1)}) custom-call(bf16[256,1024]{1,0:T(8,128)(2,1)} %collective-permute-done.2.refs_0_, bf16[256,1024]{1,0:T(8,128)(2,1)} %collective-permute-done.5.refs_1_, bf16[3,4096,256]{2,1,0:T(8,128)(2,1)} %refs_2_.3, f32[3,256,256]{2,1,0:T(8,128)} %shard_map.84.refs_3_, ...), custom_call_target="tpu_custom_call" | custom-call | flops 805306368 | tf_op jit(solution)/shard_map/pallas_call | solution.py:126
  40.2 0.0 copy-start.1
  40.2 2.7 %all-to-all-done.1.parts_ref = bf16[8,3,64,128]{3,2,1,0:T(8,128)(2,1)S(1)} async-done(((bf16[8,3,64,128]{3,2,1,0:T(8,128)(2,1)}), bf16[8,3,64,128]{3,2,1,0:T(8,128)(2,1)S(1)}, u32[]{:S(2)}, u32[]{:S(2)}) %all-to-all-start.1) | async-done | bytes 393248 | tf_op jit(solution)/shard_map/all_to_all | solution.py:436
  42.9 0.0 collective-permute-start.6
  42.9 1.0 %shard_map.89 = bf16[8,64,128]{2,1,0:T(8,128)(2,1)} custom-call(bf16[8,3,64,128]{3,2,1,0:T(8,128)(2,1)S(1)} %all-to-all-done.1.parts_ref), custom_call_target="tpu_custom_call" | custom-call | tf_op jit(solution)/shard_map/pallas_call | solution.py:126
  43.9 5.3 %all-to-all-start.2 = ((bf16[8,64,128]{2,1,0:T(8,128)(2,1)}), bf16[8,64,128]{2,1,0:T(8,128)(2,1)S(1)}, u32[]{:S(2)}, u32[]{:S(2)}) async-start(bf16[8,64,128]{2,1,0:T(8,128)(2,1)} %shard_map.89), calls=%async_computation.2 | async-start | bytes 262144 | tf_op jit(solution)/shard_map/all_to_all | solution.py:436
  49.2 0.0 collective-permute-done.6.got_ref
  49.2 2.5 %shard_map.90 = (f32[256,1024]{1,0:T(8,128)}, bf16[256,1024]{1,0:T(8,128)(2,1)}) custom-call(bf16[256,4096]{1,0:T(8,128)(2,1)} %w_out.1, bf16[2,256,1024]{2,1,0:T(8,128)(2,1)S(1)} %collective-permute-done.6.got_ref, bf16[256,256]{1,0:T(8,128)(2,1)S(1)} %get-tuple-element.49.heads_ref), custom_call_target="tpu_custom_call" | custom-call | flops 268435456 | tf_op jit(solution)/shard_map/pallas_call | solution.py:126
  51.7 0.0 copy-start.2
  51.7 1.7 %collective-permute-start.7 = (bf16[256,1024]{1,0:T(8,128)(2,1)}, bf16[256,1024]{1,0:T(8,128)(2,1)S(1)}, u32[]{:S(2)}, u32[]{:S(2)}) collective-permute-start(bf16[256,1024]{1,0:T(8,128)(2,1)} %get-tuple-element.51), channel_id=1, source_target_pairs={{0,2},{1,3},{2,0},{3,1},{4,6},{5,7},{6,4},{7,5},{8,10},{9,11},{10,... | collective-permute-start | bytes 1572872 | tf_op jit(solution)/shard_map/ppermute | solution.py:521
  53.4 0.7 all-to-all-done.2.heads_ref
  54.1 0.0 copy-done.1
  54.1 0.5 shard_map.91
  54.6 11.0 %all_to_all.20.back_ref = bf16[8,32,512]{2,1,0:T(8,128)(2,1)S(1)} all-to-all(bf16[8,32,512]{2,1,0:T(8,128)(2,1)S(1)} %shard_map.91), channel_id=1, replica_groups={{12,8,20,16,4,0,28,24},{13,9,21,17,5,1,29,25},{14,10,22,18,6,2,30,26},{..., dimensions={0} | all-to-all | bytes 524288 | tf_op jit(solution)/shard_map/all_to_all | solution.py:436
  65.6 0.5 collective-permute-done.7.light_far_ref
  66.1 0.1 collective-permute-start.8
  66.1 1.3 %collective-permute-done.8.got_ref = bf16[2,2,32,512]{3,2,1,0:T(8,128)(2,1)S(1)} collective-permute-done((bf16[2,2,32,512]{3,2,1,0:T(8,128)(2,1)S(1)}, bf16[2,2,32,512]{3,2,1,0:T(8,128)(2,1)S(1)}, u32[]{:S(2)}, u32[]{:S(2)}) %collective-permute-start.8) | collective-permute-done | bytes 131104 | tf_op jit(solution)/shard_map/ppermute | solution.py:535
  67.5 1.7 %collective-permute-start.9 = (bf16[2,32,512]{2,1,0:T(8,128)(2,1)S(1)}, bf16[2,32,512]{2,1,0:T(8,128)(2,1)S(1)}, u32[]{:S(2)}, u32[]{:S(2)}) collective-permute-start(bf16[2,32,512]{2,1,0:T(8,128)(2,1)S(1)} %shard_map.93), channel_id=1, source_target_pairs={{0,2},{1,3},{2,0},{3,1},{4,6},{5,7},{6,4},{7,5},{8,10},{9,11},{10,... | collective-permute-start | bytes 196616 | tf_op jit(solution)/shard_map/ppermute | solution.py:537
  69.2 2.7 %collective-permute-done.9.last_ref = bf16[2,32,512]{2,1,0:T(8,128)(2,1)S(1)} collective-permute-done((bf16[2,32,512]{2,1,0:T(8,128)(2,1)S(1)}, bf16[2,32,512]{2,1,0:T(8,128)(2,1)S(1)}, u32[]{:S(2)}, u32[]{:S(2)}) %collective-permute-start.9) | collective-permute-done | bytes 65568 | tf_op jit(solution)/shard_map/ppermute | solution.py:537
  71.8 0.0 copy-done.2
  71.8 1.3 %shard_map.94 = bf16[256,1024]{1,0:T(8,128)(2,1)} custom-call(f32[256,1024]{1,0:T(8,128)S(1)} %copy-done.2, bf16[256,1024]{1,0:T(8,128)(2,1)S(1)} %collective-permute-done.7.light_far_ref, bf16[8,32,512]{2,1,0:T(8,128)(2,1)S(1)} %all_to_all.20.back_ref, bf16[2,2,32,512]{3,2,1,0:T(8,128)(2,1)S(1)} %collective-permute-done.8.got_ref, ...), custom_call_target="tpu_custom_call" | custom-call | tf_op jit(solution)/shard_map/pallas_call | solution.py:126
  (3 shorter events, 0.0 us)
Async XLA Ops:
  0.0 5.7 %collective-permute-start.1 = (bf16[256,1024]{1,0:T(8,128)(2,1)}, bf16[256,1024]{1,0:T(8,128)(2,1)}, u32[]{:S(2)}, u32[]{:S(2)}) collective-permute-start(bf16[256,1024]{1,0:T(8,128)(2,1)} %refs_0_), channel_id=1, source_target_pairs={{0,1},{1,0},{2,3},{3,2},{4,5},{5,4},{6,7},{7,6},{8,9},{9,8},{10,11... | collective-permute-start | bytes 1572872 | tf_op jit(solution)/shard_map/ppermute | solution.py:463
  1.9 3.1 %collective-permute-start = (bf16[32,1024]{1,0:T(8,128)(2,1)S(1)}, bf16[32,1024]{1,0:T(8,128)(2,1)S(1)}, u32[]{:S(2)}, u32[]{:S(2)}) collective-permute-start(bf16[32,1024]{1,0:T(8,128)(2,1)S(1)} %get-tuple-element.33), channel_id=1, source_target_pairs={{0,1},{1,0},{2,3},{3,2},{4,5},{5,4},{6,7},{7,6},{8,9},{9,8},{10,11... | collective-permute-start | bytes 196616 | tf_op jit(solution)/shard_map/ppermute | solution.py:460
  2.0 15.4 %collective-permute-start.2 = (bf16[256,1024]{1,0:T(8,128)(2,1)}, bf16[256,1024]{1,0:T(8,128)(2,1)}, u32[]{:S(2)}, u32[]{:S(2)}) collective-permute-start(bf16[256,1024]{1,0:T(8,128)(2,1)} %refs_0_), channel_id=1, source_target_pairs={{0,2},{1,3},{2,0},{3,1},{4,6},{5,7},{6,4},{7,5},{8,10},{9,11},{10,... | collective-permute-start | bytes 1572872 | tf_op jit(solution)/shard_map/ppermute | solution.py:462
  5.7 13.1 %all-to-all-start = ((bf16[8,32,512]{2,1,0:T(8,128)(2,1)}), bf16[8,32,512]{2,1,0:T(8,128)(2,1)S(1)}, u32[]{:S(2)}, u32[]{:S(2)}) async-start(bf16[8,32,512]{2,1,0:T(8,128)(2,1)} %shard_map.83), calls=%async_computation | async-start | bytes 524288 | tf_op jit(solution)/shard_map/all_to_all | solution.py:436
  12.1 13.5 %copy-start = (bf16[3,512,1024]{2,1,0:T(8,128)(2,1)S(1)}, bf16[3,512,1024]{2,1,0:T(8,128)(2,1)}, u32[]{:S(2)}) copy-start(bf16[3,512,1024]{2,1,0:T(8,128)(2,1)} %weight_ref.2) | copy-start | bytes 9437188
  18.8 8.3 %collective-permute-start.5 = (bf16[256,1024]{1,0:T(8,128)(2,1)}, bf16[256,1024]{1,0:T(8,128)(2,1)}, u32[]{:S(2)}, u32[]{:S(2)}) collective-permute-start(bf16[256,1024]{1,0:T(8,128)(2,1)} %collective-permute-done.2.refs_0_), channel_id=1, source_target_pairs={{0,1},{1,0},{2,3},{3,2},{4,5},{5,4},{6,7},{7,6},{8,9},{9,8},{10,11... | collective-permute-start | bytes 1572872 | tf_op jit(solution)/shard_map/ppermute | solution.py:474
  18.9 5.4 %collective-permute-start.3 = (bf16[64,512]{1,0:T(8,128)(2,1)S(1)}, bf16[64,512]{1,0:T(8,128)(2,1)S(1)}, u32[]{:S(2)}, u32[]{:S(2)}) collective-permute-start(bf16[64,512]{1,0:T(8,128)(2,1)S(1)} %shard_map.85.mine_ref), channel_id=1, source_target_pairs={{0,2},{1,3},{4,6},{5,7},{8,10},{9,11},{12,14},{13,15},{18,16},{19,... | collective-permute-start | bytes 196616 | tf_op jit(solution)/shard_map/ppermute | solution.py:483
  24.3 1.3 %collective-permute-start.4 = (bf16[64,512]{1,0:T(8,128)(2,1)S(1)}, bf16[64,512]{1,0:T(8,128)(2,1)S(1)}, u32[]{:S(2)}, u32[]{:S(2)}) collective-permute-start(bf16[64,512]{1,0:T(8,128)(2,1)S(1)} %shard_map.86.mine_ref), channel_id=1, source_target_pairs={{0,1},{1,0},{2,3},{3,2},{4,5},{5,4},{6,7},{7,6},{8,9},{9,8},{10,11... | collective-permute-start | bytes 196616 | tf_op jit(solution)/shard_map/ppermute | solution.py:485
  27.0 15.8 %all-to-all-start.1 = ((bf16[8,3,64,128]{3,2,1,0:T(8,128)(2,1)}), bf16[8,3,64,128]{3,2,1,0:T(8,128)(2,1)S(1)}, u32[]{:S(2)}, u32[]{:S(2)}) async-start(bf16[8,3,64,128]{3,2,1,0:T(8,128)(2,1)} %shard_map.87), calls=%async_computation.1 | async-start | bytes 786432 | tf_op jit(solution)/shard_map/all_to_all | solution.py:436
  40.2 13.9 %copy-start.1 = (bf16[1024,512]{1,0:T(8,128)(2,1)S(1)}, bf16[1024,512]{1,0:T(8,128)(2,1)}, u32[]{:S(2)}) copy-start(bf16[1024,512]{1,0:T(8,128)(2,1)} %weight_ref.3) | copy-start | bytes 3145732
  42.9 6.3 %collective-permute-start.6 = (bf16[2,256,1024]{2,1,0:T(8,128)(2,1)}, bf16[2,256,1024]{2,1,0:T(8,128)(2,1)S(1)}, u32[]{:S(2)}, u32[]{:S(2)}) collective-permute-start(bf16[2,256,1024]{2,1,0:T(8,128)(2,1)} %get-tuple-element.48), channel_id=1, source_target_pairs={{0,1},{1,0},{2,3},{3,2},{4,5},{5,4},{6,7},{7,6},{8,9},{9,8},{10,11... | collective-permute-start | bytes 3145736 | tf_op jit(solution)/shard_map/ppermute | solution.py:508
  43.9 10.2 %all-to-all-start.2 = ((bf16[8,64,128]{2,1,0:T(8,128)(2,1)}), bf16[8,64,128]{2,1,0:T(8,128)(2,1)S(1)}, u32[]{:S(2)}, u32[]{:S(2)}) async-start(bf16[8,64,128]{2,1,0:T(8,128)(2,1)} %shard_map.89), calls=%async_computation.2 | async-start | bytes 262144 | tf_op jit(solution)/shard_map/all_to_all | solution.py:436
  51.7 20.1 %copy-start.2 = (f32[256,1024]{1,0:T(8,128)S(1)}, f32[256,1024]{1,0:T(8,128)}, u32[]{:S(2)}) copy-start(f32[256,1024]{1,0:T(8,128)} %get-tuple-element.52.light_ref) | copy-start | bytes 3145732
  51.7 14.3 %collective-permute-start.7 = (bf16[256,1024]{1,0:T(8,128)(2,1)}, bf16[256,1024]{1,0:T(8,128)(2,1)S(1)}, u32[]{:S(2)}, u32[]{:S(2)}) collective-permute-start(bf16[256,1024]{1,0:T(8,128)(2,1)} %get-tuple-element.51), channel_id=1, source_target_pairs={{0,2},{1,3},{2,0},{3,1},{4,6},{5,7},{6,4},{7,5},{8,10},{9,11},{10,... | collective-permute-start | bytes 1572872 | tf_op jit(solution)/shard_map/ppermute | solution.py:521
  66.1 1.4 %collective-permute-start.8 = (bf16[2,2,32,512]{3,2,1,0:T(8,128)(2,1)S(1)}, bf16[2,2,32,512]{3,2,1,0:T(8,128)(2,1)S(1)}, u32[]{:S(2)}, u32[]{:S(2)}) collective-permute-start(bf16[2,2,32,512]{3,2,1,0:T(8,128)(2,1)S(1)} %shard_map.92), channel_id=1, source_target_pairs={{0,1},{1,0},{2,3},{3,2},{4,5},{5,4},{6,7},{7,6},{8,9},{9,8},{10,11... | collective-permute-start | bytes 393224 | tf_op jit(solution)/shard_map/ppermute | solution.py:535
  67.5 4.3 %collective-permute-start.9 = (bf16[2,32,512]{2,1,0:T(8,128)(2,1)S(1)}, bf16[2,32,512]{2,1,0:T(8,128)(2,1)S(1)}, u32[]{:S(2)}, u32[]{:S(2)}) collective-permute-start(bf16[2,32,512]{2,1,0:T(8,128)(2,1)S(1)} %shard_map.93), channel_id=1, source_target_pairs={{0,2},{1,3},{2,0},{3,1},{4,6},{5,7},{6,4},{7,5},{8,10},{9,11},{10,... | collective-permute-start | bytes 196616 | tf_op jit(solution)/shard_map/ppermute | solution.py:537

commit v10 on v9

--- a/solution.py
+++ b/solution.py
@@ -243,15 +243,13 @@
     out_ref[...] = jnp.dot(chosen_ref[...], rows, preferred_element_type=F32).astype(BF)
 
 
-def choose_kernel(mine_ref, crossed_ref, out_ref):
+def project_kernel(mine_ref, pair_ref, across_ref, last_ref, weight_ref, out_ref):
     pairs = lax.axis_size("head") // 2
     holder = lax.axis_index("seq") * pairs // lax.axis_size("seq")
-    out_ref[...] = jnp.where(holder == lax.axis_index("head") // 2, mine_ref[...], crossed_ref[...])
-
-
-def project_kernel(mine_ref, other_ref, weight_ref, out_ref):
+    holds = holder == lax.axis_index("head") // 2
+    mine = jnp.where(holds, mine_ref[...], across_ref[...])
+    other = jnp.where(holds, pair_ref[...], last_ref[...])
     odd = lax.axis_index("head") % 2
-    mine, other = mine_ref[...], other_ref[...]
     query = jnp.where(odd == 0, mine, other)
     source = jnp.where(odd == 0, other, mine)
     spot = spots(out_ref.shape[0])
@@ -473,18 +471,10 @@
     spread, token_far, light_sum = lax.optimization_barrier((spread, token_far, light_sum))
     token_last = lax.ppermute(token_far, "head", pair)
     mine = on_chip(compact_kernel, [((routed, part_width), BF)], spread, mine_map, moved=20 << 20)
-    half = seq_count * 2 // head_count
-    holds = [
-        (s * head_count + h, s * head_count + (h ^ 2))
-        for s in range(seq_count)
-        for h in range(head_count)
-        if s // half == h // 2
-    ]
-    crossed = lax.ppermute(mine, ("seq", "head"), holds)
-    mine = on_chip(choose_kernel, [((routed, part_width), BF)], mine, crossed)
-    other = lax.ppermute(mine, "head", pair)
+    diagonal = [(i, i ^ 3) for i in range(head_count)]
+    rows = [mine, *(lax.ppermute(mine, "head", p) for p in (pair, across, diagonal))]
     parts = on_chip(
-        project_kernel, [((seq_count, 3, routed, HD), BF)], mine, other, heavy_input
+        project_kernel, [((seq_count, 3, routed, HD), BF)], *rows, heavy_input
     )
 
     parts, light_sum, token_far, token_last = lax.optimization_barrier(

time: 73.6 us -> 70.9 us (0.963)
  starting transfers between devices: 28.4 us -> 26.5 us
  waiting for transfers between devices: 13 us -> 11.9 us
    ppermute x2 -> x3, starting transfers between devices: 3.43 us -> 2.2 us  [one_head_a_device(): lax.ppermute(mine, 'head', p)]
    all_to_all x3, waiting for transfers between devices: 4.72 us -> 3.52 us  [swap(): lax.all_to_all(x, 'seq', split_axis=0, concat_axis=0, tiled=True, axis_in...]
    all_to_all x3, starting transfers between devices: 18 us -> 17.1 us  [swap(): lax.all_to_all(x, 'seq', split_axis=0, concat_axis=0, tiled=True, axis_in...]
    ppermute x2 -> x3, waiting for transfers between devices: 3.24 us -> 3.69 us  [one_head_a_device(): lax.ppermute(mine, 'head', p)]
    pallas_call x13 -> x12, Pallas kernels: 20.6 us -> 20.6 us  [on_chip(): pl.pallas_call(kernel, in_specs=[pl.BlockSpec(memory_space=pl.ANY)] * len...]
  transfers between devices with their start and end apart: 13 -> 14, of which waited for: 9 -> 9; matrix products, arithmetic and copies ran while one was open for 0% -> 0% of each run, Pallas kernels for 26% -> 27%
where the time goes in v10:
time: 70.9 us; the launch traced here: 70.4 us
  starting transfers between devices  26.5 us (37%)
  Pallas kernels  20.6 us (29%)
  waiting for transfers between devices  11.9 us (17%)
  blocking collectives  11.2 us (16%)
    pallas_call x12, Pallas kernels, on_chip(): pl.pallas_call(kernel, in_specs=[pl.BlockSpec(memory_space=pl.ANY)] * len...  20.6 us
    all_to_all x3, starting transfers between devices, swap(): lax.all_to_all(x, 'seq', split_axis=0, concat_axis=0, tiled=True, axis_in...  17.1 us
    all_to_all x1, blocking collectives, swap(): lax.all_to_all(x, 'seq', split_axis=0, concat_axis=0, tiled=True, axis_in...  11.2 us
    ppermute x3, waiting for transfers between devices, one_head_a_device(): lax.ppermute(mine, 'head', p)  3.69 us
    all_to_all x3, waiting for transfers between devices, swap(): lax.all_to_all(x, 'seq', split_axis=0, concat_axis=0, tiled=True, axis_in...  3.52 us
    ppermute x1, starting transfers between devices, one_head_a_device(): token_far = lax.ppermute(tokens, 'head', across)  2.94 us
    ppermute x1, waiting for transfers between devices, one_head_a_device(): last = lax.ppermute(far, 'head', across)  2.52 us
    ppermute x3, starting transfers between devices, one_head_a_device(): lax.ppermute(mine, 'head', p)  2.2 us
  transfers between devices with their start and end apart: 14, of which 9 were waited for; matrix products, arithmetic and copies ran while one was open for 0% of the time, Pallas kernels for 27%

profile of v10, /device:TPU:0, one launch (start us, length us, event | category | flops | bytes accessed | tf_op | source)
XLA Modules:
  0.0 70.4 jit_solution(12695006341529723295)
XLA Ops:
  0.0 0.5 collective-permute-start.1
  0.5 1.4 %shard_map.82 = (bf16[32,1024]{1,0:T(8,128)(2,1)S(1)}, bf16[32,1024]{1,0:T(8,128)(2,1)S(1)}, bf16[64,256]{1,0:T(8,128)(2,1)S(1)}, bf16[64,256]{1,0:T(8,128)(2,1)...) custom-call(bf16[256,1024]{1,0:T(8,128)(2,1)} %refs_0_, s32[8,32]{1,0:T(8,128)} %query_hbm.1, ...), custom_call_target="tpu_custom_call" | custom-call | tf_op jit(solution)/shard_map/pallas_call | solution.py:126
  1.9 0.1 collective-permute-start
  2.0 2.9 %collective-permute-start.2 = (bf16[256,1024]{1,0:T(8,128)(2,1)}, bf16[256,1024]{1,0:T(8,128)(2,1)}, u32[]{:S(2)}, u32[]{:S(2)}) collective-permute-start(bf16[256,1024]{1,0:T(8,128)(2,1)} %refs_0_), channel_id=1, source_target_pairs={{0,2},{1,3},{2,0},{3,1},{4,6},{5,7},{6,4},{7,5},{8,10},{9,11},{10,... | collective-permute-start | bytes 1572872 | tf_op jit(solution)/shard_map/ppermute | solution.py:460
  5.0 0.0 collective-permute-done.got_ref
  5.0 0.7 %shard_map.83 = bf16[8,32,512]{2,1,0:T(8,128)(2,1)} custom-call(bf16[32,1024]{1,0:T(8,128)(2,1)S(1)} %get-tuple-element.32.keep_ref, bf16[32,1024]{1,0:T(8,128)(2,1)S(1)} %collective-permute-done.got_ref), custom_call_target="tpu_custom_call" | custom-call | tf_op jit(solution)/shard_map/pallas_call | solution.py:126
  5.7 0.0 collective-permute-done.1.refs_1_
  5.7 6.4 %all-to-all-start = ((bf16[8,32,512]{2,1,0:T(8,128)(2,1)}), bf16[8,32,512]{2,1,0:T(8,128)(2,1)S(1)}, u32[]{:S(2)}, u32[]{:S(2)}) async-start(bf16[8,32,512]{2,1,0:T(8,128)(2,1)} %shard_map.83), calls=%async_computation | async-start | bytes 524288 | tf_op jit(solution)/shard_map/all_to_all | solution.py:434
  12.1 0.0 copy-start
  12.1 4.8 %shard_map.84.refs_3_ = f32[3,256,256]{2,1,0:T(8,128)} custom-call(bf16[256,1024]{1,0:T(8,128)(2,1)} %refs_0_, bf16[256,1024]{1,0:T(8,128)(2,1)} %collective-permute-done.1.refs_1_, bf16[3,4096,256]{2,1,0:T(8,128)(2,1)} %refs_2_.3), custom_call_target="tpu_custom_call" | custom-call | flops 805306368 | tf_op jit(solution)/shard_map/pallas_call | solution.py:126
  16.9 0.5 collective-permute-done.2.refs_0_
  17.4 1.3 %all-to-all-done.slots_ref = bf16[8,32,512]{2,1,0:T(8,128)(2,1)S(1)} async-done(((bf16[8,32,512]{2,1,0:T(8,128)(2,1)}), bf16[8,32,512]{2,1,0:T(8,128)(2,1)S(1)}, u32[]{:S(2)}, u32[]{:S(2)}) %all-to-all-start) | async-done | bytes 262176 | tf_op jit(solution)/shard_map/all_to_all | solution.py:434
  18.8 0.0 collective-permute-start.6
  18.8 0.2 shard_map.85.mine_ref
  18.9 1.6 %collective-permute-start.5 = (bf16[64,512]{1,0:T(8,128)(2,1)S(1)}, bf16[64,512]{1,0:T(8,128)(2,1)S(1)}, u32[]{:S(2)}, u32[]{:S(2)}) collective-permute-start(bf16[64,512]{1,0:T(8,128)(2,1)S(1)} %shard_map.85.mine_ref), channel_id=1, source_target_pairs={{0,3},{1,2},{2,1},{3,0},{4,7},{5,6},{6,5},{7,4},{8,11},{9,10},{10,... | collective-permute-start | bytes 196616 | tf_op jit(solution)/shard_map/ppermute | solution.py:475
  20.6 0.6 collective-permute-start.4
  21.1 0.0 collective-permute-start.3
  21.1 1.9 %collective-permute-done.5.last_ref = bf16[64,512]{1,0:T(8,128)(2,1)S(1)} collective-permute-done((bf16[64,512]{1,0:T(8,128)(2,1)S(1)}, bf16[64,512]{1,0:T(8,128)(2,1)S(1)}, u32[]{:S(2)}, u32[]{:S(2)}) %collective-permute-start.5) | collective-permute-done | bytes 65568 | tf_op jit(solution)/shard_map/ppermute | solution.py:475
  23.0 1.8 %collective-permute-done.4.across_ref = bf16[64,512]{1,0:T(8,128)(2,1)S(1)} collective-permute-done((bf16[64,512]{1,0:T(8,128)(2,1)S(1)}, bf16[64,512]{1,0:T(8,128)(2,1)S(1)}, u32[]{:S(2)}, u32[]{:S(2)}) %collective-permute-start.4) | collective-permute-done | bytes 65568 | tf_op jit(solution)/shard_map/ppermute | solution.py:475
  24.8 0.0 collective-permute-done.3.pair_ref
  24.8 0.0 copy-done
  24.8 1.4 %shard_map.86 = bf16[8,3,64,128]{3,2,1,0:T(8,128)(2,1)} custom-call(bf16[64,512]{1,0:T(8,128)(2,1)S(1)} %shard_map.85.mine_ref, bf16[64,512]{1,0:T(8,128)(2,1)S(1)} %collective-permute-done.3.pair_ref, bf16[64,512]{1,0:T(8,128)(2,1)S(1)} %collective-permute-done.4.across_ref, bf16[64,512]{1,0:T(8,128)(2,1)S(1)} %collective-permute-done.5.last_ref, ...), custom_call_target="tpu_custom_call" | custom-call | tf_op jit(solution)/shard_map/pallas_call | solution.py:126
  26.2 0.0 collective-permute-done.6.refs_1_
  26.2 5.4 %all-to-all-start.1 = ((bf16[8,3,64,128]{3,2,1,0:T(8,128)(2,1)}), bf16[8,3,64,128]{3,2,1,0:T(8,128)(2,1)S(1)}, u32[]{:S(2)}, u32[]{:S(2)}) async-start(bf16[8,3,64,128]{3,2,1,0:T(8,128)(2,1)} %shard_map.86), calls=%async_computation.1 | async-start | bytes 786432 | tf_op jit(solution)/shard_map/all_to_all | solution.py:434
  31.6 6.8 %shard_map.87 = (bf16[256,256]{1,0:T(8,128)(2,1)S(1)}, bf16[2,256,1024]{2,1,0:T(8,128)(2,1)}) custom-call(bf16[256,1024]{1,0:T(8,128)(2,1)} %collective-permute-done.2.refs_0_, bf16[256,1024]{1,0:T(8,128)(2,1)} %collective-permute-done.6.refs_1_, bf16[3,4096,256]{2,1,0:T(8,128)(2,1)} %refs_2_.3, f32[3,256,256]{2,1,0:T(8,128)} %shard_map.84.refs_3_, ...), custom_call_target="tpu_custom_call" | custom-call | flops 805306368 | tf_op jit(solution)/shard_map/pallas_call | solution.py:126
  38.4 0.0 copy-start.1
  38.4 1.7 %all-to-all-done.1.parts_ref = bf16[8,3,64,128]{3,2,1,0:T(8,128)(2,1)S(1)} async-done(((bf16[8,3,64,128]{3,2,1,0:T(8,128)(2,1)}), bf16[8,3,64,128]{3,2,1,0:T(8,128)(2,1)S(1)}, u32[]{:S(2)}, u32[]{:S(2)}) %all-to-all-start.1) | async-done | bytes 393248 | tf_op jit(solution)/shard_map/all_to_all | solution.py:434
  40.1 0.0 collective-permute-start.7
  40.1 1.0 %shard_map.88 = bf16[8,64,128]{2,1,0:T(8,128)(2,1)} custom-call(bf16[8,3,64,128]{3,2,1,0:T(8,128)(2,1)S(1)} %all-to-all-done.1.parts_ref), custom_call_target="tpu_custom_call" | custom-call | tf_op jit(solution)/shard_map/pallas_call | solution.py:126
  41.1 5.3 %all-to-all-start.2 = ((bf16[8,64,128]{2,1,0:T(8,128)(2,1)}), bf16[8,64,128]{2,1,0:T(8,128)(2,1)S(1)}, u32[]{:S(2)}, u32[]{:S(2)}) async-start(bf16[8,64,128]{2,1,0:T(8,128)(2,1)} %shard_map.88), calls=%async_computation.2 | async-start | bytes 262144 | tf_op jit(solution)/shard_map/all_to_all | solution.py:434
  46.4 0.0 collective-permute-done.7.got_ref
  46.4 2.5 %shard_map.89 = (f32[256,1024]{1,0:T(8,128)}, bf16[256,1024]{1,0:T(8,128)(2,1)}) custom-call(bf16[256,4096]{1,0:T(8,128)(2,1)} %w_out.1, bf16[2,256,1024]{2,1,0:T(8,128)(2,1)S(1)} %collective-permute-done.7.got_ref, bf16[256,256]{1,0:T(8,128)(2,1)S(1)} %get-tuple-element.49.heads_ref), custom_call_target="tpu_custom_call" | custom-call | flops 268435456 | tf_op jit(solution)/shard_map/pallas_call | solution.py:126
  49.0 0.0 copy-start.2
  49.0 1.9 %collective-permute-start.8 = (bf16[256,1024]{1,0:T(8,128)(2,1)}, bf16[256,1024]{1,0:T(8,128)(2,1)S(1)}, u32[]{:S(2)}, u32[]{:S(2)}) collective-permute-start(bf16[256,1024]{1,0:T(8,128)(2,1)} %get-tuple-element.51), channel_id=1, source_target_pairs={{0,2},{1,3},{2,0},{3,1},{4,6},{5,7},{6,4},{7,5},{8,10},{9,11},{10,... | collective-permute-start | bytes 1572872 | tf_op jit(solution)/shard_map/ppermute | solution.py:511
  50.8 0.5 all-to-all-done.2.heads_ref
  51.3 0.0 copy-done.1
  51.3 0.5 shard_map.90
  51.8 11.2 %all_to_all.20.back_ref = bf16[8,32,512]{2,1,0:T(8,128)(2,1)S(1)} all-to-all(bf16[8,32,512]{2,1,0:T(8,128)(2,1)S(1)} %shard_map.90), channel_id=1, replica_groups={{12,8,20,16,4,0,28,24},{13,9,21,17,5,1,29,25},{14,10,22,18,6,2,30,26},{..., dimensions={0} | all-to-all | bytes 524288 | tf_op jit(solution)/shard_map/all_to_all | solution.py:434
  63.1 0.3 collective-permute-done.8.light_far_ref
  63.4 0.1 collective-permute-start.9
  63.4 1.3 %collective-permute-done.9.got_ref = bf16[2,2,32,512]{3,2,1,0:T(8,128)(2,1)S(1)} collective-permute-done((bf16[2,2,32,512]{3,2,1,0:T(8,128)(2,1)S(1)}, bf16[2,2,32,512]{3,2,1,0:T(8,128)(2,1)S(1)}, u32[]{:S(2)}, u32[]{:S(2)}) %collective-permute-start.9) | collective-permute-done | bytes 131104 | tf_op jit(solution)/shard_map/ppermute | solution.py:525
  64.8 1.8 %collective-permute-start.10 = (bf16[2,32,512]{2,1,0:T(8,128)(2,1)S(1)}, bf16[2,32,512]{2,1,0:T(8,128)(2,1)S(1)}, u32[]{:S(2)}, u32[]{:S(2)}) collective-permute-start(bf16[2,32,512]{2,1,0:T(8,128)(2,1)S(1)} %shard_map.92), channel_id=1, source_target_pairs={{0,2},{1,3},{2,0},{3,1},{4,6},{5,7},{6,4},{7,5},{8,10},{9,11},{10,... | collective-permute-start | bytes 196616 | tf_op jit(solution)/shard_map/ppermute | solution.py:527
  66.6 2.5 %collective-permute-done.10.last_ref = bf16[2,32,512]{2,1,0:T(8,128)(2,1)S(1)} collective-permute-done((bf16[2,32,512]{2,1,0:T(8,128)(2,1)S(1)}, bf16[2,32,512]{2,1,0:T(8,128)(2,1)S(1)}, u32[]{:S(2)}, u32[]{:S(2)}) %collective-permute-start.10) | collective-permute-done | bytes 65568 | tf_op jit(solution)/shard_map/ppermute | solution.py:527
  69.1 0.0 copy-done.2
  69.1 1.3 %shard_map.93 = bf16[256,1024]{1,0:T(8,128)(2,1)} custom-call(f32[256,1024]{1,0:T(8,128)S(1)} %copy-done.2, bf16[256,1024]{1,0:T(8,128)(2,1)S(1)} %collective-permute-done.8.light_far_ref, bf16[8,32,512]{2,1,0:T(8,128)(2,1)S(1)} %all_to_all.20.back_ref, bf16[2,2,32,512]{3,2,1,0:T(8,128)(2,1)S(1)} %collective-permute-done.9.got_ref, ...), custom_call_target="tpu_custom_call" | custom-call | tf_op jit(solution)/shard_map/pallas_call | solution.py:126
  (2 shorter events, 0.0 us)
Async XLA Ops:
  0.0 5.7 %collective-permute-start.1 = (bf16[256,1024]{1,0:T(8,128)(2,1)}, bf16[256,1024]{1,0:T(8,128)(2,1)}, u32[]{:S(2)}, u32[]{:S(2)}) collective-permute-start(bf16[256,1024]{1,0:T(8,128)(2,1)} %refs_0_), channel_id=1, source_target_pairs={{0,1},{1,0},{2,3},{3,2},{4,5},{5,4},{6,7},{7,6},{8,9},{9,8},{10,11... | collective-permute-start | bytes 1572872 | tf_op jit(solution)/shard_map/ppermute | solution.py:461
  1.9 3.1 %collective-permute-start = (bf16[32,1024]{1,0:T(8,128)(2,1)S(1)}, bf16[32,1024]{1,0:T(8,128)(2,1)S(1)}, u32[]{:S(2)}, u32[]{:S(2)}) collective-permute-start(bf16[32,1024]{1,0:T(8,128)(2,1)S(1)} %get-tuple-element.33), channel_id=1, source_target_pairs={{0,1},{1,0},{2,3},{3,2},{4,5},{5,4},{6,7},{7,6},{8,9},{9,8},{10,11... | collective-permute-start | bytes 196616 | tf_op jit(solution)/shard_map/ppermute | solution.py:458
  2.0 15.4 %collective-permute-start.2 = (bf16[256,1024]{1,0:T(8,128)(2,1)}, bf16[256,1024]{1,0:T(8,128)(2,1)}, u32[]{:S(2)}, u32[]{:S(2)}) collective-permute-start(bf16[256,1024]{1,0:T(8,128)(2,1)} %refs_0_), channel_id=1, source_target_pairs={{0,2},{1,3},{2,0},{3,1},{4,6},{5,7},{6,4},{7,5},{8,10},{9,11},{10,... | collective-permute-start | bytes 1572872 | tf_op jit(solution)/shard_map/ppermute | solution.py:460
  5.7 13.1 %all-to-all-start = ((bf16[8,32,512]{2,1,0:T(8,128)(2,1)}), bf16[8,32,512]{2,1,0:T(8,128)(2,1)S(1)}, u32[]{:S(2)}, u32[]{:S(2)}) async-start(bf16[8,32,512]{2,1,0:T(8,128)(2,1)} %shard_map.83), calls=%async_computation | async-start | bytes 524288 | tf_op jit(solution)/shard_map/all_to_all | solution.py:434
  12.1 12.7 %copy-start = (bf16[3,512,1024]{2,1,0:T(8,128)(2,1)S(1)}, bf16[3,512,1024]{2,1,0:T(8,128)(2,1)}, u32[]{:S(2)}) copy-start(bf16[3,512,1024]{2,1,0:T(8,128)(2,1)} %weight_ref.2) | copy-start | bytes 9437188
  18.8 7.5 %collective-permute-start.6 = (bf16[256,1024]{1,0:T(8,128)(2,1)}, bf16[256,1024]{1,0:T(8,128)(2,1)}, u32[]{:S(2)}, u32[]{:S(2)}) collective-permute-start(bf16[256,1024]{1,0:T(8,128)(2,1)} %collective-permute-done.2.refs_0_), channel_id=1, source_target_pairs={{0,1},{1,0},{2,3},{3,2},{4,5},{5,4},{6,7},{7,6},{8,9},{9,8},{10,11... | collective-permute-start | bytes 1572872 | tf_op jit(solution)/shard_map/ppermute | solution.py:472
  18.9 4.1 %collective-permute-start.5 = (bf16[64,512]{1,0:T(8,128)(2,1)S(1)}, bf16[64,512]{1,0:T(8,128)(2,1)S(1)}, u32[]{:S(2)}, u32[]{:S(2)}) collective-permute-start(bf16[64,512]{1,0:T(8,128)(2,1)S(1)} %shard_map.85.mine_ref), channel_id=1, source_target_pairs={{0,3},{1,2},{2,1},{3,0},{4,7},{5,6},{6,5},{7,4},{8,11},{9,10},{10,... | collective-permute-start | bytes 196616 | tf_op jit(solution)/shard_map/ppermute | solution.py:475
  20.6 4.3 %collective-permute-start.4 = (bf16[64,512]{1,0:T(8,128)(2,1)S(1)}, bf16[64,512]{1,0:T(8,128)(2,1)S(1)}, u32[]{:S(2)}, u32[]{:S(2)}) collective-permute-start(bf16[64,512]{1,0:T(8,128)(2,1)S(1)} %shard_map.85.mine_ref), channel_id=1, source_target_pairs={{0,2},{1,3},{2,0},{3,1},{4,6},{5,7},{6,4},{7,5},{8,10},{9,11},{10,... | collective-permute-start | bytes 196616 | tf_op jit(solution)/shard_map/ppermute | solution.py:475
  21.1 3.7 %collective-permute-start.3 = (bf16[64,512]{1,0:T(8,128)(2,1)S(1)}, bf16[64,512]{1,0:T(8,128)(2,1)S(1)}, u32[]{:S(2)}, u32[]{:S(2)}) collective-permute-start(bf16[64,512]{1,0:T(8,128)(2,1)S(1)} %shard_map.85.mine_ref), channel_id=1, source_target_pairs={{0,1},{1,0},{2,3},{3,2},{4,5},{5,4},{6,7},{7,6},{8,9},{9,8},{10,11... | collective-permute-start | bytes 196616 | tf_op jit(solution)/shard_map/ppermute | solution.py:475
  26.2 13.9 %all-to-all-start.1 = ((bf16[8,3,64,128]{3,2,1,0:T(8,128)(2,1)}), bf16[8,3,64,128]{3,2,1,0:T(8,128)(2,1)S(1)}, u32[]{:S(2)}, u32[]{:S(2)}) async-start(bf16[8,3,64,128]{3,2,1,0:T(8,128)(2,1)} %shard_map.86), calls=%async_computation.1 | async-start | bytes 786432 | tf_op jit(solution)/shard_map/all_to_all | solution.py:434
  38.4 12.9 %copy-start.1 = (bf16[1024,512]{1,0:T(8,128)(2,1)S(1)}, bf16[1024,512]{1,0:T(8,128)(2,1)}, u32[]{:S(2)}) copy-start(bf16[1024,512]{1,0:T(8,128)(2,1)} %weight_ref.3) | copy-start | bytes 3145732
  40.1 6.3 %collective-permute-start.7 = (bf16[2,256,1024]{2,1,0:T(8,128)(2,1)}, bf16[2,256,1024]{2,1,0:T(8,128)(2,1)S(1)}, u32[]{:S(2)}, u32[]{:S(2)}) collective-permute-start(bf16[2,256,1024]{2,1,0:T(8,128)(2,1)} %get-tuple-element.48), channel_id=1, source_target_pairs={{0,1},{1,0},{2,3},{3,2},{4,5},{5,4},{6,7},{7,6},{8,9},{9,8},{10,11... | collective-permute-start | bytes 3145736 | tf_op jit(solution)/shard_map/ppermute | solution.py:498
  41.1 10.2 %all-to-all-start.2 = ((bf16[8,64,128]{2,1,0:T(8,128)(2,1)}), bf16[8,64,128]{2,1,0:T(8,128)(2,1)S(1)}, u32[]{:S(2)}, u32[]{:S(2)}) async-start(bf16[8,64,128]{2,1,0:T(8,128)(2,1)} %shard_map.88), calls=%async_computation.2 | async-start | bytes 262144 | tf_op jit(solution)/shard_map/all_to_all | solution.py:434
  49.0 20.2 %copy-start.2 = (f32[256,1024]{1,0:T(8,128)S(1)}, f32[256,1024]{1,0:T(8,128)}, u32[]{:S(2)}) copy-start(f32[256,1024]{1,0:T(8,128)} %get-tuple-element.52.light_ref) | copy-start | bytes 3145732
  49.0 14.4 %collective-permute-start.8 = (bf16[256,1024]{1,0:T(8,128)(2,1)}, bf16[256,1024]{1,0:T(8,128)(2,1)S(1)}, u32[]{:S(2)}, u32[]{:S(2)}) collective-permute-start(bf16[256,1024]{1,0:T(8,128)(2,1)} %get-tuple-element.51), channel_id=1, source_target_pairs={{0,2},{1,3},{2,0},{3,1},{4,6},{5,7},{6,4},{7,5},{8,10},{9,11},{10,... | collective-permute-start | bytes 1572872 | tf_op jit(solution)/shard_map/ppermute | solution.py:511
  63.4 1.4 %collective-permute-start.9 = (bf16[2,2,32,512]{3,2,1,0:T(8,128)(2,1)S(1)}, bf16[2,2,32,512]{3,2,1,0:T(8,128)(2,1)S(1)}, u32[]{:S(2)}, u32[]{:S(2)}) collective-permute-start(bf16[2,2,32,512]{3,2,1,0:T(8,128)(2,1)S(1)} %shard_map.91), channel_id=1, source_target_pairs={{0,1},{1,0},{2,3},{3,2},{4,5},{5,4},{6,7},{7,6},{8,9},{9,8},{10,11... | collective-permute-start | bytes 393224 | tf_op jit(solution)/shard_map/ppermute | solution.py:525
  64.8 4.3 %collective-permute-start.10 = (bf16[2,32,512]{2,1,0:T(8,128)(2,1)S(1)}, bf16[2,32,512]{2,1,0:T(8,128)(2,1)S(1)}, u32[]{:S(2)}, u32[]{:S(2)}) collective-permute-start(bf16[2,32,512]{2,1,0:T(8,128)(2,1)S(1)} %shard_map.92), channel_id=1, source_target_pairs={{0,2},{1,3},{2,0},{3,1},{4,6},{5,7},{6,4},{7,5},{8,10},{9,11},{10,... | collective-permute-start | bytes 196616 | tf_op jit(solution)/shard_map/ppermute | solution.py:527

commit v11 on v10

--- a/solution.py
+++ b/solution.py
@@ -138,8 +138,9 @@
 
 
 def listed(count):
-    inner = sorted(range(count), key=lambda i: 2 * abs(2 * i + 1 - count) // count)
-    return [i ^ 1 for i in inner]
+    inner = range(count // 4, count - count // 4)
+    order = sorted(inner, key=lambda i: (abs(2 * i + 1 - count), -i))
+    return order + [i for i in reversed(range(count)) if i not in inner]
 
 
 def spots(count):

time: 70.9 us -> 70.5 us (level)
  transfers between devices with their start and end apart: 14 -> 14, of which waited for: 9 -> 8; matrix products, arithmetic and copies ran while one was open for 0% -> 0% of each run, Pallas kernels for 27% -> 28%
where the time goes in v11:
time: 70.5 us; the launch traced here: 70 us
  starting transfers between devices  26.6 us (38%)
  Pallas kernels  20.6 us (29%)
  blocking collectives  11.4 us (16%)
  waiting for transfers between devices  11.3 us (16%)
    pallas_call x12, Pallas kernels, on_chip(): pl.pallas_call(kernel, in_specs=[pl.BlockSpec(memory_space=pl.ANY)] * len...  20.6 us
    all_to_all x3, starting transfers between devices, swap(): lax.all_to_all(x, 'seq', split_axis=0, concat_axis=0, tiled=True, axis_in...  17 us
    all_to_all x1, blocking collectives, swap(): lax.all_to_all(x, 'seq', split_axis=0, concat_axis=0, tiled=True, axis_in...  11.4 us
    ppermute x3, waiting for transfers between devices, one_head_a_device(): lax.ppermute(mine, 'head', p)  3.69 us
    all_to_all x3, waiting for transfers between devices, swap(): lax.all_to_all(x, 'seq', split_axis=0, concat_axis=0, tiled=True, axis_in...  3.23 us
    ppermute x1, starting transfers between devices, one_head_a_device(): token_far = lax.ppermute(tokens, 'head', across)  2.94 us
    ppermute x1, waiting for transfers between devices, one_head_a_device(): last = lax.ppermute(far, 'head', across)  2.45 us
    ppermute x3, starting transfers between devices, one_head_a_device(): lax.ppermute(mine, 'head', p)  2.2 us
  transfers between devices with their start and end apart: 14, of which 8 were waited for; matrix products, arithmetic and copies ran while one was open for 0% of the time, Pallas kernels for 28%

profile of v11, /device:TPU:0, one launch (start us, length us, event | category | flops | bytes accessed | tf_op | source)
XLA Modules:
  0.0 70.0 jit_solution(17470267762212098708)
XLA Ops:
  0.0 0.5 collective-permute-start.1
  0.5 1.4 %shard_map.82 = (bf16[32,1024]{1,0:T(8,128)(2,1)S(1)}, bf16[32,1024]{1,0:T(8,128)(2,1)S(1)}, bf16[64,256]{1,0:T(8,128)(2,1)S(1)}, bf16[64,256]{1,0:T(8,128)(2,1)...) custom-call(bf16[256,1024]{1,0:T(8,128)(2,1)} %refs_0_, s32[8,32]{1,0:T(8,128)} %query_hbm.1, ...), custom_call_target="tpu_custom_call" | custom-call | tf_op jit(solution)/shard_map/pallas_call | solution.py:126
  1.9 0.1 collective-permute-start
  2.0 2.9 %collective-permute-start.2 = (bf16[256,1024]{1,0:T(8,128)(2,1)}, bf16[256,1024]{1,0:T(8,128)(2,1)}, u32[]{:S(2)}, u32[]{:S(2)}) collective-permute-start(bf16[256,1024]{1,0:T(8,128)(2,1)} %refs_0_), channel_id=1, source_target_pairs={{0,2},{1,3},{2,0},{3,1},{4,6},{5,7},{6,4},{7,5},{8,10},{9,11},{10,... | collective-permute-start | bytes 1572872 | tf_op jit(solution)/shard_map/ppermute | solution.py:461
  5.0 0.0 collective-permute-done.got_ref
  5.0 0.7 %shard_map.83 = bf16[8,32,512]{2,1,0:T(8,128)(2,1)} custom-call(bf16[32,1024]{1,0:T(8,128)(2,1)S(1)} %get-tuple-element.32.keep_ref, bf16[32,1024]{1,0:T(8,128)(2,1)S(1)} %collective-permute-done.got_ref), custom_call_target="tpu_custom_call" | custom-call | tf_op jit(solution)/shard_map/pallas_call | solution.py:126
  5.7 0.0 collective-permute-done.1.refs_1_
  5.7 6.4 %all-to-all-start = ((bf16[8,32,512]{2,1,0:T(8,128)(2,1)}), bf16[8,32,512]{2,1,0:T(8,128)(2,1)S(1)}, u32[]{:S(2)}, u32[]{:S(2)}) async-start(bf16[8,32,512]{2,1,0:T(8,128)(2,1)} %shard_map.83), calls=%async_computation | async-start | bytes 524288 | tf_op jit(solution)/shard_map/all_to_all | solution.py:435
  12.1 0.0 copy-start
  12.1 4.8 %shard_map.84.refs_3_ = f32[3,256,256]{2,1,0:T(8,128)} custom-call(bf16[256,1024]{1,0:T(8,128)(2,1)} %refs_0_, bf16[256,1024]{1,0:T(8,128)(2,1)} %collective-permute-done.1.refs_1_, bf16[3,4096,256]{2,1,0:T(8,128)(2,1)} %refs_2_.3), custom_call_target="tpu_custom_call" | custom-call | flops 805306368 | tf_op jit(solution)/shard_map/pallas_call | solution.py:126
  16.9 0.5 collective-permute-done.2.refs_0_
  17.4 1.3 %all-to-all-done.slots_ref = bf16[8,32,512]{2,1,0:T(8,128)(2,1)S(1)} async-done(((bf16[8,32,512]{2,1,0:T(8,128)(2,1)}), bf16[8,32,512]{2,1,0:T(8,128)(2,1)S(1)}, u32[]{:S(2)}, u32[]{:S(2)}) %all-to-all-start) | async-done | bytes 262176 | tf_op jit(solution)/shard_map/all_to_all | solution.py:435
  18.8 0.0 collective-permute-start.6
  18.8 0.2 shard_map.85.mine_ref
  18.9 1.6 %collective-permute-start.5 = (bf16[64,512]{1,0:T(8,128)(2,1)S(1)}, bf16[64,512]{1,0:T(8,128)(2,1)S(1)}, u32[]{:S(2)}, u32[]{:S(2)}) collective-permute-start(bf16[64,512]{1,0:T(8,128)(2,1)S(1)} %shard_map.85.mine_ref), channel_id=1, source_target_pairs={{0,3},{1,2},{2,1},{3,0},{4,7},{5,6},{6,5},{7,4},{8,11},{9,10},{10,... | collective-permute-start | bytes 196616 | tf_op jit(solution)/shard_map/ppermute | solution.py:476
  20.6 0.6 collective-permute-start.4
  21.1 0.0 collective-permute-start.3
  21.1 1.9 %collective-permute-done.5.last_ref = bf16[64,512]{1,0:T(8,128)(2,1)S(1)} collective-permute-done((bf16[64,512]{1,0:T(8,128)(2,1)S(1)}, bf16[64,512]{1,0:T(8,128)(2,1)S(1)}, u32[]{:S(2)}, u32[]{:S(2)}) %collective-permute-start.5) | collective-permute-done | bytes 65568 | tf_op jit(solution)/shard_map/ppermute | solution.py:476
  23.0 1.8 %collective-permute-done.4.across_ref = bf16[64,512]{1,0:T(8,128)(2,1)S(1)} collective-permute-done((bf16[64,512]{1,0:T(8,128)(2,1)S(1)}, bf16[64,512]{1,0:T(8,128)(2,1)S(1)}, u32[]{:S(2)}, u32[]{:S(2)}) %collective-permute-start.4) | collective-permute-done | bytes 65568 | tf_op jit(solution)/shard_map/ppermute | solution.py:476
  24.8 0.0 collective-permute-done.3.pair_ref
  24.8 0.0 copy-done
  24.8 1.4 %shard_map.86 = bf16[8,3,64,128]{3,2,1,0:T(8,128)(2,1)} custom-call(bf16[64,512]{1,0:T(8,128)(2,1)S(1)} %shard_map.85.mine_ref, bf16[64,512]{1,0:T(8,128)(2,1)S(1)} %collective-permute-done.3.pair_ref, bf16[64,512]{1,0:T(8,128)(2,1)S(1)} %collective-permute-done.4.across_ref, bf16[64,512]{1,0:T(8,128)(2,1)S(1)} %collective-permute-done.5.last_ref, ...), custom_call_target="tpu_custom_call" | custom-call | tf_op jit(solution)/shard_map/pallas_call | solution.py:126
  26.2 0.0 collective-permute-done.6.refs_1_
  26.2 5.4 %all-to-all-start.1 = ((bf16[8,3,64,128]{3,2,1,0:T(8,128)(2,1)}), bf16[8,3,64,128]{3,2,1,0:T(8,128)(2,1)S(1)}, u32[]{:S(2)}, u32[]{:S(2)}) async-start(bf16[8,3,64,128]{3,2,1,0:T(8,128)(2,1)} %shard_map.86), calls=%async_computation.1 | async-start | bytes 786432 | tf_op jit(solution)/shard_map/all_to_all | solution.py:435
  31.6 6.8 %shard_map.87 = (bf16[256,256]{1,0:T(8,128)(2,1)S(1)}, bf16[2,256,1024]{2,1,0:T(8,128)(2,1)}) custom-call(bf16[256,1024]{1,0:T(8,128)(2,1)} %collective-permute-done.2.refs_0_, bf16[256,1024]{1,0:T(8,128)(2,1)} %collective-permute-done.6.refs_1_, bf16[3,4096,256]{2,1,0:T(8,128)(2,1)} %refs_2_.3, f32[3,256,256]{2,1,0:T(8,128)} %shard_map.84.refs_3_, ...), custom_call_target="tpu_custom_call" | custom-call | flops 805306368 | tf_op jit(solution)/shard_map/pallas_call | solution.py:126
  38.4 0.0 copy-start.1
  38.4 1.6 %all-to-all-done.1.parts_ref = bf16[8,3,64,128]{3,2,1,0:T(8,128)(2,1)S(1)} async-done(((bf16[8,3,64,128]{3,2,1,0:T(8,128)(2,1)}), bf16[8,3,64,128]{3,2,1,0:T(8,128)(2,1)S(1)}, u32[]{:S(2)}, u32[]{:S(2)}) %all-to-all-start.1) | async-done | bytes 393248 | tf_op jit(solution)/shard_map/all_to_all | solution.py:435
  40.0 0.0 collective-permute-start.7
  40.0 1.0 %shard_map.88 = bf16[8,64,128]{2,1,0:T(8,128)(2,1)} custom-call(bf16[8,3,64,128]{3,2,1,0:T(8,128)(2,1)S(1)} %all-to-all-done.1.parts_ref), custom_call_target="tpu_custom_call" | custom-call | tf_op jit(solution)/shard_map/pallas_call | solution.py:126
  41.0 5.3 %all-to-all-start.2 = ((bf16[8,64,128]{2,1,0:T(8,128)(2,1)}), bf16[8,64,128]{2,1,0:T(8,128)(2,1)S(1)}, u32[]{:S(2)}, u32[]{:S(2)}) async-start(bf16[8,64,128]{2,1,0:T(8,128)(2,1)} %shard_map.88), calls=%async_computation.2 | async-start | bytes 262144 | tf_op jit(solution)/shard_map/all_to_all | solution.py:435
  46.3 0.0 collective-permute-done.7.got_ref
  46.3 2.5 %shard_map.89 = (f32[256,1024]{1,0:T(8,128)}, bf16[256,1024]{1,0:T(8,128)(2,1)}) custom-call(bf16[256,4096]{1,0:T(8,128)(2,1)} %w_out.1, bf16[2,256,1024]{2,1,0:T(8,128)(2,1)S(1)} %collective-permute-done.7.got_ref, bf16[256,256]{1,0:T(8,128)(2,1)S(1)} %get-tuple-element.49.heads_ref), custom_call_target="tpu_custom_call" | custom-call | flops 268435456 | tf_op jit(solution)/shard_map/pallas_call | solution.py:126
  48.8 0.0 copy-start.2
  48.8 1.9 %collective-permute-start.8 = (bf16[256,1024]{1,0:T(8,128)(2,1)}, bf16[256,1024]{1,0:T(8,128)(2,1)S(1)}, u32[]{:S(2)}, u32[]{:S(2)}) collective-permute-start(bf16[256,1024]{1,0:T(8,128)(2,1)} %get-tuple-element.51), channel_id=1, source_target_pairs={{0,2},{1,3},{2,0},{3,1},{4,6},{5,7},{6,4},{7,5},{8,10},{9,11},{10,... | collective-permute-start | bytes 1572872 | tf_op jit(solution)/shard_map/ppermute | solution.py:512
  50.7 0.3 all-to-all-done.2.heads_ref
  51.0 0.0 copy-done.1
  51.0 0.5 shard_map.90
  51.5 11.4 %all_to_all.20.back_ref = bf16[8,32,512]{2,1,0:T(8,128)(2,1)S(1)} all-to-all(bf16[8,32,512]{2,1,0:T(8,128)(2,1)S(1)} %shard_map.90), channel_id=1, replica_groups={{16,12,20,8,28,24,4,0},{17,13,21,9,29,25,5,1},{18,14,22,10,30,26,6,2},{..., dimensions={0} | all-to-all | bytes 524288 | tf_op jit(solution)/shard_map/all_to_all | solution.py:435
  62.9 0.0 collective-permute-done.8.light_far_ref
  63.0 0.1 collective-permute-start.9
  63.0 1.3 %collective-permute-done.9.got_ref = bf16[2,2,32,512]{3,2,1,0:T(8,128)(2,1)S(1)} collective-permute-done((bf16[2,2,32,512]{3,2,1,0:T(8,128)(2,1)S(1)}, bf16[2,2,32,512]{3,2,1,0:T(8,128)(2,1)S(1)}, u32[]{:S(2)}, u32[]{:S(2)}) %collective-permute-start.9) | collective-permute-done | bytes 131104 | tf_op jit(solution)/shard_map/ppermute | solution.py:526
  64.4 1.9 %collective-permute-start.10 = (bf16[2,32,512]{2,1,0:T(8,128)(2,1)S(1)}, bf16[2,32,512]{2,1,0:T(8,128)(2,1)S(1)}, u32[]{:S(2)}, u32[]{:S(2)}) collective-permute-start(bf16[2,32,512]{2,1,0:T(8,128)(2,1)S(1)} %shard_map.92), channel_id=1, source_target_pairs={{0,2},{1,3},{2,0},{3,1},{4,6},{5,7},{6,4},{7,5},{8,10},{9,11},{10,... | collective-permute-start | bytes 196616 | tf_op jit(solution)/shard_map/ppermute | solution.py:528
  66.3 2.5 %collective-permute-done.10.last_ref = bf16[2,32,512]{2,1,0:T(8,128)(2,1)S(1)} collective-permute-done((bf16[2,32,512]{2,1,0:T(8,128)(2,1)S(1)}, bf16[2,32,512]{2,1,0:T(8,128)(2,1)S(1)}, u32[]{:S(2)}, u32[]{:S(2)}) %collective-permute-start.10) | collective-permute-done | bytes 65568 | tf_op jit(solution)/shard_map/ppermute | solution.py:528
  68.7 0.0 copy-done.2
  68.7 1.3 %shard_map.93 = bf16[256,1024]{1,0:T(8,128)(2,1)} custom-call(f32[256,1024]{1,0:T(8,128)S(1)} %copy-done.2, bf16[256,1024]{1,0:T(8,128)(2,1)S(1)} %collective-permute-done.8.light_far_ref, bf16[8,32,512]{2,1,0:T(8,128)(2,1)S(1)} %all_to_all.20.back_ref, bf16[2,2,32,512]{3,2,1,0:T(8,128)(2,1)S(1)} %collective-permute-done.9.got_ref, ...), custom_call_target="tpu_custom_call" | custom-call | tf_op jit(solution)/shard_map/pallas_call | solution.py:126
  (2 shorter events, 0.0 us)
Async XLA Ops:
  0.0 5.7 %collective-permute-start.1 = (bf16[256,1024]{1,0:T(8,128)(2,1)}, bf16[256,1024]{1,0:T(8,128)(2,1)}, u32[]{:S(2)}, u32[]{:S(2)}) collective-permute-start(bf16[256,1024]{1,0:T(8,128)(2,1)} %refs_0_), channel_id=1, source_target_pairs={{0,1},{1,0},{2,3},{3,2},{4,5},{5,4},{6,7},{7,6},{8,9},{9,8},{10,11... | collective-permute-start | bytes 1572872 | tf_op jit(solution)/shard_map/ppermute | solution.py:462
  1.9 3.1 %collective-permute-start = (bf16[32,1024]{1,0:T(8,128)(2,1)S(1)}, bf16[32,1024]{1,0:T(8,128)(2,1)S(1)}, u32[]{:S(2)}, u32[]{:S(2)}) collective-permute-start(bf16[32,1024]{1,0:T(8,128)(2,1)S(1)} %get-tuple-element.33), channel_id=1, source_target_pairs={{0,1},{1,0},{2,3},{3,2},{4,5},{5,4},{6,7},{7,6},{8,9},{9,8},{10,11... | collective-permute-start | bytes 196616 | tf_op jit(solution)/shard_map/ppermute | solution.py:459
  2.0 15.4 %collective-permute-start.2 = (bf16[256,1024]{1,0:T(8,128)(2,1)}, bf16[256,1024]{1,0:T(8,128)(2,1)}, u32[]{:S(2)}, u32[]{:S(2)}) collective-permute-start(bf16[256,1024]{1,0:T(8,128)(2,1)} %refs_0_), channel_id=1, source_target_pairs={{0,2},{1,3},{2,0},{3,1},{4,6},{5,7},{6,4},{7,5},{8,10},{9,11},{10,... | collective-permute-start | bytes 1572872 | tf_op jit(solution)/shard_map/ppermute | solution.py:461
  5.7 13.1 %all-to-all-start = ((bf16[8,32,512]{2,1,0:T(8,128)(2,1)}), bf16[8,32,512]{2,1,0:T(8,128)(2,1)S(1)}, u32[]{:S(2)}, u32[]{:S(2)}) async-start(bf16[8,32,512]{2,1,0:T(8,128)(2,1)} %shard_map.83), calls=%async_computation | async-start | bytes 524288 | tf_op jit(solution)/shard_map/all_to_all | solution.py:435
  12.1 12.7 %copy-start = (bf16[3,512,1024]{2,1,0:T(8,128)(2,1)S(1)}, bf16[3,512,1024]{2,1,0:T(8,128)(2,1)}, u32[]{:S(2)}) copy-start(bf16[3,512,1024]{2,1,0:T(8,128)(2,1)} %weight_ref.2) | copy-start | bytes 9437188
  18.8 7.5 %collective-permute-start.6 = (bf16[256,1024]{1,0:T(8,128)(2,1)}, bf16[256,1024]{1,0:T(8,128)(2,1)}, u32[]{:S(2)}, u32[]{:S(2)}) collective-permute-start(bf16[256,1024]{1,0:T(8,128)(2,1)} %collective-permute-done.2.refs_0_), channel_id=1, source_target_pairs={{0,1},{1,0},{2,3},{3,2},{4,5},{5,4},{6,7},{7,6},{8,9},{9,8},{10,11... | collective-permute-start | bytes 1572872 | tf_op jit(solution)/shard_map/ppermute | solution.py:473
  18.9 4.1 %collective-permute-start.5 = (bf16[64,512]{1,0:T(8,128)(2,1)S(1)}, bf16[64,512]{1,0:T(8,128)(2,1)S(1)}, u32[]{:S(2)}, u32[]{:S(2)}) collective-permute-start(bf16[64,512]{1,0:T(8,128)(2,1)S(1)} %shard_map.85.mine_ref), channel_id=1, source_target_pairs={{0,3},{1,2},{2,1},{3,0},{4,7},{5,6},{6,5},{7,4},{8,11},{9,10},{10,... | collective-permute-start | bytes 196616 | tf_op jit(solution)/shard_map/ppermute | solution.py:476
  20.6 4.3 %collective-permute-start.4 = (bf16[64,512]{1,0:T(8,128)(2,1)S(1)}, bf16[64,512]{1,0:T(8,128)(2,1)S(1)}, u32[]{:S(2)}, u32[]{:S(2)}) collective-permute-start(bf16[64,512]{1,0:T(8,128)(2,1)S(1)} %shard_map.85.mine_ref), channel_id=1, source_target_pairs={{0,2},{1,3},{2,0},{3,1},{4,6},{5,7},{6,4},{7,5},{8,10},{9,11},{10,... | collective-permute-start | bytes 196616 | tf_op jit(solution)/shard_map/ppermute | solution.py:476
  21.1 3.7 %collective-permute-start.3 = (bf16[64,512]{1,0:T(8,128)(2,1)S(1)}, bf16[64,512]{1,0:T(8,128)(2,1)S(1)}, u32[]{:S(2)}, u32[]{:S(2)}) collective-permute-start(bf16[64,512]{1,0:T(8,128)(2,1)S(1)} %shard_map.85.mine_ref), channel_id=1, source_target_pairs={{0,1},{1,0},{2,3},{3,2},{4,5},{5,4},{6,7},{7,6},{8,9},{9,8},{10,11... | collective-permute-start | bytes 196616 | tf_op jit(solution)/shard_map/ppermute | solution.py:476
  26.2 13.7 %all-to-all-start.1 = ((bf16[8,3,64,128]{3,2,1,0:T(8,128)(2,1)}), bf16[8,3,64,128]{3,2,1,0:T(8,128)(2,1)S(1)}, u32[]{:S(2)}, u32[]{:S(2)}) async-start(bf16[8,3,64,128]{3,2,1,0:T(8,128)(2,1)} %shard_map.86), calls=%async_computation.1 | async-start | bytes 786432 | tf_op jit(solution)/shard_map/all_to_all | solution.py:435
  38.4 12.6 %copy-start.1 = (bf16[1024,512]{1,0:T(8,128)(2,1)S(1)}, bf16[1024,512]{1,0:T(8,128)(2,1)}, u32[]{:S(2)}) copy-start(bf16[1024,512]{1,0:T(8,128)(2,1)} %weight_ref.3) | copy-start | bytes 3145732
  40.0 6.3 %collective-permute-start.7 = (bf16[2,256,1024]{2,1,0:T(8,128)(2,1)}, bf16[2,256,1024]{2,1,0:T(8,128)(2,1)S(1)}, u32[]{:S(2)}, u32[]{:S(2)}) collective-permute-start(bf16[2,256,1024]{2,1,0:T(8,128)(2,1)} %get-tuple-element.48), channel_id=1, source_target_pairs={{0,1},{1,0},{2,3},{3,2},{4,5},{5,4},{6,7},{7,6},{8,9},{9,8},{10,11... | collective-permute-start | bytes 3145736 | tf_op jit(solution)/shard_map/ppermute | solution.py:499
  41.0 10.0 %all-to-all-start.2 = ((bf16[8,64,128]{2,1,0:T(8,128)(2,1)}), bf16[8,64,128]{2,1,0:T(8,128)(2,1)S(1)}, u32[]{:S(2)}, u32[]{:S(2)}) async-start(bf16[8,64,128]{2,1,0:T(8,128)(2,1)} %shard_map.88), calls=%async_computation.2 | async-start | bytes 262144 | tf_op jit(solution)/shard_map/all_to_all | solution.py:435
  48.8 19.9 %copy-start.2 = (f32[256,1024]{1,0:T(8,128)S(1)}, f32[256,1024]{1,0:T(8,128)}, u32[]{:S(2)}) copy-start(f32[256,1024]{1,0:T(8,128)} %get-tuple-element.52.light_ref) | copy-start | bytes 3145732
  48.8 14.2 %collective-permute-start.8 = (bf16[256,1024]{1,0:T(8,128)(2,1)}, bf16[256,1024]{1,0:T(8,128)(2,1)S(1)}, u32[]{:S(2)}, u32[]{:S(2)}) collective-permute-start(bf16[256,1024]{1,0:T(8,128)(2,1)} %get-tuple-element.51), channel_id=1, source_target_pairs={{0,2},{1,3},{2,0},{3,1},{4,6},{5,7},{6,4},{7,5},{8,10},{9,11},{10,... | collective-permute-start | bytes 1572872 | tf_op jit(solution)/shard_map/ppermute | solution.py:512
  63.0 1.4 %collective-permute-start.9 = (bf16[2,2,32,512]{3,2,1,0:T(8,128)(2,1)S(1)}, bf16[2,2,32,512]{3,2,1,0:T(8,128)(2,1)S(1)}, u32[]{:S(2)}, u32[]{:S(2)}) collective-permute-start(bf16[2,2,32,512]{3,2,1,0:T(8,128)(2,1)S(1)} %shard_map.91), channel_id=1, source_target_pairs={{0,1},{1,0},{2,3},{3,2},{4,5},{5,4},{6,7},{7,6},{8,9},{9,8},{10,11... | collective-permute-start | bytes 393224 | tf_op jit(solution)/shard_map/ppermute | solution.py:526
  64.4 4.3 %collective-permute-start.10 = (bf16[2,32,512]{2,1,0:T(8,128)(2,1)S(1)}, bf16[2,32,512]{2,1,0:T(8,128)(2,1)S(1)}, u32[]{:S(2)}, u32[]{:S(2)}) collective-permute-start(bf16[2,32,512]{2,1,0:T(8,128)(2,1)S(1)} %shard_map.92), channel_id=1, source_target_pairs={{0,2},{1,3},{2,0},{3,1},{4,6},{5,7},{6,4},{7,5},{8,10},{9,11},{10,... | collective-permute-start | bytes 196616 | tf_op jit(solution)/shard_map/ppermute | solution.py:528

commit v12 on v11

--- a/solution.py
+++ b/solution.py
@@ -306,8 +306,20 @@
         out_ref[i] = (mine + got_ref[1, i].astype(F32)).astype(BF)
 
 
+def merge_kernel(own, far, out_ref, far_ref, sems):
+    copies = [
+        pltpu.make_async_copy(own, out_ref, sems.at[0]),
+        pltpu.make_async_copy(far, far_ref, sems.at[1]),
+    ]
+    for copy in copies:
+        copy.start()
+    for copy in copies:
+        copy.wait()
+    out_ref[...] = out_ref[...] + far_ref[...].astype(F32)
+
+
 def finish_kernel(
-    light_ref, light_far_ref, back_ref, got_ref, last_ref, own_map_ref, gate_ref, out_ref
+    light_ref, back_ref, got_ref, last_ref, own_map_ref, gate_ref, out_ref
 ):
     head = lax.axis_index("head")
     per = last_ref.shape[0]
@@ -322,8 +334,7 @@
             chosen, fine, preferred_element_type=F32
         )
         cols = slice(j * width, (j + 1) * width)
-        light = light_ref[:, cols] + light_far_ref[:, cols].astype(F32)
-        out_ref[:, cols] = (light + added).astype(BF)
+        out_ref[:, cols] = (light_ref[:, cols] + added).astype(BF)
 
 
 def light_kernel(flips, last, *refs):
@@ -523,14 +534,20 @@
     back = swap(back)
     back, light_far = lax.optimization_barrier((back, light_far))
     give = on_chip(give_kernel, [((2, per, slots, out_cols), BF)], back)
+    give, light_own, light_far = lax.optimization_barrier((give, light_own, light_far))
+    light = on_chip(
+        merge_kernel,
+        [((tok_rows, own_width), F32)],
+        hbm=(light_own, light_far),
+        scratch=[pltpu.VMEM((tok_rows, own_width), BF), pltpu.SemaphoreType.DMA((2,))],
+    )
     got = lax.ppermute(give, "head", pair)
     far = on_chip(far_kernel, [((per, slots, out_cols), BF)], back, got)
     last = lax.ppermute(far, "head", across)
     return on_chip(
         finish_kernel,
         [((tok_rows, own_width), BF)],
-        light_own,
-        light_far,
+        light,
         back,
         got,
         last,

time: 70.5 us -> 70.5 us (level)
  waiting for transfers between devices: 11.3 us -> 9.78 us
  Pallas kernels: 20.6 us -> 22.1 us
    ppermute x1, waiting for transfers between devices: 2.45 us -> 0.97 us  [one_head_a_device(): last = lax.ppermute(far, 'head', across)]
    pallas_call x12 -> x13, Pallas kernels: 20.6 us -> 22.1 us  [on_chip(): pl.pallas_call(kernel, in_specs=[pl.BlockSpec(memory_space=pl.ANY)] * len...]
  transfers between devices with their start and end apart: 14 -> 14, of which waited for: 8 -> 8; matrix products, arithmetic and copies ran while one was open for 0% -> 0% of each run, Pallas kernels for 28% -> 30%
where the time goes in v12:
time: 70.5 us; the launch traced here: 70 us
  starting transfers between devices  26.6 us (38%)
  Pallas kernels  22.1 us (31%)
  blocking collectives  11.4 us (16%)
  waiting for transfers between devices  9.78 us (14%)
    pallas_call x13, Pallas kernels, on_chip(): pl.pallas_call(kernel, in_specs=[pl.BlockSpec(memory_space=pl.ANY)] * len...  22.1 us
    all_to_all x3, starting transfers between devices, swap(): lax.all_to_all(x, 'seq', split_axis=0, concat_axis=0, tiled=True, axis_in...  17 us
    all_to_all x1, blocking collectives, swap(): lax.all_to_all(x, 'seq', split_axis=0, concat_axis=0, tiled=True, axis_in...  11.4 us
    ppermute x3, waiting for transfers between devices, one_head_a_device(): lax.ppermute(mine, 'head', p)  3.69 us
    all_to_all x3, waiting for transfers between devices, swap(): lax.all_to_all(x, 'seq', split_axis=0, concat_axis=0, tiled=True, axis_in...  3.24 us
    ppermute x1, starting transfers between devices, one_head_a_device(): token_far = lax.ppermute(tokens, 'head', across)  2.94 us
    ppermute x3, starting transfers between devices, one_head_a_device(): lax.ppermute(mine, 'head', p)  2.2 us
    ppermute x1, starting transfers between devices, one_head_a_device(): far_sent = lax.ppermute(light_far, 'head', across)  1.91 us
  transfers between devices with their start and end apart: 14, of which 8 were waited for; matrix products, arithmetic and copies ran while one was open for 0% of the time, Pallas kernels for 30%

profile of v12, /device:TPU:0, one launch (start us, length us, event | category | flops | bytes accessed | tf_op | source)
XLA Modules:
  0.0 70.0 jit_solution(2495797591607400685)
XLA Ops:
  0.0 0.5 collective-permute-start.1
  0.5 1.4 %shard_map.82 = (bf16[32,1024]{1,0:T(8,128)(2,1)S(1)}, bf16[32,1024]{1,0:T(8,128)(2,1)S(1)}, bf16[64,256]{1,0:T(8,128)(2,1)S(1)}, bf16[64,256]{1,0:T(8,128)(2,1)...) custom-call(bf16[256,1024]{1,0:T(8,128)(2,1)} %refs_0_, s32[8,32]{1,0:T(8,128)} %query_hbm.1, ...), custom_call_target="tpu_custom_call" | custom-call | tf_op jit(solution)/shard_map/pallas_call | solution.py:126
  1.9 0.1 collective-permute-start
  2.0 2.9 %collective-permute-start.2 = (bf16[256,1024]{1,0:T(8,128)(2,1)}, bf16[256,1024]{1,0:T(8,128)(2,1)}, u32[]{:S(2)}, u32[]{:S(2)}) collective-permute-start(bf16[256,1024]{1,0:T(8,128)(2,1)} %refs_0_), channel_id=1, source_target_pairs={{0,2},{1,3},{2,0},{3,1},{4,6},{5,7},{6,4},{7,5},{8,10},{9,11},{10,... | collective-permute-start | bytes 1572872 | tf_op jit(solution)/shard_map/ppermute | solution.py:472
  5.0 0.0 collective-permute-done.got_ref
  5.0 0.7 %shard_map.83 = bf16[8,32,512]{2,1,0:T(8,128)(2,1)} custom-call(bf16[32,1024]{1,0:T(8,128)(2,1)S(1)} %get-tuple-element.35.keep_ref, bf16[32,1024]{1,0:T(8,128)(2,1)S(1)} %collective-permute-done.got_ref), custom_call_target="tpu_custom_call" | custom-call | tf_op jit(solution)/shard_map/pallas_call | solution.py:126
  5.7 0.0 collective-permute-done.1.refs_1_
  5.7 6.4 %all-to-all-start = ((bf16[8,32,512]{2,1,0:T(8,128)(2,1)}), bf16[8,32,512]{2,1,0:T(8,128)(2,1)S(1)}, u32[]{:S(2)}, u32[]{:S(2)}) async-start(bf16[8,32,512]{2,1,0:T(8,128)(2,1)} %shard_map.83), calls=%async_computation | async-start | bytes 524288 | tf_op jit(solution)/shard_map/all_to_all | solution.py:446
  12.1 0.0 copy-start
  12.1 4.8 %shard_map.84.refs_3_ = f32[3,256,256]{2,1,0:T(8,128)} custom-call(bf16[256,1024]{1,0:T(8,128)(2,1)} %refs_0_, bf16[256,1024]{1,0:T(8,128)(2,1)} %collective-permute-done.1.refs_1_, bf16[3,4096,256]{2,1,0:T(8,128)(2,1)} %refs_2_.3), custom_call_target="tpu_custom_call" | custom-call | flops 805306368 | tf_op jit(solution)/shard_map/pallas_call | solution.py:126
  16.9 0.5 collective-permute-done.2.refs_0_
  17.4 1.3 %all-to-all-done.slots_ref = bf16[8,32,512]{2,1,0:T(8,128)(2,1)S(1)} async-done(((bf16[8,32,512]{2,1,0:T(8,128)(2,1)}), bf16[8,32,512]{2,1,0:T(8,128)(2,1)S(1)}, u32[]{:S(2)}, u32[]{:S(2)}) %all-to-all-start) | async-done | bytes 262176 | tf_op jit(solution)/shard_map/all_to_all | solution.py:446
  18.8 0.0 collective-permute-start.6
  18.8 0.2 shard_map.85.mine_ref
  18.9 1.6 %collective-permute-start.5 = (bf16[64,512]{1,0:T(8,128)(2,1)S(1)}, bf16[64,512]{1,0:T(8,128)(2,1)S(1)}, u32[]{:S(2)}, u32[]{:S(2)}) collective-permute-start(bf16[64,512]{1,0:T(8,128)(2,1)S(1)} %shard_map.85.mine_ref), channel_id=1, source_target_pairs={{0,3},{1,2},{2,1},{3,0},{4,7},{5,6},{6,5},{7,4},{8,11},{9,10},{10,... | collective-permute-start | bytes 196616 | tf_op jit(solution)/shard_map/ppermute | solution.py:487
  20.6 0.6 collective-permute-start.4
  21.1 0.0 collective-permute-start.3
  21.1 1.9 %collective-permute-done.5.last_ref = bf16[64,512]{1,0:T(8,128)(2,1)S(1)} collective-permute-done((bf16[64,512]{1,0:T(8,128)(2,1)S(1)}, bf16[64,512]{1,0:T(8,128)(2,1)S(1)}, u32[]{:S(2)}, u32[]{:S(2)}) %collective-permute-start.5) | collective-permute-done | bytes 65568 | tf_op jit(solution)/shard_map/ppermute | solution.py:487
  23.0 1.8 %collective-permute-done.4.across_ref = bf16[64,512]{1,0:T(8,128)(2,1)S(1)} collective-permute-done((bf16[64,512]{1,0:T(8,128)(2,1)S(1)}, bf16[64,512]{1,0:T(8,128)(2,1)S(1)}, u32[]{:S(2)}, u32[]{:S(2)}) %collective-permute-start.4) | collective-permute-done | bytes 65568 | tf_op jit(solution)/shard_map/ppermute | solution.py:487
  24.8 0.0 collective-permute-done.3.pair_ref
  24.8 0.0 copy-done
  24.8 1.4 %shard_map.86 = bf16[8,3,64,128]{3,2,1,0:T(8,128)(2,1)} custom-call(bf16[64,512]{1,0:T(8,128)(2,1)S(1)} %shard_map.85.mine_ref, bf16[64,512]{1,0:T(8,128)(2,1)S(1)} %collective-permute-done.3.pair_ref, bf16[64,512]{1,0:T(8,128)(2,1)S(1)} %collective-permute-done.4.across_ref, bf16[64,512]{1,0:T(8,128)(2,1)S(1)} %collective-permute-done.5.last_ref, ...), custom_call_target="tpu_custom_call" | custom-call | tf_op jit(solution)/shard_map/pallas_call | solution.py:126
  26.2 0.0 collective-permute-done.6.refs_1_
  26.2 5.4 %all-to-all-start.1 = ((bf16[8,3,64,128]{3,2,1,0:T(8,128)(2,1)}), bf16[8,3,64,128]{3,2,1,0:T(8,128)(2,1)S(1)}, u32[]{:S(2)}, u32[]{:S(2)}) async-start(bf16[8,3,64,128]{3,2,1,0:T(8,128)(2,1)} %shard_map.86), calls=%async_computation.1 | async-start | bytes 786432 | tf_op jit(solution)/shard_map/all_to_all | solution.py:446
  31.6 6.8 %shard_map.87 = (bf16[256,256]{1,0:T(8,128)(2,1)S(1)}, bf16[2,256,1024]{2,1,0:T(8,128)(2,1)}) custom-call(bf16[256,1024]{1,0:T(8,128)(2,1)} %collective-permute-done.2.refs_0_, bf16[256,1024]{1,0:T(8,128)(2,1)} %collective-permute-done.6.refs_1_, bf16[3,4096,256]{2,1,0:T(8,128)(2,1)} %refs_2_.3, f32[3,256,256]{2,1,0:T(8,128)} %shard_map.84.refs_3_, ...), custom_call_target="tpu_custom_call" | custom-call | flops 805306368 | tf_op jit(solution)/shard_map/pallas_call | solution.py:126
  38.4 0.0 copy-start.1
  38.4 1.6 %all-to-all-done.1.parts_ref = bf16[8,3,64,128]{3,2,1,0:T(8,128)(2,1)S(1)} async-done(((bf16[8,3,64,128]{3,2,1,0:T(8,128)(2,1)}), bf16[8,3,64,128]{3,2,1,0:T(8,128)(2,1)S(1)}, u32[]{:S(2)}, u32[]{:S(2)}) %all-to-all-start.1) | async-done | bytes 393248 | tf_op jit(solution)/shard_map/all_to_all | solution.py:446
  40.0 0.0 collective-permute-start.7
  40.0 1.0 %shard_map.88 = bf16[8,64,128]{2,1,0:T(8,128)(2,1)} custom-call(bf16[8,3,64,128]{3,2,1,0:T(8,128)(2,1)S(1)} %all-to-all-done.1.parts_ref), custom_call_target="tpu_custom_call" | custom-call | tf_op jit(solution)/shard_map/pallas_call | solution.py:126
  41.0 5.3 %all-to-all-start.2 = ((bf16[8,64,128]{2,1,0:T(8,128)(2,1)}), bf16[8,64,128]{2,1,0:T(8,128)(2,1)S(1)}, u32[]{:S(2)}, u32[]{:S(2)}) async-start(bf16[8,64,128]{2,1,0:T(8,128)(2,1)} %shard_map.88), calls=%async_computation.2 | async-start | bytes 262144 | tf_op jit(solution)/shard_map/all_to_all | solution.py:446
  46.3 0.0 collective-permute-done.7.got_ref
  46.3 2.5 %shard_map.89 = (f32[256,1024]{1,0:T(8,128)}, bf16[256,1024]{1,0:T(8,128)(2,1)}) custom-call(bf16[256,4096]{1,0:T(8,128)(2,1)} %w_out.1, bf16[2,256,1024]{2,1,0:T(8,128)(2,1)S(1)} %collective-permute-done.7.got_ref, bf16[256,256]{1,0:T(8,128)(2,1)S(1)} %get-tuple-element.52.heads_ref), custom_call_target="tpu_custom_call" | custom-call | flops 268435456 | tf_op jit(solution)/shard_map/pallas_call | solution.py:126
  48.8 1.9 %collective-permute-start.8 = (bf16[256,1024]{1,0:T(8,128)(2,1)}, bf16[256,1024]{1,0:T(8,128)(2,1)S(1)}, u32[]{:S(2)}, u32[]{:S(2)}) collective-permute-start(bf16[256,1024]{1,0:T(8,128)(2,1)} %get-tuple-element.54), channel_id=1, source_target_pairs={{0,2},{1,3},{2,0},{3,1},{4,6},{5,7},{6,4},{7,5},{8,10},{9,11},{10,... | collective-permute-start | bytes 1572872 | tf_op jit(solution)/shard_map/ppermute | solution.py:523
  50.7 0.3 all-to-all-done.2.heads_ref
  51.0 0.0 copy-done.1
  51.0 0.5 shard_map.90
  51.5 11.4 %all_to_all.20.back_ref = bf16[8,32,512]{2,1,0:T(8,128)(2,1)S(1)} all-to-all(bf16[8,32,512]{2,1,0:T(8,128)(2,1)S(1)} %shard_map.90), channel_id=1, replica_groups={{16,12,20,8,28,24,4,0},{17,13,21,9,29,25,5,1},{18,14,22,10,30,26,6,2},{..., dimensions={0} | all-to-all | bytes 524288 | tf_op jit(solution)/shard_map/all_to_all | solution.py:446
  62.9 0.0 collective-permute-done.8.far
  62.9 0.0 copy-start.2
  62.9 0.1 collective-permute-start.9
  63.0 1.3 %collective-permute-done.9.got_ref = bf16[2,2,32,512]{3,2,1,0:T(8,128)(2,1)S(1)} collective-permute-done((bf16[2,2,32,512]{3,2,1,0:T(8,128)(2,1)S(1)}, bf16[2,2,32,512]{3,2,1,0:T(8,128)(2,1)S(1)}, u32[]{:S(2)}, u32[]{:S(2)}) %collective-permute-start.9) | collective-permute-done | bytes 131104 | tf_op jit(solution)/shard_map/ppermute | solution.py:544
  64.4 1.9 %collective-permute-start.10 = (bf16[2,32,512]{2,1,0:T(8,128)(2,1)S(1)}, bf16[2,32,512]{2,1,0:T(8,128)(2,1)S(1)}, u32[]{:S(2)}, u32[]{:S(2)}) collective-permute-start(bf16[2,32,512]{2,1,0:T(8,128)(2,1)S(1)} %shard_map.93), channel_id=1, source_target_pairs={{0,2},{1,3},{2,0},{3,1},{4,6},{5,7},{6,4},{7,5},{8,10},{9,11},{10,... | collective-permute-start | bytes 196616 | tf_op jit(solution)/shard_map/ppermute | solution.py:546
  66.3 0.0 copy-done.2
  66.3 1.5 %shard_map.92.light_ref = f32[256,1024]{1,0:T(8,128)S(1)} custom-call(f32[256,1024]{1,0:T(8,128)} %get-tuple-element.60.own, bf16[256,1024]{1,0:T(8,128)(2,1)} %copy-done.2), custom_call_target="tpu_custom_call" | custom-call | tf_op jit(solution)/shard_map/pallas_call | solution.py:126
  67.7 1.0 %collective-permute-done.10.last_ref = bf16[2,32,512]{2,1,0:T(8,128)(2,1)S(1)} collective-permute-done((bf16[2,32,512]{2,1,0:T(8,128)(2,1)S(1)}, bf16[2,32,512]{2,1,0:T(8,128)(2,1)S(1)}, u32[]{:S(2)}, u32[]{:S(2)}) %collective-permute-start.10) | collective-permute-done | bytes 65568 | tf_op jit(solution)/shard_map/ppermute | solution.py:546
  68.7 1.3 %shard_map.94 = bf16[256,1024]{1,0:T(8,128)(2,1)} custom-call(f32[256,1024]{1,0:T(8,128)S(1)} %shard_map.92.light_ref, bf16[8,32,512]{2,1,0:T(8,128)(2,1)S(1)} %all_to_all.20.back_ref, bf16[2,2,32,512]{3,2,1,0:T(8,128)(2,1)S(1)} %collective-permute-done.9.got_ref, bf16[2,32,512]{2,1,0:T(8,128)(2,1)S(1)} %collective-permute-done.10.last_ref, ...), custom_call_target="tpu_custom_call" | custom-call | tf_op jit(solution)/shard_map/pallas_call | solution.py:126
  (2 shorter events, 0.0 us)
Async XLA Ops:
  0.0 5.7 %collective-permute-start.1 = (bf16[256,1024]{1,0:T(8,128)(2,1)}, bf16[256,1024]{1,0:T(8,128)(2,1)}, u32[]{:S(2)}, u32[]{:S(2)}) collective-permute-start(bf16[256,1024]{1,0:T(8,128)(2,1)} %refs_0_), channel_id=1, source_target_pairs={{0,1},{1,0},{2,3},{3,2},{4,5},{5,4},{6,7},{7,6},{8,9},{9,8},{10,11... | collective-permute-start | bytes 1572872 | tf_op jit(solution)/shard_map/ppermute | solution.py:473
  1.9 3.1 %collective-permute-start = (bf16[32,1024]{1,0:T(8,128)(2,1)S(1)}, bf16[32,1024]{1,0:T(8,128)(2,1)S(1)}, u32[]{:S(2)}, u32[]{:S(2)}) collective-permute-start(bf16[32,1024]{1,0:T(8,128)(2,1)S(1)} %get-tuple-element.36), channel_id=1, source_target_pairs={{0,1},{1,0},{2,3},{3,2},{4,5},{5,4},{6,7},{7,6},{8,9},{9,8},{10,11... | collective-permute-start | bytes 196616 | tf_op jit(solution)/shard_map/ppermute | solution.py:470
  2.0 15.4 %collective-permute-start.2 = (bf16[256,1024]{1,0:T(8,128)(2,1)}, bf16[256,1024]{1,0:T(8,128)(2,1)}, u32[]{:S(2)}, u32[]{:S(2)}) collective-permute-start(bf16[256,1024]{1,0:T(8,128)(2,1)} %refs_0_), channel_id=1, source_target_pairs={{0,2},{1,3},{2,0},{3,1},{4,6},{5,7},{6,4},{7,5},{8,10},{9,11},{10,... | collective-permute-start | bytes 1572872 | tf_op jit(solution)/shard_map/ppermute | solution.py:472
  5.7 13.1 %all-to-all-start = ((bf16[8,32,512]{2,1,0:T(8,128)(2,1)}), bf16[8,32,512]{2,1,0:T(8,128)(2,1)S(1)}, u32[]{:S(2)}, u32[]{:S(2)}) async-start(bf16[8,32,512]{2,1,0:T(8,128)(2,1)} %shard_map.83), calls=%async_computation | async-start | bytes 524288 | tf_op jit(solution)/shard_map/all_to_all | solution.py:446
  12.1 12.7 %copy-start = (bf16[3,512,1024]{2,1,0:T(8,128)(2,1)S(1)}, bf16[3,512,1024]{2,1,0:T(8,128)(2,1)}, u32[]{:S(2)}) copy-start(bf16[3,512,1024]{2,1,0:T(8,128)(2,1)} %weight_ref.2) | copy-start | bytes 9437188
  18.8 7.5 %collective-permute-start.6 = (bf16[256,1024]{1,0:T(8,128)(2,1)}, bf16[256,1024]{1,0:T(8,128)(2,1)}, u32[]{:S(2)}, u32[]{:S(2)}) collective-permute-start(bf16[256,1024]{1,0:T(8,128)(2,1)} %collective-permute-done.2.refs_0_), channel_id=1, source_target_pairs={{0,1},{1,0},{2,3},{3,2},{4,5},{5,4},{6,7},{7,6},{8,9},{9,8},{10,11... | collective-permute-start | bytes 1572872 | tf_op jit(solution)/shard_map/ppermute | solution.py:484
  18.9 4.1 %collective-permute-start.5 = (bf16[64,512]{1,0:T(8,128)(2,1)S(1)}, bf16[64,512]{1,0:T(8,128)(2,1)S(1)}, u32[]{:S(2)}, u32[]{:S(2)}) collective-permute-start(bf16[64,512]{1,0:T(8,128)(2,1)S(1)} %shard_map.85.mine_ref), channel_id=1, source_target_pairs={{0,3},{1,2},{2,1},{3,0},{4,7},{5,6},{6,5},{7,4},{8,11},{9,10},{10,... | collective-permute-start | bytes 196616 | tf_op jit(solution)/shard_map/ppermute | solution.py:487
  20.6 4.3 %collective-permute-start.4 = (bf16[64,512]{1,0:T(8,128)(2,1)S(1)}, bf16[64,512]{1,0:T(8,128)(2,1)S(1)}, u32[]{:S(2)}, u32[]{:S(2)}) collective-permute-start(bf16[64,512]{1,0:T(8,128)(2,1)S(1)} %shard_map.85.mine_ref), channel_id=1, source_target_pairs={{0,2},{1,3},{2,0},{3,1},{4,6},{5,7},{6,4},{7,5},{8,10},{9,11},{10,... | collective-permute-start | bytes 196616 | tf_op jit(solution)/shard_map/ppermute | solution.py:487
  21.1 3.7 %collective-permute-start.3 = (bf16[64,512]{1,0:T(8,128)(2,1)S(1)}, bf16[64,512]{1,0:T(8,128)(2,1)S(1)}, u32[]{:S(2)}, u32[]{:S(2)}) collective-permute-start(bf16[64,512]{1,0:T(8,128)(2,1)S(1)} %shard_map.85.mine_ref), channel_id=1, source_target_pairs={{0,1},{1,0},{2,3},{3,2},{4,5},{5,4},{6,7},{7,6},{8,9},{9,8},{10,11... | collective-permute-start | bytes 196616 | tf_op jit(solution)/shard_map/ppermute | solution.py:487
  26.2 13.7 %all-to-all-start.1 = ((bf16[8,3,64,128]{3,2,1,0:T(8,128)(2,1)}), bf16[8,3,64,128]{3,2,1,0:T(8,128)(2,1)S(1)}, u32[]{:S(2)}, u32[]{:S(2)}) async-start(bf16[8,3,64,128]{3,2,1,0:T(8,128)(2,1)} %shard_map.86), calls=%async_computation.1 | async-start | bytes 786432 | tf_op jit(solution)/shard_map/all_to_all | solution.py:446
  38.4 12.6 %copy-start.1 = (bf16[1024,512]{1,0:T(8,128)(2,1)S(1)}, bf16[1024,512]{1,0:T(8,128)(2,1)}, u32[]{:S(2)}) copy-start(bf16[1024,512]{1,0:T(8,128)(2,1)} %weight_ref.3) | copy-start | bytes 3145732
  40.0 6.3 %collective-permute-start.7 = (bf16[2,256,1024]{2,1,0:T(8,128)(2,1)}, bf16[2,256,1024]{2,1,0:T(8,128)(2,1)S(1)}, u32[]{:S(2)}, u32[]{:S(2)}) collective-permute-start(bf16[2,256,1024]{2,1,0:T(8,128)(2,1)} %get-tuple-element.51), channel_id=1, source_target_pairs={{0,1},{1,0},{2,3},{3,2},{4,5},{5,4},{6,7},{7,6},{8,9},{9,8},{10,11... | collective-permute-start | bytes 3145736 | tf_op jit(solution)/shard_map/ppermute | solution.py:510
  41.0 10.0 %all-to-all-start.2 = ((bf16[8,64,128]{2,1,0:T(8,128)(2,1)}), bf16[8,64,128]{2,1,0:T(8,128)(2,1)S(1)}, u32[]{:S(2)}, u32[]{:S(2)}) async-start(bf16[8,64,128]{2,1,0:T(8,128)(2,1)} %shard_map.88), calls=%async_computation.2 | async-start | bytes 262144 | tf_op jit(solution)/shard_map/all_to_all | solution.py:446
  48.8 14.2 %collective-permute-start.8 = (bf16[256,1024]{1,0:T(8,128)(2,1)}, bf16[256,1024]{1,0:T(8,128)(2,1)S(1)}, u32[]{:S(2)}, u32[]{:S(2)}) collective-permute-start(bf16[256,1024]{1,0:T(8,128)(2,1)} %get-tuple-element.54), channel_id=1, source_target_pairs={{0,2},{1,3},{2,0},{3,1},{4,6},{5,7},{6,4},{7,5},{8,10},{9,11},{10,... | collective-permute-start | bytes 1572872 | tf_op jit(solution)/shard_map/ppermute | solution.py:523
  62.9 3.3 %copy-start.2 = (bf16[256,1024]{1,0:T(8,128)(2,1)}, bf16[256,1024]{1,0:T(8,128)(2,1)S(1)}, u32[]{:S(2)}) copy-start(bf16[256,1024]{1,0:T(8,128)(2,1)S(1)} %collective-permute-done.8.far) | copy-start | bytes 1572868
  62.9 1.4 %collective-permute-start.9 = (bf16[2,2,32,512]{3,2,1,0:T(8,128)(2,1)S(1)}, bf16[2,2,32,512]{3,2,1,0:T(8,128)(2,1)S(1)}, u32[]{:S(2)}, u32[]{:S(2)}) collective-permute-start(bf16[2,2,32,512]{3,2,1,0:T(8,128)(2,1)S(1)} %shard_map.91), channel_id=1, source_target_pairs={{0,1},{1,0},{2,3},{3,2},{4,5},{5,4},{6,7},{7,6},{8,9},{9,8},{10,11... | collective-permute-start | bytes 393224 | tf_op jit(solution)/shard_map/ppermute | solution.py:544
  64.4 4.3 %collective-permute-start.10 = (bf16[2,32,512]{2,1,0:T(8,128)(2,1)S(1)}, bf16[2,32,512]{2,1,0:T(8,128)(2,1)S(1)}, u32[]{:S(2)}, u32[]{:S(2)}) collective-permute-start(bf16[2,32,512]{2,1,0:T(8,128)(2,1)S(1)} %shard_map.93), channel_id=1, source_target_pairs={{0,2},{1,3},{2,0},{3,1},{4,6},{5,7},{6,4},{7,5},{8,10},{9,11},{10,... | collective-permute-start | bytes 196616 | tf_op jit(solution)/shard_map/ppermute | solution.py:546
